TPU v7x, 32 devices: a whole 2x2x4 slice. The times are simulated.
32 devices in a mesh: sample: 4 (over x, core), space: 8 (over z, y).
Axes of the slice: x: 2, y: 2, z: 4, core: 2. Of those that a mesh axis runs over, the one named last changes fastest.
Arguments:
- activations: bfloat16 [4, 64, 32, 1024], P('sample', 'space'), may hold values from -6 to 6
- open_cells: int32 [4, 64, 512], P('sample', 'space'), may hold values 0 or 1
- wind_class: int32 [4], P('sample'), may hold values from 0 to 7
- w_early: bfloat16 [3, 3, 3, 64, 128], replicated, may hold values from -0.15625 to 0.15625
- bias_table: float32 [8, 128], replicated, may hold values from -3 to 3
- w_deep: bfloat16 [2, 2, 2, 128, 256], replicated, may hold values from -0.1875 to 0.1875
- cotangent: bfloat16 [4, 16, 8, 1024], P('sample', 'space'), may hold values from -0.119628906 to 0.119628906
Outputs:
- deep: bfloat16 [4, 16, 8, 1024], P('sample', 'space')
- grad_deep: float32 [2, 2, 2, 128, 256], replicated
- grad_early: float32 [3, 3, 3, 64, 128], replicated
All inputs are finite; a program needn't handle non-finite values. No bound on the sum of `open_cells` on one device may be relied on, other than what follows from the above.
Results may differ from a plain program's by a relative error of at most 0.005.
Values may be sent and summed in bfloat16 or wider, within the bound.
No kernel may reach another device: no remote copies, remote signals or barrier semaphores. Data moves between devices by JAX's collectives and lax.ppermute only.
A program may use at most 64 MiB of HBM per device.

v0:
```python
import jax
import jax.numpy as jnp
from jax import lax
from jax.sharding import PartitionSpec as P

SLOPE = 0.3


def passed_along(value, axis, by):
    peers = lax.axis_size(axis)
    pairs = [(i, i + by) for i in range(peers) if 0 <= i + by < peers]
    return lax.ppermute(value, axis, pairs)


def early_forward(padded, w_early, bias):
    out = lax.conv_general_dilated(
        padded[None],
        w_early,
        (2, 2, 2),
        ((0, 0), (0, 0), (0, 0)),
        dimension_numbers=("NDHWC", "DHWIO", "NDHWC"),
        preferred_element_type=jnp.float32,
    )
    return out[0] + bias


def deep_terms(hidden, w_deep, upstream):
    zh, yh, xh, c1 = hidden.shape
    c2 = w_deep.shape[4]
    patches = (
        hidden.reshape(zh // 2, 2, yh // 2, 2, xh // 2, 2, c1)
        .transpose(0, 2, 4, 1, 3, 5, 6)
        .reshape(-1, 8 * c1)
    )
    out = jnp.dot(patches, w_deep.reshape(8 * c1, c2), preferred_element_type=jnp.float32)
    flat_up = upstream.reshape(-1, c2)
    grad_w = lax.dot_general(
        patches, flat_up, (((0,), (0,)), ((), ())), preferred_element_type=jnp.float32
    ).reshape(2, 2, 2, c1, c2)
    back = lax.dot_general(
        flat_up,
        w_deep.reshape(8, c1, c2),
        (((1,), (2,)), ((), ())),
        preferred_element_type=jnp.float32,
    )
    back = (
        back.reshape(zh // 2, yh // 2, xh // 2, 2, 2, 2, c1)
        .transpose(0, 3, 1, 4, 2, 5, 6)
        .reshape(zh, yh, xh, c1)
    )
    return (out, grad_w, back)


def early_grad(padded, delta):
    zo, yo, xo, c1 = delta.shape
    c0 = padded.shape[3]
    flat_delta = delta.reshape(-1, c1)
    pieces = []
    for a in range(3):
        for b in range(3):
            for c in range(3):
                piece = lax.slice(
                    padded,
                    (a, b, c, 0),
                    (a + 2 * zo - 1, b + 2 * yo - 1, c + 2 * xo - 1, c0),
                    (2, 2, 2, 1),
                ).reshape(-1, c0)
                pieces.append(
                    lax.dot_general(
                        piece,
                        flat_delta,
                        (((0,), (0,)), ((), ())),
                        preferred_element_type=jnp.float32,
                    )
                )
    return jnp.stack(pieces).reshape(3, 3, 3, c0, c1)


def total_terms(grad):
    flat = grad.reshape(-1)
    summed = lax.psum(flat, ("sample", "space"))
    return summed.reshape(grad.shape)


def body(activations, open_cells, wind_class, w_early, bias_table, w_deep, cotangent):
    depth = activations.shape[1]
    rows_y = activations.shape[2]
    chan_in = w_early.shape[3]
    chan_out = w_deep.shape[4]
    rows_x = activations.shape[3] // chan_in
    opens = open_cells[0].reshape(depth, rows_y, rows_x, 1).astype(jnp.bfloat16)
    masked = (activations[0].reshape(depth, rows_y, rows_x, chan_in) * opens).reshape(
        depth, rows_y, rows_x * chan_in
    )
    below = passed_along(masked[depth - 1], "space", 1)
    field = jnp.concatenate([below[None], masked], axis=0).reshape(
        depth + 1, rows_y, rows_x, chan_in
    )
    padded = jnp.pad(field, ((0, 0), (1, 0), (1, 0), (0, 0)))
    chosen = jnp.arange(bias_table.shape[0], dtype=jnp.int32)[:, None] == wind_class[0]
    bias = jnp.sum(jnp.where(chosen, bias_table, jnp.zeros_like(bias_table)), axis=0)
    pre = early_forward(padded, w_early, bias)
    hidden = jnp.where(pre > 0, pre, SLOPE * pre).astype(jnp.bfloat16)
    upstream = cotangent[0].reshape(depth // 4, rows_y // 4, rows_x // 4, chan_out)
    out, grad_w, back = deep_terms(hidden, w_deep, upstream)
    delta = (back * jnp.where(pre > 0, 1.0, SLOPE)).astype(jnp.bfloat16)
    grad_deep = total_terms(grad_w)
    grad_early = total_terms(early_grad(padded, delta))
    deep = out.astype(jnp.bfloat16).reshape(1, depth // 4, rows_y // 4, rows_x // 4 * chan_out)
    return (deep, grad_deep, grad_early)


def solution(mesh):
    in_specs = (
        P("sample", "space", None, None),
        P("sample", "space", None),
        P("sample"),
        P(),
        P(),
        P(),
        P("sample", "space", None, None),
    )
    out_specs = (P("sample", "space", None, None), P(), P())
    return jax.shard_map(body, mesh=mesh, in_specs=in_specs, out_specs=out_specs, check_vma=False)
```

profile of v0, /device:TPU:0, one launch (start us, length us, event | category | flops | bytes accessed | tf_op | source)
XLA Modules:
  0.0 380.3 jit_solution(18190275280594896844)
XLA Ops:
  7.2 1.8 reshape_squeeze.4
  10.9 4.9 %collective-permute-start = (bf16[32,1024]{1,0:T(8,128)(2,1)S(1)}, bf16[32,1024]{1,0:T(8,128)(2,1)S(1)}, u32[]{:S(2)}, u32[]{:S(2)}) collective-permute-start(bf16[32,1024]{1,0:T(8,128)(2,1)S(1)} %squeeze.11), channel_id=1, source_target_pairs={{0,1},{1,2},{2,3},{3,4},{4,5},{5,6},{6,7},{8,9},{9,10},{10,11},{11... | collective-permute-start | bytes 196616 | tf_op jit(solution)/shard_map/ppermute | solution.py:12
  17.9 1.8 fusion.111
  20.3 9.8 %slice.86 = bf16[4,16,8,64]{3,1,2,0:T(8,128)(2,1)} slice(bf16[9,33,17,64]{3,1,2,0:T(8,128)(2,1)S(1)} %fusion.11), slice={[0:7:2], [0:31:2], [0:15:2], [0:64:1]} | slice | bytes 131072 | tf_op jit(solution)/shard_map/slice | solution.py:62
  30.0 9.7 %slice.87 = bf16[4,16,8,64]{3,1,2,0:T(8,128)(2,1)} slice(bf16[9,33,17,64]{3,1,2,0:T(8,128)(2,1)S(1)} %fusion.11), slice={[0:7:2], [0:31:2], [1:16:2], [0:64:1]} | slice | bytes 131072 | tf_op jit(solution)/shard_map/slice | solution.py:62
  39.8 9.8 %slice.88 = bf16[4,16,8,64]{3,1,2,0:T(8,128)(2,1)} slice(bf16[9,33,17,64]{3,1,2,0:T(8,128)(2,1)S(1)} %fusion.11), slice={[0:7:2], [0:31:2], [2:17:2], [0:64:1]} | slice | bytes 131072 | tf_op jit(solution)/shard_map/slice | solution.py:62
  49.6 9.7 %slice.89 = bf16[4,16,8,64]{3,1,2,0:T(8,128)(2,1)} slice(bf16[9,33,17,64]{3,1,2,0:T(8,128)(2,1)S(1)} %fusion.11), slice={[0:7:2], [1:32:2], [0:15:2], [0:64:1]} | slice | bytes 131072 | tf_op jit(solution)/shard_map/slice | solution.py:62
  59.3 9.7 %slice.90 = bf16[4,16,8,64]{3,1,2,0:T(8,128)(2,1)} slice(bf16[9,33,17,64]{3,1,2,0:T(8,128)(2,1)S(1)} %fusion.11), slice={[0:7:2], [1:32:2], [1:16:2], [0:64:1]} | slice | bytes 131072 | tf_op jit(solution)/shard_map/slice | solution.py:62
  69.0 9.8 %slice.91 = bf16[4,16,8,64]{3,1,2,0:T(8,128)(2,1)} slice(bf16[9,33,17,64]{3,1,2,0:T(8,128)(2,1)S(1)} %fusion.11), slice={[0:7:2], [1:32:2], [2:17:2], [0:64:1]} | slice | bytes 131072 | tf_op jit(solution)/shard_map/slice | solution.py:62
  78.7 9.8 %slice.92 = bf16[4,16,8,64]{3,1,2,0:T(8,128)(2,1)} slice(bf16[9,33,17,64]{3,1,2,0:T(8,128)(2,1)S(1)} %fusion.11), slice={[0:7:2], [2:33:2], [0:15:2], [0:64:1]} | slice | bytes 131072 | tf_op jit(solution)/shard_map/slice | solution.py:62
  88.5 9.7 %slice.93 = bf16[4,16,8,64]{3,1,2,0:T(8,128)(2,1)} slice(bf16[9,33,17,64]{3,1,2,0:T(8,128)(2,1)S(1)} %fusion.11), slice={[0:7:2], [2:33:2], [1:16:2], [0:64:1]} | slice | bytes 131072 | tf_op jit(solution)/shard_map/slice | solution.py:62
  98.2 9.8 %slice.94 = bf16[4,16,8,64]{3,1,2,0:T(8,128)(2,1)} slice(bf16[9,33,17,64]{3,1,2,0:T(8,128)(2,1)S(1)} %fusion.11), slice={[0:7:2], [2:33:2], [2:17:2], [0:64:1]} | slice | bytes 131072 | tf_op jit(solution)/shard_map/slice | solution.py:62
  108.0 9.7 %slice.95 = bf16[4,16,8,64]{3,1,2,0:T(8,128)(2,1)} slice(bf16[9,33,17,64]{3,1,2,0:T(8,128)(2,1)S(1)} %fusion.11), slice={[1:8:2], [0:31:2], [0:15:2], [0:64:1]} | slice | bytes 131072 | tf_op jit(solution)/shard_map/slice | solution.py:62
  117.7 9.7 %slice.96 = bf16[4,16,8,64]{3,1,2,0:T(8,128)(2,1)} slice(bf16[9,33,17,64]{3,1,2,0:T(8,128)(2,1)S(1)} %fusion.11), slice={[1:8:2], [0:31:2], [1:16:2], [0:64:1]} | slice | bytes 131072 | tf_op jit(solution)/shard_map/slice | solution.py:62
  127.4 9.8 %slice.97 = bf16[4,16,8,64]{3,1,2,0:T(8,128)(2,1)} slice(bf16[9,33,17,64]{3,1,2,0:T(8,128)(2,1)S(1)} %fusion.11), slice={[1:8:2], [0:31:2], [2:17:2], [0:64:1]} | slice | bytes 131072 | tf_op jit(solution)/shard_map/slice | solution.py:62
  137.2 9.7 %slice.98 = bf16[4,16,8,64]{3,1,2,0:T(8,128)(2,1)} slice(bf16[9,33,17,64]{3,1,2,0:T(8,128)(2,1)S(1)} %fusion.11), slice={[1:8:2], [1:32:2], [0:15:2], [0:64:1]} | slice | bytes 131072 | tf_op jit(solution)/shard_map/slice | solution.py:62
  146.9 9.7 %slice.99 = bf16[4,16,8,64]{3,1,2,0:T(8,128)(2,1)} slice(bf16[9,33,17,64]{3,1,2,0:T(8,128)(2,1)S(1)} %fusion.11), slice={[1:8:2], [1:32:2], [1:16:2], [0:64:1]} | slice | bytes 131072 | tf_op jit(solution)/shard_map/slice | solution.py:62
  156.6 9.8 %slice.100 = bf16[4,16,8,64]{3,1,2,0:T(8,128)(2,1)} slice(bf16[9,33,17,64]{3,1,2,0:T(8,128)(2,1)S(1)} %fusion.11), slice={[1:8:2], [1:32:2], [2:17:2], [0:64:1]} | slice | bytes 131072 | tf_op jit(solution)/shard_map/slice | solution.py:62
  166.4 9.8 %slice.101 = bf16[4,16,8,64]{3,1,2,0:T(8,128)(2,1)} slice(bf16[9,33,17,64]{3,1,2,0:T(8,128)(2,1)S(1)} %fusion.11), slice={[1:8:2], [2:33:2], [0:15:2], [0:64:1]} | slice | bytes 131072 | tf_op jit(solution)/shard_map/slice | solution.py:62
  176.2 9.7 %slice.102 = bf16[4,16,8,64]{3,1,2,0:T(8,128)(2,1)} slice(bf16[9,33,17,64]{3,1,2,0:T(8,128)(2,1)S(1)} %fusion.11), slice={[1:8:2], [2:33:2], [1:16:2], [0:64:1]} | slice | bytes 131072 | tf_op jit(solution)/shard_map/slice | solution.py:62
  185.9 9.8 %slice.103 = bf16[4,16,8,64]{3,1,2,0:T(8,128)(2,1)} slice(bf16[9,33,17,64]{3,1,2,0:T(8,128)(2,1)S(1)} %fusion.11), slice={[1:8:2], [2:33:2], [2:17:2], [0:64:1]} | slice | bytes 131072 | tf_op jit(solution)/shard_map/slice | solution.py:62
  195.7 9.7 %slice.104 = bf16[4,16,8,64]{3,1,2,0:T(8,128)(2,1)} slice(bf16[9,33,17,64]{3,1,2,0:T(8,128)(2,1)S(1)} %fusion.11), slice={[2:9:2], [0:31:2], [0:15:2], [0:64:1]} | slice | bytes 131072 | tf_op jit(solution)/shard_map/slice | solution.py:62
  235.6 134.6 %all-reduce.4.cloned.1.call-done = (f32[2,2,2,128,256]{4,3,2,1,0:T(8,128)}, f32[3,3,3,64,128]{4,3,2,1,0:T(8,128)}) async-done(((f32[2,2,2,128,256]{4,3,2,1,0:T(8,128)}, f32[3,3,3,64,128]{4,3,2,1,0:T(8,128)}), (f32[2,2,2,128,256]{4,3,2,1,0:T(8,128)}, f32[3,3,3,64,128]{4,3,2,1,0:T(8,128)})) %all-reduce.4.cloned.1.call-update) | async-done | bytes 1933328 | tf_op jit(solution)/shard_map/psum | solution.py:81
  370.2 2.3 copy.90
  (111 shorter events, 34.5 us)
Async XLA Ops:
  7.2 9.4 %copy-start = (bf16[2,2,2,128,256]{4,3,2,1,0:T(8,128)(2,1)S(1)}, bf16[2,2,2,128,256]{4,3,2,1,0:T(8,128)(2,1)}, u32[]{:S(2)}) copy-start(bf16[2,2,2,128,256]{4,3,2,1,0:T(8,128)(2,1)} %param.12) | copy-start | bytes 1572868
  7.2 9.3 %copy-start.3 = (bf16[1,2,8,1024]{3,2,1,0:T(8,128)(2,1)S(1)}, bf16[1,2,8,1024]{3,2,1,0:T(8,128)(2,1)}, u32[]{:S(2)}) copy-start(bf16[1,2,8,1024]{3,2,1,0:T(8,128)(2,1)} %param.13) | copy-start | bytes 98308
  7.2 363.0 %all-reduce.4.cloned.1.call-start = ((), (), s32[]{:S(2)}) async-start(), calls=%async_computation | async-start | bytes 3866624 | tf_op jit(solution)/shard_map/psum | solution.py:81
  9.0 7.9 %copy-start.19 = (f32[8,128]{1,0:T(8,128)S(1)}, f32[8,128]{1,0:T(8,128)}, u32[]{:S(2)}) copy-start(f32[8,128]{1,0:T(8,128)} %param.11) | copy-start | bytes 12292
  10.9 6.8 %collective-permute-start = (bf16[32,1024]{1,0:T(8,128)(2,1)S(1)}, bf16[32,1024]{1,0:T(8,128)(2,1)S(1)}, u32[]{:S(2)}, u32[]{:S(2)}) collective-permute-start(bf16[32,1024]{1,0:T(8,128)(2,1)S(1)} %squeeze.11), channel_id=1, source_target_pairs={{0,1},{1,2},{2,3},{3,4},{4,5},{5,6},{6,7},{8,9},{9,10},{10,11},{11... | collective-permute-start | bytes 196616 | tf_op jit(solution)/shard_map/ppermute | solution.py:12
  216.2 1.0 copy-start.20
  216.2 1.0 copy-start.21
  218.6 3.7 copy-start.16
  218.6 4.9 %copy-start.15 = (bf16[4,16,8,64]{3,1,2,0:T(8,128)(2,1)S(1)}, bf16[4,16,8,64]{3,1,2,0:T(8,128)(2,1)}, u32[]{:S(2)}) copy-start(bf16[4,16,8,64]{3,1,2,0:T(8,128)(2,1)} %slice.89) | copy-start | bytes 196612
  218.6 6.0 %copy-start.14 = (bf16[4,16,8,64]{3,1,2,0:T(8,128)(2,1)S(1)}, bf16[4,16,8,64]{3,1,2,0:T(8,128)(2,1)}, u32[]{:S(2)}) copy-start(bf16[4,16,8,64]{3,1,2,0:T(8,128)(2,1)} %slice.90) | copy-start | bytes 196612
  218.6 6.2 %copy-start.13 = (bf16[4,16,8,64]{3,1,2,0:T(8,128)(2,1)S(1)}, bf16[4,16,8,64]{3,1,2,0:T(8,128)(2,1)}, u32[]{:S(2)}) copy-start(bf16[4,16,8,64]{3,1,2,0:T(8,128)(2,1)} %slice.91) | copy-start | bytes 196612
  219.5 5.1 %copy-start.17 = (bf16[4,16,8,128]{3,1,2,0:T(8,128)(2,1)S(1)}, bf16[4,16,8,128]{3,1,2,0:T(8,128)(2,1)}, u32[]{:S(2)}) copy-start(bf16[4,16,8,128]{3,1,2,0:T(8,128)(2,1)} %fusion.45) | copy-start | bytes 393220
  219.8 7.6 %copy-start.18 = (bf16[4,16,8,128]{3,1,2,0:T(8,128)(2,1)S(1)}, bf16[4,16,8,128]{3,1,2,0:T(8,128)(2,1)}, u32[]{:S(2)}) copy-start(bf16[4,16,8,128]{3,1,2,0:T(8,128)(2,1)} %fusion.45) | copy-start | bytes 393220
  219.8 9.8 %copy-start.12 = (bf16[4,16,8,64]{3,1,2,0:T(8,128)(2,1)S(1)}, bf16[4,16,8,64]{3,1,2,0:T(8,128)(2,1)}, u32[]{:S(2)}) copy-start(bf16[4,16,8,64]{3,1,2,0:T(8,128)(2,1)} %slice.96) | copy-start | bytes 196612
  221.0 8.8 %copy-start.11 = (bf16[4,16,8,64]{3,1,2,0:T(8,128)(2,1)S(1)}, bf16[4,16,8,64]{3,1,2,0:T(8,128)(2,1)}, u32[]{:S(2)}) copy-start(bf16[4,16,8,64]{3,1,2,0:T(8,128)(2,1)} %slice.97) | copy-start | bytes 196612
  222.3 7.8 %copy-start.10 = (bf16[4,16,8,64]{3,1,2,0:T(8,128)(2,1)S(1)}, bf16[4,16,8,64]{3,1,2,0:T(8,128)(2,1)}, u32[]{:S(2)}) copy-start(bf16[4,16,8,64]{3,1,2,0:T(8,128)(2,1)} %slice.98) | copy-start | bytes 196612
  223.4 6.9 %copy-start.9 = (bf16[4,16,8,64]{3,1,2,0:T(8,128)(2,1)S(1)}, bf16[4,16,8,64]{3,1,2,0:T(8,128)(2,1)}, u32[]{:S(2)}) copy-start(bf16[4,16,8,64]{3,1,2,0:T(8,128)(2,1)} %slice.99) | copy-start | bytes 196612
  224.6 5.9 %copy-start.8 = (bf16[4,16,8,64]{3,1,2,0:T(8,128)(2,1)S(1)}, bf16[4,16,8,64]{3,1,2,0:T(8,128)(2,1)}, u32[]{:S(2)}) copy-start(bf16[4,16,8,64]{3,1,2,0:T(8,128)(2,1)} %slice.100) | copy-start | bytes 196612
  224.8 5.9 %copy-start.7 = (bf16[4,16,8,64]{3,1,2,0:T(8,128)(2,1)S(1)}, bf16[4,16,8,64]{3,1,2,0:T(8,128)(2,1)}, u32[]{:S(2)}) copy-start(bf16[4,16,8,64]{3,1,2,0:T(8,128)(2,1)} %slice.101) | copy-start | bytes 196612
  225.0 5.9 %copy-start.6 = (bf16[4,16,8,64]{3,1,2,0:T(8,128)(2,1)S(1)}, bf16[4,16,8,64]{3,1,2,0:T(8,128)(2,1)}, u32[]{:S(2)}) copy-start(bf16[4,16,8,64]{3,1,2,0:T(8,128)(2,1)} %slice.102) | copy-start | bytes 196612
  226.2 5.0 %copy-start.5 = (bf16[4,16,8,64]{3,1,2,0:T(8,128)(2,1)S(1)}, bf16[4,16,8,64]{3,1,2,0:T(8,128)(2,1)}, u32[]{:S(2)}) copy-start(bf16[4,16,8,64]{3,1,2,0:T(8,128)(2,1)} %slice.103) | copy-start | bytes 196612
  227.4 4.0 %copy-start.4 = (bf16[4,16,8,64]{3,1,2,0:T(8,128)(2,1)S(1)}, bf16[4,16,8,64]{3,1,2,0:T(8,128)(2,1)}, u32[]{:S(2)}) copy-start(bf16[4,16,8,64]{3,1,2,0:T(8,128)(2,1)} %slice.104) | copy-start | bytes 196612
  233.4 1.3 copy-start.2
  370.2 2.4 copy-start.1
Sparse Core Ops, SparseCore 0:
  234.8 135.3 all-reduce.3
where the time goes:
time: 381 us; the launch traced here: 380 us
  local copies, waits for them, and re-layouts  204 us (54%)
  waiting for transfers between devices  135 us (35%)
  matrix products  16.5 us (4%)
  between operations  15.2 us (4%)
  starting transfers between devices  4.91 us (1%)
  other arithmetic  4.8 us (1%)
    slice x27, local copies, waits for them, and re-layouts, early_grad(): lax.slice(padded, (a, b, c, 0), (a + 2 * zo - 1, b + 2 * yo - 1, c + 2 *...  194 us
    psum x1, waiting for transfers between devices, total_terms(): summed = lax.psum(flat, ('sample', 'space'))  135 us
    dot_general x27, matrix products, early_grad(): lax.dot_general(piece, flat_delta, (((0,), (0,)), ((), ())), preferred_el...  13.3 us
  transfers between devices with their start and end apart: 2, of which 2 were waited for; matrix products, arithmetic and copies ran while one was open for 0% of the time, Pallas kernels for 0%

commit v1 on v0

v1 whole, which is shorter than its diff:
```python
import jax
import jax.numpy as jnp
from jax import lax
from jax.experimental import pallas as pl
from jax.experimental.pallas import tpu as pltpu
from jax.sharding import PartitionSpec as P

SLOPE = 0.3
BF16 = jnp.bfloat16
F32 = jnp.float32

DEPTH, ROWS, CELLS, C0, C1, C2 = 8, 32, 16, 64, 128, 256
PAIR = 2 * C0
WIDE = CELLS * C0
CHUNKS = 8
DEEP_ROWS = 8 * C1 * C2 // 128 // CHUNKS
EARLY_ROWS = 27 * C0 // CHUNKS
CHUNK_ROWS = DEEP_ROWS + EARLY_ROWS
VMEM_BYTES = 48 * 1024 * 1024


def iota(shape, dim):
    return lax.broadcasted_iota(jnp.int32, shape, dim)


def masked_rows(acts, opens):
    planes = opens.shape[0]
    cells = ROWS * CELLS
    own = (iota((ROWS, cells), 1) // CELLS) == iota((ROWS, cells), 0)
    spread = jnp.concatenate(
        [jnp.where(own, opens[z : z + 1, :], 0).astype(F32).astype(BF16) for z in range(planes)], axis=0
    )
    pick = ((iota((cells, 128), 0) % CELLS) == iota((cells, 128), 1)).astype(F32).astype(BF16)
    by_cell = jnp.dot(spread, pick, preferred_element_type=F32).astype(BF16)
    widen = (iota((128, WIDE), 0) == (iota((128, WIDE), 1) // C0)).astype(F32).astype(BF16)
    mask = jnp.dot(by_cell, widen, preferred_element_type=F32).astype(BF16)
    return acts * mask


def edge_kernel(acts_ref, opens_ref, edge_ref):
    edge_ref[...] = masked_rows(acts_ref[0], opens_ref[DEPTH - 1 : DEPTH, :])


def row_of_slot(q):
    return 2 * (q % 8) + q // 8


def local_kernel(
    kind_ref, acts_ref, opens_ref, below_ref, w1_ref, bias_ref, w2_ref, cot_ref,
    deep_ref, keep_ref, send_ref,
    even_ref, odd_ref, patch_ref, early_ref,
):
    core = lax.axis_index("sample") % 2
    place = ((lax.axis_index("sample") // 2) % 2) * 2 + lax.axis_index("space") % 2

    field = masked_rows(acts_ref[...].reshape(DEPTH * ROWS, WIDE), opens_ref[...])
    half = 3 * 64
    r = iota((2 * half, DEPTH * ROWS), 0)
    par = (r >= half).astype(jnp.int32)
    s = r - half * par
    y = 2 * row_of_slot(s % 16) + s // 64 - 1
    z = 2 * ((s % 64) // 16) + par
    want = jnp.where(y >= 0, z * ROWS + y, -1)
    pick = (iota(r.shape, 1) == want).astype(F32).astype(BF16)
    rows = jnp.dot(pick, field, preferred_element_type=F32).astype(BF16)
    r = iota((48, ROWS), 0)
    y = 2 * row_of_slot(r % 16) + r // 16 - 1
    pick = (iota(r.shape, 1) == y).astype(F32).astype(BF16)
    rows_below = jnp.dot(pick, below_ref[...], preferred_element_type=F32).astype(BF16)
    for b in range(3):
        even_ref[b, :, :PAIR] = jnp.zeros((64, PAIR), BF16)
        odd_ref[b, :, :PAIR] = jnp.zeros((80, PAIR), BF16)
        even_ref[b, :, PAIR:] = rows[b * 64 : (b + 1) * 64]
        odd_ref[b, :16, PAIR:] = rows_below[b * 16 : (b + 1) * 16]
        odd_ref[b, 16:, PAIR:] = rows[half + b * 64 : half + (b + 1) * 64]

    def windows(a, b):
        ref, top = (even_ref, 0) if a == 1 else (odd_ref, 8 * a)
        return jnp.concatenate(
            [ref[b, top : top + 64, x * PAIR : (x + 2) * PAIR] for x in range(CELLS // 2)], axis=0
        )

    classes = bias_ref.shape[0]
    chosen = iota((classes, C1), 0) == kind_ref[0]
    bias = jnp.sum(jnp.where(chosen, bias_ref[...], 0.0), axis=0, keepdims=True)
    pre = jnp.zeros((512, C1), F32)
    for a in range(3):
        for b in range(3):
            w = jnp.concatenate([jnp.zeros((C0, C1), BF16), w1_ref[a * 3 + b]], axis=0)
            pre = pre + jnp.dot(windows(a, b), w, preferred_element_type=F32)
    pre = pre + bias
    hidden = jnp.where(pre > 0, pre, SLOPE * pre)

    def piece(xs, zs, a, b, c):
        return (2 * xs + c) * 64 + (2 * zs + a) * 16 + b * 8

    pieces = [(xs, zs) for xs in range(CELLS // 4) for zs in range(DEPTH // 4)]
    taps = [(a, b, c) for a in range(2) for b in range(2) for c in range(2)]
    cot = jnp.concatenate([cot_ref[:, x * C2 : (x + 1) * C2] for x in range(CELLS // 4)], axis=0)
    out = jnp.zeros((64, C2), F32)
    delta_at = {}
    for t, (a, b, c) in enumerate(taps):
        starts = [piece(xs, zs, a, b, c) for xs, zs in pieces]
        patch = jnp.concatenate([hidden[at : at + 8] for at in starts], axis=0).astype(BF16)
        patch_ref[t] = patch
        out = out + jnp.dot(patch, w2_ref[t], preferred_element_type=F32)
        back = lax.dot_general(cot, w2_ref[t], (((1,), (1,)), ((), ())), preferred_element_type=F32)
        for k, at in enumerate(starts):
            delta_at[at] = back[k * 8 : (k + 1) * 8]
    out = out.astype(BF16)
    for x in range(CELLS // 4):
        deep_ref[:, x * C2 : (x + 1) * C2] = out[x * 16 : (x + 1) * 16]
    back = jnp.concatenate([delta_at[at] for at in sorted(delta_at)], axis=0)
    delta = (back * jnp.where(pre > 0, 1.0, SLOPE)).astype(BF16)

    for a in range(3):
        for b in range(3):
            grad = lax.dot_general(
                windows(a, b), delta, (((0,), (0,)), ((), ())), preferred_element_type=F32
            )
            at = (a * 3 + b) * 3 * C0
            early_ref[at : at + 3 * C0] = grad[C0:]

    for far in range(2):
        for m in range(4):
            chunk = ((core + far) % 2) * 4 + (place ^ m)
            grad = lax.dot_general(
                patch_ref[chunk], cot, (((0,), (0,)), ((), ())), preferred_element_type=F32
            )
            early = early_ref[pl.ds(pl.multiple_of(chunk * EARLY_ROWS, 8), EARLY_ROWS), :]
            ref, kind = (send_ref, BF16) if far else (keep_ref, F32)
            ref[m, :C1] = grad[:, :128].astype(kind)
            ref[m, C1 : 2 * C1] = grad[:, 128:].astype(kind)
            ref[m, 2 * C1 :] = early.astype(kind)


def spread_kernel(near_ref, far_ref, deep_ref, early_ref):
    core = lax.axis_index("sample") % 2
    place = ((lax.axis_index("sample") // 2) % 2) * 2 + lax.axis_index("space") % 2
    for far in range(2):
        ref = far_ref if far else near_ref
        for m in range(4):
            chunk = ((core + far) % 2) * 4 + (place ^ m)
            deep_ref[chunk, :, :128] = ref[m, :C1].astype(F32)
            deep_ref[chunk, :, 128:] = ref[m, C1 : 2 * C1].astype(F32)
            at = pl.multiple_of(chunk * EARLY_ROWS, 8)
            early_ref[pl.ds(at, EARLY_ROWS), :] = ref[m, 2 * C1 :].astype(F32)


def swapped(value, sample_bits=0, space_bits=0):
    samples, spaces = lax.axis_size("sample"), lax.axis_size("space")
    pairs = [
        (i * spaces + j, (i ^ sample_bits) * spaces + (j ^ space_bits))
        for i in range(samples)
        for j in range(spaces)
    ]
    return lax.ppermute(value, ("sample", "space"), pairs)


QUAD = ((0, 1), (2, 0), (2, 1))


def total(keep, send):
    near = keep + swapped(send, 1).astype(F32)
    mine = near[0]
    others = near[1:].astype(BF16)
    for k, (i, j) in enumerate(QUAD):
        mine = mine + swapped(others[k], i, j).astype(F32)
    for axis, first in (("space", 2), ("sample", 4)):
        bit = first
        while bit < lax.axis_size(axis):
            own = mine.astype(BF16)
            peer = swapped(own, bit, 0) if axis == "sample" else swapped(own, 0, bit)
            mine = own.astype(F32) + peer.astype(F32)
            bit *= 2
    own = mine.astype(BF16)
    near = jnp.stack([own] + [swapped(own, i, j) for i, j in QUAD])
    return near, swapped(near, 1)


def body(activations, open_cells, wind_class, w_early, bias_table, w_deep, cotangent):
    params = pltpu.CompilerParams(vmem_limit_bytes=VMEM_BYTES)
    acts = activations[0]
    opens = open_cells[0]
    edge = pl.pallas_call(
        edge_kernel,
        grid=(1,),
        in_specs=[
            pl.BlockSpec((1, ROWS, WIDE), lambda i: (DEPTH - 1, 0, 0)),
            pl.BlockSpec((DEPTH, ROWS * CELLS), lambda i: (0, 0)),
        ],
        out_specs=pl.BlockSpec((ROWS, WIDE), lambda i: (0, 0)),
        out_shape=jax.ShapeDtypeStruct((ROWS, WIDE), BF16),
        compiler_params=params,
        name="edge_plane",
    )(acts, opens)
    spaces = lax.axis_size("space")
    below = lax.ppermute(edge, "space", [(i, i + 1) for i in range(spaces - 1)])
    vmem = pl.BlockSpec(memory_space=pltpu.VMEM)
    smem = pl.BlockSpec(memory_space=pltpu.SMEM)
    deep, keep, send = pl.pallas_call(
        local_kernel,
        in_specs=[smem] + [vmem] * 7,
        out_specs=[vmem] * 3,
        out_shape=[
            jax.ShapeDtypeStruct((DEPTH // 4 * ROWS // 4, CELLS // 4 * C2), BF16),
            jax.ShapeDtypeStruct((4, CHUNK_ROWS, 128), F32),
            jax.ShapeDtypeStruct((4, CHUNK_ROWS, 128), BF16),
        ],
        scratch_shapes=[
            pltpu.VMEM((3, 64, WIDE + PAIR), BF16),
            pltpu.VMEM((3, 80, WIDE + PAIR), BF16),
            pltpu.VMEM((8, 64, C1), BF16),
            pltpu.VMEM((27 * C0, C1), F32),
        ],
        compiler_params=params,
        name="local_terms",
    )(
        wind_class,
        acts,
        opens,
        below,
        w_early.reshape(9, 3 * C0, C1),
        bias_table,
        w_deep.reshape(8, C1, C2),
        cotangent.reshape(DEPTH // 4 * ROWS // 4, CELLS // 4 * C2),
    )
    near, far = total(keep, send)
    grad_deep, grad_early = pl.pallas_call(
        spread_kernel,
        in_specs=[vmem] * 2,
        out_specs=[vmem] * 2,
        out_shape=[
            jax.ShapeDtypeStruct((8, C1, C2), F32),
            jax.ShapeDtypeStruct((27 * C0, C1), F32),
        ],
        compiler_params=params,
        name="spread_sums",
    )(near, far)
    return (
        deep.reshape(1, DEPTH // 4, ROWS // 4, CELLS // 4 * C2),
        grad_deep.reshape(w_deep.shape),
        grad_early.reshape(w_early.shape),
    )


def solution(mesh):
    in_specs = (
        P("sample", "space", None, None),
        P("sample", "space", None),
        P("sample"),
        P(),
        P(),
        P(),
        P("sample", "space", None, None),
    )
    out_specs = (P("sample", "space", None, None), P(), P())
    return jax.shard_map(body, mesh=mesh, in_specs=in_specs, out_specs=out_specs, check_vma=False)
```

time: 381 us -> 49.3 us (0.13)
  local copies, waits for them, and re-layouts: 204 us -> 2.8 us
  waiting for transfers between devices: 135 us -> 21.3 us
  matrix products: 16.5 us -> 0 us
  between operations: 15.2 us -> 1.37 us
  starting transfers between devices: 4.91 us -> 18.7 us
  Pallas kernels: 0 us -> 4.59 us
  other arithmetic: 4.8 us -> 0.34 us
    slice x29 -> x0, local copies, waits for them, and re-layouts: 194 us -> none  [the longest x27 194 us: early_grad(): lax.slice(padded, (a, b, c, 0), (a + 2 * zo - 1, b + 2 * yo - 1, c + 2 *...]
    psum x1 -> x0, waiting for transfers between devices: 135 us -> none  [total_terms(): summed = lax.psum(flat, ('sample', 'space'))]
    ppermute x1 -> x11, waiting for transfers between devices: 0.64 us -> 21.3 us  [the longest x10 20 us: swapped(): return lax.ppermute(value, ('sample', 'space'), pairs)]
    dot_general x30 -> x0, matrix products: 15.1 us -> none  [the longest x27 13.3 us: early_grad(): lax.dot_general(piece, flat_delta, (((0,), (0,)), ((), ())), preferred_el...]
    ppermute x1 -> x11, starting transfers between devices: 4.87 us -> 18.7 us  [the longest x10 13.8 us: swapped(): return lax.ppermute(value, ('sample', 'space'), pairs)]
    pallas_call x0 -> x3, Pallas kernels: none -> 4.59 us  [the longest x1 2.91 us: body(): pl.pallas_call(local_kernel, in_specs=[smem] + [vmem] * 7, out_specs=[vme...]
  transfers between devices with their start and end apart: 2 -> 11, of which waited for: 2 -> 11; matrix products, arithmetic and copies ran while one was open for 0% -> 0% of each run, Pallas kernels for 0% -> 0%
where the time goes in v1:
time: 49.3 us; the launch traced here: 49 us
  waiting for transfers between devices  21.3 us (43%)
  starting transfers between devices  18.7 us (38%)
  Pallas kernels  4.59 us (9%)
  local copies, waits for them, and re-layouts  2.8 us (6%)
  between operations  1.37 us (3%)
    ppermute x10, waiting for transfers between devices, swapped(): return lax.ppermute(value, ('sample', 'space'), pairs)  20 us
    ppermute x10, starting transfers between devices, swapped(): return lax.ppermute(value, ('sample', 'space'), pairs)  13.8 us
    ppermute x1, starting transfers between devices, body(): below = lax.ppermute(edge, 'space', [(i, i + 1) for i in range(spaces - 1)])  4.87 us
    pallas_call x1, Pallas kernels, body(): pl.pallas_call(local_kernel, in_specs=[smem] + [vmem] * 7, out_specs=[vme...  2.91 us
    unnamed x12, local copies, waits for them, and re-layouts  2.77 us
    pallas_call x1, Pallas kernels, body(): pl.pallas_call(spread_kernel, in_specs=[vmem] * 2, out_specs=[vmem] * 2,...  1.4 us
    ppermute x1, waiting for transfers between devices, body(): below = lax.ppermute(edge, 'space', [(i, i + 1) for i in range(spaces - 1)])  1.24 us
  transfers between devices with their start and end apart: 11, of which 11 were waited for; matrix products, arithmetic and copies ran while one was open for 0% of the time, Pallas kernels for 0%

profile of v1, /device:TPU:0, one launch (start us, length us, event | category | flops | bytes accessed | tf_op | source)
XLA Modules:
  0.0 49.0 jit_solution(15584282363437308650)
XLA Ops:
  0.6 1.0 %copy-done = bf16[1,8,32,1024]{3,2,1,0:T(8,128)(2,1)S(1)} copy-done((bf16[1,8,32,1024]{3,2,1,0:T(8,128)(2,1)S(1)}, bf16[1,8,32,1024]{3,2,1,0:T(8,128)(2,1)}, u32[]{:S(2)}) %copy-start) | copy-done | bytes 524312
  1.7 0.7 %copy-done.3 = s32[1,8,512]{2,1,0:T(8,128)S(1)} copy-done((s32[1,8,512]{2,1,0:T(8,128)S(1)}, s32[1,8,512]{2,1,0:T(8,128)}, u32[]{:S(2)}) %copy-start.3) | copy-done | bytes 16408
  2.7 4.9 %collective-permute-start = (bf16[32,1024]{1,0:T(8,128)(2,1)S(1)}, bf16[32,1024]{1,0:T(8,128)(2,1)S(1)}, u32[]{:S(2)}, u32[]{:S(2)}) collective-permute-start(bf16[32,1024]{1,0:T(8,128)(2,1)S(1)} %edge_plane.1), channel_id=1, source_target_pairs={{0,1},{1,2},{2,3},{3,4},{4,5},{5,6},{6,7},{8,9},{9,10},{10,11},{11... | collective-permute-start | bytes 196616 | tf_op jit(solution)/shard_map/ppermute | solution.py:198
  8.2 1.2 %collective-permute-done.below_ref = bf16[32,1024]{1,0:T(8,128)(2,1)S(1)} collective-permute-done((bf16[32,1024]{1,0:T(8,128)(2,1)S(1)}, bf16[32,1024]{1,0:T(8,128)(2,1)S(1)}, u32[]{:S(2)}, u32[]{:S(2)}) %collective-permute-start) | collective-permute-done | bytes 65568 | tf_op jit(solution)/shard_map/ppermute | solution.py:198
  9.5 1.0 %copy-done.2 = bf16[3,3,3,64,128]{4,3,2,1,0:T(8,128)(2,1)S(1)} copy-done((bf16[3,3,3,64,128]{4,3,2,1,0:T(8,128)(2,1)S(1)}, bf16[3,3,3,64,128]{4,3,2,1,0:T(8,128)(2,1)}, u32[]{:S(2)}) %copy-start.2) | copy-done | bytes 442392
  10.5 2.9 %local_terms.1 = (bf16[16,1024]{1,0:T(8,128)(2,1)}, f32[4,472,128]{2,1,0:T(8,128)S(1)}, bf16[4,472,128]{2,1,0:T(8,128)(2,1)S(1)}) custom-call(s32[1]{0:T(128)S(6)} %copy.10.kind_ref, bf16[8,32,1024]{2,1,0:T(8,128)(2,1)S(1)} %bitcast.29, s32[8,512]{1,0:T(8,128)S(1)} %bitcast.33, bf16[32,1024]{1,0:T(8,128)(2,1)S(1)} %collective-permute-done.below_ref, ...), custom_call_target="tpu_custom_call" | custom-call | tf_op jit(solution)/shard_map/local_terms/pallas_call | solution.py:201
  13.5 1.8 %collective-permute-done.1 = bf16[4,472,128]{2,1,0:T(8,128)(2,1)S(1)} collective-permute-done((bf16[4,472,128]{2,1,0:T(8,128)(2,1)S(1)}, bf16[4,472,128]{2,1,0:T(8,128)(2,1)S(1)}, u32[]{:S(2)}, u32[]{:S(2)}) %collective-permute-start.1) | collective-permute-done | bytes 483360 | tf_op jit(solution)/shard_map/ppermute | solution.py:157
  15.5 2.4 %collective-permute-start.2 = (bf16[472,128]{1,0:T(8,128)(2,1)S(1)}, bf16[472,128]{1,0:T(8,128)(2,1)S(1)}, u32[]{:S(2)}, u32[]{:S(2)}) collective-permute-start(bf16[472,128]{1,0:T(8,128)(2,1)S(1)} %get-tuple-element.15), channel_id=1, source_target_pairs={{0,1},{1,0},{2,3},{3,2},{4,5},{5,4},{6,7},{7,6},{8,9},{9,8},{10,11... | collective-permute-start | bytes 362504 | tf_op jit(solution)/shard_map/ppermute | solution.py:157
  17.9 1.0 %collective-permute-start.4 = (bf16[472,128]{1,0:T(8,128)(2,1)S(1)}, bf16[472,128]{1,0:T(8,128)(2,1)S(1)}, u32[]{:S(2)}, u32[]{:S(2)}) collective-permute-start(bf16[472,128]{1,0:T(8,128)(2,1)S(1)} %get-tuple-element.16), channel_id=1, source_target_pairs={{0,17},{1,16},{2,19},{3,18},{4,21},{5,20},{6,23},{7,22},{8,25},{9,... | collective-permute-start | bytes 362504 | tf_op jit(solution)/shard_map/ppermute | solution.py:157
  18.9 0.5 %collective-permute-start.3 = (bf16[472,128]{1,0:T(8,128)(2,1)S(1)}, bf16[472,128]{1,0:T(8,128)(2,1)S(1)}, u32[]{:S(2)}, u32[]{:S(2)}) collective-permute-start(bf16[472,128]{1,0:T(8,128)(2,1)S(1)} %get-tuple-element.17), channel_id=1, source_target_pairs={{0,16},{1,17},{2,18},{3,19},{4,20},{5,21},{6,22},{7,23},{8,24},{9,... | collective-permute-start | bytes 362504 | tf_op jit(solution)/shard_map/ppermute | solution.py:157
  19.5 3.9 %collective-permute-done.2 = bf16[472,128]{1,0:T(8,128)(2,1)S(1)} collective-permute-done((bf16[472,128]{1,0:T(8,128)(2,1)S(1)}, bf16[472,128]{1,0:T(8,128)(2,1)S(1)}, u32[]{:S(2)}, u32[]{:S(2)}) %collective-permute-start.2) | collective-permute-done | bytes 120864 | tf_op jit(solution)/shard_map/ppermute | solution.py:157
  23.4 1.6 %collective-permute-done.4 = bf16[472,128]{1,0:T(8,128)(2,1)S(1)} collective-permute-done((bf16[472,128]{1,0:T(8,128)(2,1)S(1)}, bf16[472,128]{1,0:T(8,128)(2,1)S(1)}, u32[]{:S(2)}, u32[]{:S(2)}) %collective-permute-start.4) | collective-permute-done | bytes 120864 | tf_op jit(solution)/shard_map/ppermute | solution.py:157
  25.0 0.4 collective-permute-done.3
  25.5 2.7 %collective-permute-start.5 = (bf16[472,128]{1,0:T(8,128)(2,1)S(1)}, bf16[472,128]{1,0:T(8,128)(2,1)S(1)}, u32[]{:S(2)}, u32[]{:S(2)}) collective-permute-start(bf16[472,128]{1,0:T(8,128)(2,1)S(1)} %fusion.3), channel_id=1, source_target_pairs={{0,2},{1,3},{2,0},{3,1},{4,6},{5,7},{6,4},{7,5},{8,10},{9,11},{10,... | collective-permute-start | bytes 362504 | tf_op jit(solution)/shard_map/ppermute | solution.py:157
  28.1 2.8 %collective-permute-done.5 = bf16[472,128]{1,0:T(8,128)(2,1)S(1)} collective-permute-done((bf16[472,128]{1,0:T(8,128)(2,1)S(1)}, bf16[472,128]{1,0:T(8,128)(2,1)S(1)}, u32[]{:S(2)}, u32[]{:S(2)}) %collective-permute-start.5) | collective-permute-done | bytes 120864 | tf_op jit(solution)/shard_map/ppermute | solution.py:157
  31.0 3.1 %collective-permute-start.6 = (bf16[472,128]{1,0:T(8,128)(2,1)S(1)}, bf16[472,128]{1,0:T(8,128)(2,1)S(1)}, u32[]{:S(2)}, u32[]{:S(2)}) collective-permute-start(bf16[472,128]{1,0:T(8,128)(2,1)S(1)} %add_convert_fusion.1), channel_id=1, source_target_pairs={{0,4},{1,5},{2,6},{3,7},{4,0},{5,1},{6,2},{7,3},{8,12},{9,13},{10,... | collective-permute-start | bytes 362504 | tf_op jit(solution)/shard_map/ppermute | solution.py:157
  34.1 2.8 %collective-permute-done.6 = bf16[472,128]{1,0:T(8,128)(2,1)S(1)} collective-permute-done((bf16[472,128]{1,0:T(8,128)(2,1)S(1)}, bf16[472,128]{1,0:T(8,128)(2,1)S(1)}, u32[]{:S(2)}, u32[]{:S(2)}) %collective-permute-start.6) | collective-permute-done | bytes 120864 | tf_op jit(solution)/shard_map/ppermute | solution.py:157
  37.0 3.2 %collective-permute-start.9 = (bf16[472,128]{1,0:T(8,128)(2,1)S(1)}, bf16[472,128]{1,0:T(8,128)(2,1)S(1)}, u32[]{:S(2)}, u32[]{:S(2)}) collective-permute-start(bf16[472,128]{1,0:T(8,128)(2,1)S(1)} %add_convert_fusion), channel_id=1, source_target_pairs={{0,17},{1,16},{2,19},{3,18},{4,21},{5,20},{6,23},{7,22},{8,25},{9,... | collective-permute-start | bytes 362504 | tf_op jit(solution)/shard_map/ppermute | solution.py:157
  40.2 0.5 %collective-permute-start.8 = (bf16[472,128]{1,0:T(8,128)(2,1)S(1)}, bf16[472,128]{1,0:T(8,128)(2,1)S(1)}, u32[]{:S(2)}, u32[]{:S(2)}) collective-permute-start(bf16[472,128]{1,0:T(8,128)(2,1)S(1)} %add_convert_fusion), channel_id=1, source_target_pairs={{0,16},{1,17},{2,18},{3,19},{4,20},{5,21},{6,22},{7,23},{8,24},{9,... | collective-permute-start | bytes 362504 | tf_op jit(solution)/shard_map/ppermute | solution.py:157
  40.9 2.2 %collective-permute-done.9 = bf16[472,128]{1,0:T(8,128)(2,1)S(1)} collective-permute-done((bf16[472,128]{1,0:T(8,128)(2,1)S(1)}, bf16[472,128]{1,0:T(8,128)(2,1)S(1)}, u32[]{:S(2)}, u32[]{:S(2)}) %collective-permute-start.9) | collective-permute-done | bytes 120864 | tf_op jit(solution)/shard_map/ppermute | solution.py:157
  43.1 2.0 %collective-permute-done.8 = bf16[472,128]{1,0:T(8,128)(2,1)S(1)} collective-permute-done((bf16[472,128]{1,0:T(8,128)(2,1)S(1)}, bf16[472,128]{1,0:T(8,128)(2,1)S(1)}, u32[]{:S(2)}, u32[]{:S(2)}) %collective-permute-start.8) | collective-permute-done | bytes 120864 | tf_op jit(solution)/shard_map/ppermute | solution.py:157
  45.1 0.5 %collective-permute-done.7 = bf16[472,128]{1,0:T(8,128)(2,1)S(1)} collective-permute-done((bf16[472,128]{1,0:T(8,128)(2,1)S(1)}, bf16[472,128]{1,0:T(8,128)(2,1)S(1)}, u32[]{:S(2)}, u32[]{:S(2)}) %collective-permute-start.7) | collective-permute-done | bytes 120864 | tf_op jit(solution)/shard_map/ppermute | solution.py:157
  45.8 1.8 %collective-permute-done.10.far_ref = bf16[4,472,128]{2,1,0:T(8,128)(2,1)S(1)} collective-permute-done((bf16[4,472,128]{2,1,0:T(8,128)(2,1)S(1)}, bf16[4,472,128]{2,1,0:T(8,128)(2,1)S(1)}, u32[]{:S(2)}, u32[]{:S(2)}) %collective-permute-start.10) | collective-permute-done | bytes 483360 | tf_op jit(solution)/shard_map/ppermute | solution.py:157
  47.6 1.4 %spread_sums.1 = (f32[8,128,256]{2,1,0:T(8,128)}, f32[1728,128]{1,0:T(8,128)}) custom-call(bf16[4,472,128]{2,1,0:T(8,128)(2,1)S(1)} %pad_maximum_fusion.near_ref, bf16[4,472,128]{2,1,0:T(8,128)(2,1)S(1)} %collective-permute-done.10.far_ref), custom_call_target="tpu_custom_call" | custom-call | tf_op jit(solution)/shard_map/spread_sums/pallas_call | solution.py:229
  (19 shorter events, 0.9 us)
Async XLA Ops:
  0.6 1.0 %copy-start = (bf16[1,8,32,1024]{3,2,1,0:T(8,128)(2,1)S(1)}, bf16[1,8,32,1024]{3,2,1,0:T(8,128)(2,1)}, u32[]{:S(2)}) copy-start(bf16[1,8,32,1024]{3,2,1,0:T(8,128)(2,1)} %param.7) | copy-start | bytes 1572868
  1.7 0.7 %copy-start.3 = (s32[1,8,512]{2,1,0:T(8,128)S(1)}, s32[1,8,512]{2,1,0:T(8,128)}, u32[]{:S(2)}) copy-start(s32[1,8,512]{2,1,0:T(8,128)} %param.8) | copy-start | bytes 49156
  2.4 7.1 %copy-start.1 = (bf16[2,2,2,128,256]{4,3,2,1,0:T(8,128)(2,1)S(1)}, bf16[2,2,2,128,256]{4,3,2,1,0:T(8,128)(2,1)}, u32[]{:S(2)}) copy-start(bf16[2,2,2,128,256]{4,3,2,1,0:T(8,128)(2,1)} %param.12) | copy-start | bytes 1572868
  2.4 7.1 %copy-start.4 = (bf16[1,2,8,1024]{3,2,1,0:T(8,128)(2,1)S(1)}, bf16[1,2,8,1024]{3,2,1,0:T(8,128)(2,1)}, u32[]{:S(2)}) copy-start(bf16[1,2,8,1024]{3,2,1,0:T(8,128)(2,1)} %param.13) | copy-start | bytes 98308
  2.7 6.8 %copy-start.5 = (f32[8,128]{1,0:T(8,128)S(1)}, f32[8,128]{1,0:T(8,128)}, u32[]{:S(2)}) copy-start(f32[8,128]{1,0:T(8,128)} %bias_ref.1) | copy-start | bytes 12292
  2.7 6.8 %collective-permute-start = (bf16[32,1024]{1,0:T(8,128)(2,1)S(1)}, bf16[32,1024]{1,0:T(8,128)(2,1)S(1)}, u32[]{:S(2)}, u32[]{:S(2)}) collective-permute-start(bf16[32,1024]{1,0:T(8,128)(2,1)S(1)} %edge_plane.1), channel_id=1, source_target_pairs={{0,1},{1,2},{2,3},{3,4},{4,5},{5,6},{6,7},{8,9},{9,10},{10,11},{11... | collective-permute-start | bytes 196616 | tf_op jit(solution)/shard_map/ppermute | solution.py:198
  9.5 1.0 %copy-start.2 = (bf16[3,3,3,64,128]{4,3,2,1,0:T(8,128)(2,1)S(1)}, bf16[3,3,3,64,128]{4,3,2,1,0:T(8,128)(2,1)}, u32[]{:S(2)}) copy-start(bf16[3,3,3,64,128]{4,3,2,1,0:T(8,128)(2,1)} %param.10) | copy-start | bytes 1327108
  13.4 1.9 %collective-permute-start.1 = (bf16[4,472,128]{2,1,0:T(8,128)(2,1)S(1)}, bf16[4,472,128]{2,1,0:T(8,128)(2,1)S(1)}, u32[]{:S(2)}, u32[]{:S(2)}) collective-permute-start(bf16[4,472,128]{2,1,0:T(8,128)(2,1)S(1)} %get-tuple-element.10), channel_id=1, source_target_pairs={{0,8},{1,9},{2,10},{3,11},{4,12},{5,13},{6,14},{7,15},{8,0},{9,1},... | collective-permute-start | bytes 1449992 | tf_op jit(solution)/shard_map/ppermute | solution.py:157
  15.5 7.9 %collective-permute-start.2 = (bf16[472,128]{1,0:T(8,128)(2,1)S(1)}, bf16[472,128]{1,0:T(8,128)(2,1)S(1)}, u32[]{:S(2)}, u32[]{:S(2)}) collective-permute-start(bf16[472,128]{1,0:T(8,128)(2,1)S(1)} %get-tuple-element.15), channel_id=1, source_target_pairs={{0,1},{1,0},{2,3},{3,2},{4,5},{5,4},{6,7},{7,6},{8,9},{9,8},{10,11... | collective-permute-start | bytes 362504 | tf_op jit(solution)/shard_map/ppermute | solution.py:157
  17.9 7.1 %collective-permute-start.4 = (bf16[472,128]{1,0:T(8,128)(2,1)S(1)}, bf16[472,128]{1,0:T(8,128)(2,1)S(1)}, u32[]{:S(2)}, u32[]{:S(2)}) collective-permute-start(bf16[472,128]{1,0:T(8,128)(2,1)S(1)} %get-tuple-element.16), channel_id=1, source_target_pairs={{0,17},{1,16},{2,19},{3,18},{4,21},{5,20},{6,23},{7,22},{8,25},{9,... | collective-permute-start | bytes 362504 | tf_op jit(solution)/shard_map/ppermute | solution.py:157
  18.9 6.5 %collective-permute-start.3 = (bf16[472,128]{1,0:T(8,128)(2,1)S(1)}, bf16[472,128]{1,0:T(8,128)(2,1)S(1)}, u32[]{:S(2)}, u32[]{:S(2)}) collective-permute-start(bf16[472,128]{1,0:T(8,128)(2,1)S(1)} %get-tuple-element.17), channel_id=1, source_target_pairs={{0,16},{1,17},{2,18},{3,19},{4,20},{5,21},{6,22},{7,23},{8,24},{9,... | collective-permute-start | bytes 362504 | tf_op jit(solution)/shard_map/ppermute | solution.py:157
  25.5 5.5 %collective-permute-start.5 = (bf16[472,128]{1,0:T(8,128)(2,1)S(1)}, bf16[472,128]{1,0:T(8,128)(2,1)S(1)}, u32[]{:S(2)}, u32[]{:S(2)}) collective-permute-start(bf16[472,128]{1,0:T(8,128)(2,1)S(1)} %fusion.3), channel_id=1, source_target_pairs={{0,2},{1,3},{2,0},{3,1},{4,6},{5,7},{6,4},{7,5},{8,10},{9,11},{10,... | collective-permute-start | bytes 362504 | tf_op jit(solution)/shard_map/ppermute | solution.py:157
  31.0 5.9 %collective-permute-start.6 = (bf16[472,128]{1,0:T(8,128)(2,1)S(1)}, bf16[472,128]{1,0:T(8,128)(2,1)S(1)}, u32[]{:S(2)}, u32[]{:S(2)}) collective-permute-start(bf16[472,128]{1,0:T(8,128)(2,1)S(1)} %add_convert_fusion.1), channel_id=1, source_target_pairs={{0,4},{1,5},{2,6},{3,7},{4,0},{5,1},{6,2},{7,3},{8,12},{9,13},{10,... | collective-permute-start | bytes 362504 | tf_op jit(solution)/shard_map/ppermute | solution.py:157
  37.0 6.1 %collective-permute-start.9 = (bf16[472,128]{1,0:T(8,128)(2,1)S(1)}, bf16[472,128]{1,0:T(8,128)(2,1)S(1)}, u32[]{:S(2)}, u32[]{:S(2)}) collective-permute-start(bf16[472,128]{1,0:T(8,128)(2,1)S(1)} %add_convert_fusion), channel_id=1, source_target_pairs={{0,17},{1,16},{2,19},{3,18},{4,21},{5,20},{6,23},{7,22},{8,25},{9,... | collective-permute-start | bytes 362504 | tf_op jit(solution)/shard_map/ppermute | solution.py:157
  40.2 4.9 %collective-permute-start.8 = (bf16[472,128]{1,0:T(8,128)(2,1)S(1)}, bf16[472,128]{1,0:T(8,128)(2,1)S(1)}, u32[]{:S(2)}, u32[]{:S(2)}) collective-permute-start(bf16[472,128]{1,0:T(8,128)(2,1)S(1)} %add_convert_fusion), channel_id=1, source_target_pairs={{0,16},{1,17},{2,18},{3,19},{4,20},{5,21},{6,22},{7,23},{8,24},{9,... | collective-permute-start | bytes 362504 | tf_op jit(solution)/shard_map/ppermute | solution.py:157
  40.8 4.9 %collective-permute-start.7 = (bf16[472,128]{1,0:T(8,128)(2,1)S(1)}, bf16[472,128]{1,0:T(8,128)(2,1)S(1)}, u32[]{:S(2)}, u32[]{:S(2)}) collective-permute-start(bf16[472,128]{1,0:T(8,128)(2,1)S(1)} %add_convert_fusion), channel_id=1, source_target_pairs={{0,1},{1,0},{2,3},{3,2},{4,5},{5,4},{6,7},{7,6},{8,9},{9,8},{10,11... | collective-permute-start | bytes 362504 | tf_op jit(solution)/shard_map/ppermute | solution.py:157
  45.7 1.9 %collective-permute-start.10 = (bf16[4,472,128]{2,1,0:T(8,128)(2,1)S(1)}, bf16[4,472,128]{2,1,0:T(8,128)(2,1)S(1)}, u32[]{:S(2)}, u32[]{:S(2)}) collective-permute-start(bf16[4,472,128]{2,1,0:T(8,128)(2,1)S(1)} %pad_maximum_fusion.near_ref), channel_id=1, source_target_pairs={{0,8},{1,9},{2,10},{3,11},{4,12},{5,13},{6,14},{7,15},{8,0},{9,1},... | collective-permute-start | bytes 1449992 | tf_op jit(solution)/shard_map/ppermute | solution.py:157

commit v2 on v1

v2 whole, which is shorter than its diff:
```python
import jax
import jax.numpy as jnp
from jax import lax
from jax.experimental import pallas as pl
from jax.experimental.pallas import tpu as pltpu
from jax.sharding import PartitionSpec as P

SLOPE = 0.3
BF16 = jnp.bfloat16
F32 = jnp.float32

DEPTH, ROWS, CELLS, C0, C1, C2 = 8, 32, 16, 64, 128, 256
PAIR = 2 * C0
WIDE = CELLS * C0
CHUNKS = 8
DEEP_ROWS = 8 * C1 * C2 // 128 // CHUNKS
EARLY_ROWS = 27 * C0 // CHUNKS
CHUNK_ROWS = DEEP_ROWS + EARLY_ROWS
VMEM_BYTES = 48 * 1024 * 1024


def iota(shape, dim):
    return lax.broadcasted_iota(jnp.int32, shape, dim)


def masked_rows(acts, opens):
    planes = opens.shape[0]
    cells = ROWS * CELLS
    own = (iota((ROWS, cells), 1) // CELLS) == iota((ROWS, cells), 0)
    spread = jnp.concatenate(
        [jnp.where(own, opens[z : z + 1, :], 0).astype(F32).astype(BF16) for z in range(planes)], axis=0
    )
    pick = ((iota((cells, 128), 0) % CELLS) == iota((cells, 128), 1)).astype(F32).astype(BF16)
    by_cell = jnp.dot(spread, pick, preferred_element_type=F32).astype(BF16)
    widen = (iota((128, WIDE), 0) == (iota((128, WIDE), 1) // C0)).astype(F32).astype(BF16)
    mask = jnp.dot(by_cell, widen, preferred_element_type=F32).astype(BF16)
    return acts * mask


def edge_kernel(
    acts_ref, opens_ref, table_ref, w1_hbm, edge_ref, cells_ref, bias_ref, w1_ref, plane_ref, sems
):
    plane = pltpu.make_async_copy(acts_ref.at[DEPTH - 1], plane_ref, sems.at[0])
    cells = pltpu.make_async_copy(opens_ref, cells_ref, sems.at[1])
    table = pltpu.make_async_copy(table_ref, bias_ref, sems.at[2])
    plane.start()
    cells.start()
    table.start()
    early = pltpu.make_async_copy(w1_hbm, w1_ref, sems.at[3])
    early.start()
    cells.wait()
    table.wait()
    plane.wait()
    edge_ref[...] = masked_rows(plane_ref[...], cells_ref[DEPTH - 1 :])
    early.wait()


def places():
    core = lax.axis_index("sample") % 2
    x = (lax.axis_index("sample") // 2) % 2
    y = lax.axis_index("space") % 2
    own = jnp.where(core == 0, 2 * x + y, 2 * y + x)
    other = jnp.where(core == 0, 2 * y + x, 2 * x + y)
    return core, own, other


def chunk_of(m, far):
    core, own, other = places()
    return (1 - core) * 4 + (other ^ m) if far else core * 4 + (own ^ m)


def row_of_slot(q):
    return 2 * (q % 8) + q // 8


def windows(parts):
    return jnp.concatenate(
        [ref[b, top : top + n, x * PAIR : (x + 2) * PAIR] for x in range(CELLS // 2) for ref, b, top, n in parts],
        axis=0,
    )


def tap_weight(w):
    return jnp.concatenate([jnp.zeros((C0, C1), BF16), w], axis=0)


def inner_kernel(
    acts_ref, opens_ref, bias_ref, w1_ref, w2_hbm,
    even_ref, odd_ref, pre_ref, w2_ref,
    sem,
):
    fetch = pltpu.make_async_copy(w2_hbm, w2_ref, sem)
    fetch.start()
    field = masked_rows(acts_ref[...].reshape(DEPTH * ROWS, WIDE), opens_ref[...])
    half = 3 * 64
    r = iota((2 * half, DEPTH * ROWS), 0)
    par = (r >= half).astype(jnp.int32)
    s = r - half * par
    y = 2 * row_of_slot(s % 16) + s // 64 - 1
    z = 2 * ((s % 64) // 16) + par
    want = jnp.where(y >= 0, z * ROWS + y, -1)
    pick = (iota(r.shape, 1) == want).astype(F32).astype(BF16)
    rows = jnp.dot(pick, field, preferred_element_type=F32).astype(BF16)
    for ref, top in ((even_ref, 0), (odd_ref, half)):
        for b in range(3):
            ref[b, :, :PAIR] = jnp.zeros((64, PAIR), BF16)
            ref[b, :, PAIR:] = rows[top + b * 64 : top + (b + 1) * 64]
    pre = bias_ref[...]
    for a, ref in ((1, even_ref), (2, odd_ref)):
        for b in range(3):
            w = tap_weight(w1_ref[a * 3 + b])
            pre = pre + jnp.dot(windows([(ref, b, 0, 64)]), w, preferred_element_type=F32)
    over = jnp.zeros((8 * 48, C1), F32)
    for b in range(3):
        w = tap_weight(w1_ref[b])
        over = over + jnp.dot(windows([(odd_ref, b, 0, 48)]), w, preferred_element_type=F32)
    for x in range(8):
        pre_ref[x * 64 : x * 64 + 16] = pre[x * 64 : x * 64 + 16]
        pre_ref[x * 64 + 16 : (x + 1) * 64] = (
            pre[x * 64 + 16 : (x + 1) * 64] + over[x * 48 : (x + 1) * 48]
        )
    fetch.wait()


def local_kernel(
    below_ref, first_ref, even_ref, odd_ref, pre_ref, w2_ref, cot_ref,
    deep_ref, keep0_ref, keep1_ref, keep2_ref, keep3_ref, send0_ref, send1_ref, send2_ref, send3_ref,
    under_ref, patch_ref, early_ref,
):
    r = iota((48, ROWS), 0)
    y = 2 * row_of_slot(r % 16) + r // 16 - 1
    pick = (iota(r.shape, 1) == y).astype(F32).astype(BF16)
    rows = jnp.dot(pick, below_ref[...], preferred_element_type=F32).astype(BF16)
    for b in range(3):
        under_ref[b, :, :PAIR] = jnp.zeros((16, PAIR), BF16)
        under_ref[b, :, PAIR:] = rows[b * 16 : (b + 1) * 16]
    low = jnp.zeros((8 * 16, C1), F32)
    for b in range(3):
        w = tap_weight(first_ref[b])
        low = low + jnp.dot(windows([(under_ref, b, 0, 16)]), w, preferred_element_type=F32)
    pre = jnp.concatenate(
        [
            part
            for x in range(8)
            for part in (
                pre_ref[x * 64 : x * 64 + 16] + low[x * 16 : (x + 1) * 16],
                pre_ref[x * 64 + 16 : (x + 1) * 64],
            )
        ],
        axis=0,
    )

    def rows_of(a, b):
        if a == 0:
            return windows([(under_ref, b, 0, 16), (odd_ref, b, 0, 48)])
        return windows([(even_ref if a == 1 else odd_ref, b, 0, 64)])

    hidden = jnp.where(pre > 0, pre, SLOPE * pre)

    def piece(xs, zs, a, b, c):
        return (2 * xs + c) * 64 + (2 * zs + a) * 16 + b * 8

    pieces = [(xs, zs) for xs in range(CELLS // 4) for zs in range(DEPTH // 4)]
    taps = [(a, b, c) for a in range(2) for b in range(2) for c in range(2)]
    cot = jnp.concatenate([cot_ref[:, x * C2 : (x + 1) * C2] for x in range(CELLS // 4)], axis=0)
    out = jnp.zeros((64, C2), F32)
    delta_at = {}
    for t, (a, b, c) in enumerate(taps):
        starts = [piece(xs, zs, a, b, c) for xs, zs in pieces]
        patch = jnp.concatenate([hidden[at : at + 8] for at in starts], axis=0).astype(BF16)
        patch_ref[t] = patch
        out = out + jnp.dot(patch, w2_ref[t], preferred_element_type=F32)
        back = lax.dot_general(cot, w2_ref[t], (((1,), (1,)), ((), ())), preferred_element_type=F32)
        for k, at in enumerate(starts):
            delta_at[at] = back[k * 8 : (k + 1) * 8]
    out = out.astype(BF16)
    for x in range(CELLS // 4):
        deep_ref[:, x * C2 : (x + 1) * C2] = out[x * 16 : (x + 1) * 16]
    back = jnp.concatenate([delta_at[at] for at in sorted(delta_at)], axis=0)
    delta = (back * jnp.where(pre > 0, 1.0, SLOPE)).astype(BF16)

    for a in range(3):
        for b in range(3):
            grad = lax.dot_general(
                rows_of(a, b), delta, (((0,), (0,)), ((), ())), preferred_element_type=F32
            )
            at = (a * 3 + b) * 3 * C0
            early_ref[at : at + 3 * C0] = grad[C0:]

    for far in range(2):
        for m in range(4):
            chunk = chunk_of(m, far)
            grad = lax.dot_general(
                patch_ref[chunk], cot, (((0,), (0,)), ((), ())), preferred_element_type=F32
            )
            early = early_ref[pl.ds(pl.multiple_of(chunk * EARLY_ROWS, 8), EARLY_ROWS), :]
            keeps = (keep0_ref, keep1_ref, keep2_ref, keep3_ref)
            ref = ((send0_ref, send1_ref, send2_ref, send3_ref) if far else keeps)[m]
            kind = BF16 if far else F32
            ref[:C1] = grad[:, :128].astype(kind)
            ref[C1 : 2 * C1] = grad[:, 128:].astype(kind)
            ref[2 * C1 :] = early.astype(kind)


def spread_kernel(*refs):
    deep_ref, early_ref, wide_ref, low_ref, sems = refs[8:]
    copies = []
    for k in range(8):
        chunk = chunk_of(k % 4, k // 4)
        wide_ref[k, :, :128] = refs[k][:C1].astype(F32)
        wide_ref[k, :, 128:] = refs[k][C1 : 2 * C1].astype(F32)
        copies.append(pltpu.make_async_copy(wide_ref.at[k], deep_ref.at[chunk], sems.at[2 * k]))
        copies[-1].start()
        low_ref[k] = refs[k][2 * C1 :].astype(F32)
        at = pl.multiple_of(chunk * EARLY_ROWS, 8)
        copies.append(
            pltpu.make_async_copy(
                low_ref.at[k], early_ref.at[pl.ds(at, EARLY_ROWS), :], sems.at[2 * k + 1]
            )
        )
        copies[-1].start()
    for copy in copies:
        copy.wait()


def spread(chunks):
    return pl.pallas_call(
        spread_kernel,
        in_specs=[pl.BlockSpec(memory_space=pltpu.VMEM)] * 8,
        out_specs=[pl.BlockSpec(memory_space=pltpu.HBM)] * 2,
        out_shape=[
            jax.ShapeDtypeStruct((8, C1, C2), F32),
            jax.ShapeDtypeStruct((27 * C0, C1), F32),
        ],
        scratch_shapes=[
            pltpu.VMEM((8, C1, C2), F32),
            pltpu.VMEM((8, EARLY_ROWS, 128), F32),
            pltpu.SemaphoreType.DMA((16,)),
        ],
        compiler_params=pltpu.CompilerParams(vmem_limit_bytes=VMEM_BYTES),
        name="spread_sums",
    )(*chunks)


def swapped(value, flips):
    samples, spaces = lax.axis_size("sample"), lax.axis_size("space")
    pairs = [
        (i * spaces + j, (i ^ flips[i % 2][0]) * spaces + (j ^ flips[i % 2][1]))
        for i in range(samples)
        for j in range(spaces)
    ]
    return lax.ppermute(value, ("sample", "space"), pairs)


SIBLING = ((1, 0), (1, 0))
QUAD = {m: ((m // 2 * 2, m % 2), (m % 2 * 2, m // 2)) for m in (1, 2, 3)}


def total(keep, send):
    got = {m: swapped(send[m], SIBLING) for m in (3, 2, 1, 0)}
    quad = {}
    for m in (3, 2, 1):
        quad[m] = swapped((keep[m] + got[m].astype(F32)).astype(BF16), QUAD[m])
    mine = keep[0] + got[0].astype(F32)
    for m in (3, 2, 1):
        mine = mine + quad[m].astype(F32)
    rest = []
    for axis, bit in (("space", 2), ("sample", 4)):
        while bit < lax.axis_size(axis):
            rest.append((bit, 0) if axis == "sample" else (0, bit))
            bit *= 2
    for flips in zip(rest, rest[::-1]):
        own = mine.astype(BF16)
        mine = own.astype(F32) + swapped(own, flips).astype(F32)
    near = {0: mine.astype(BF16)}
    for m in (3, 2, 1):
        near[m] = swapped(near[0], QUAD[m])
    far = {m: swapped(near[m], SIBLING) for m in range(4)}
    return [near[m] for m in range(4)] + [far[m] for m in range(4)]


def in_hbm(value):
    return pltpu.with_memory_space_constraint(value, pltpu.HBM)


def body(activations, open_cells, wind_class, w_early, bias_table, w_deep, cotangent):
    params = pltpu.CompilerParams(vmem_limit_bytes=VMEM_BYTES)
    acts = activations[0]
    opens = open_cells[0]
    vmem = pl.BlockSpec(memory_space=pltpu.VMEM)
    hbm = pl.BlockSpec(memory_space=pltpu.HBM)
    edge, opens, table, early = pl.pallas_call(
        edge_kernel,
        in_specs=[hbm] * 4,
        out_specs=[vmem] * 4,
        out_shape=[
            jax.ShapeDtypeStruct((ROWS, WIDE), BF16),
            jax.ShapeDtypeStruct(opens.shape, opens.dtype),
            jax.ShapeDtypeStruct(bias_table.shape, bias_table.dtype),
            jax.ShapeDtypeStruct((9, 3 * C0, C1), BF16),
        ],
        scratch_shapes=[pltpu.VMEM((ROWS, WIDE), BF16), pltpu.SemaphoreType.DMA((4,))],
        compiler_params=params,
        name="edge_plane",
    )(in_hbm(acts), in_hbm(opens), in_hbm(bias_table), in_hbm(w_early.reshape(9, 3 * C0, C1)))
    spaces = lax.axis_size("space")
    below = lax.ppermute(edge, "space", [(i, i + 1) for i in range(spaces - 1)])
    chosen = jnp.arange(bias_table.shape[0], dtype=jnp.int32)[:, None] == wind_class[0]
    bias = jnp.sum(jnp.where(chosen, table, jnp.zeros_like(table)), axis=0, keepdims=True)
    pair_rows = jax.ShapeDtypeStruct((3, 64, WIDE + PAIR), BF16)
    inner = pl.pallas_call(
        inner_kernel,
        in_specs=[vmem] * 4 + [hbm],
        out_specs=[vmem] * 4,
        out_shape=[
            pair_rows,
            pair_rows,
            jax.ShapeDtypeStruct((512, C1), F32),
            jax.ShapeDtypeStruct((8, C1, C2), BF16),
        ],
        scratch_shapes=[pltpu.SemaphoreType.DMA],
        compiler_params=params,
        name="inner_terms",
    )(
        acts,
        opens,
        bias,
        early,
        in_hbm(w_deep.reshape(8, C1, C2)),
    )
    deep, *chunks = pl.pallas_call(
        local_kernel,
        in_specs=[vmem] * 7,
        out_specs=[vmem] * 9,
        out_shape=[
            jax.ShapeDtypeStruct((DEPTH // 4 * ROWS // 4, CELLS // 4 * C2), BF16),
        ]
        + [jax.ShapeDtypeStruct((CHUNK_ROWS, 128), F32)] * 4
        + [jax.ShapeDtypeStruct((CHUNK_ROWS, 128), BF16)] * 4,
        scratch_shapes=[
            pltpu.VMEM((3, 16, WIDE + PAIR), BF16),
            pltpu.VMEM((8, 64, C1), BF16),
            pltpu.VMEM((27 * C0, C1), F32),
        ],
        compiler_params=params,
        name="local_terms",
    )(below, early, *inner, cotangent.reshape(DEPTH // 4 * ROWS // 4, CELLS // 4 * C2))
    grad_deep, grad_early = spread(total(chunks[:4], chunks[4:]))
    return (
        deep.reshape(1, DEPTH // 4, ROWS // 4, CELLS // 4 * C2),
        grad_deep.reshape(w_deep.shape),
        grad_early.reshape(w_early.shape),
    )


def solution(mesh):
    in_specs = (
        P("sample", "space", None, None),
        P("sample", "space", None),
        P("sample"),
        P(),
        P(),
        P(),
        P("sample", "space", None, None),
    )
    out_specs = (P("sample", "space", None, None), P(), P())
    return jax.shard_map(body, mesh=mesh, in_specs=in_specs, out_specs=out_specs, check_vma=False)
```

time: 49.3 us -> 43.8 us (0.89)
  waiting for transfers between devices: 21.3 us -> 18 us
  local copies, waits for them, and re-layouts: 2.8 us -> 0.01 us
  Pallas kernels: 4.59 us -> 5.57 us
    unnamed x12 -> x4, local copies, waits for them, and re-layouts: 2.77 us -> 0.01 us
    ppermute x10 -> x16, waiting for transfers between devices: 20 us -> 18 us  [swapped(): return lax.ppermute(value, ('sample', 'space'), pairs)]
    ppermute x1, waiting for transfers between devices: 1.24 us -> 0.01 us  [body(): below = lax.ppermute(edge, 'space', [(i, i + 1) for i in range(spaces - 1)])]
    pallas_call x3 -> x4, Pallas kernels: 4.59 us -> 5.57 us  [the longest x1 1.52 us: body(): pl.pallas_call(local_kernel, in_specs=[vmem] * 7, out_specs=[vmem] * 9, o...]
    ppermute x10 -> x16, starting transfers between devices: 13.8 us -> 13.5 us  [swapped(): return lax.ppermute(value, ('sample', 'space'), pairs)]
  transfers between devices with their start and end apart: 11 -> 17, of which waited for: 11 -> 10; matrix products, arithmetic and copies ran while one was open for 0% -> 0% of each run, Pallas kernels for 0% -> 3%
where the time goes in v2:
time: 43.8 us; the launch traced here: 43.7 us
  starting transfers between devices  18.4 us (42%)
  waiting for transfers between devices  18 us (41%)
  Pallas kernels  5.57 us (13%)
  between operations  1.39 us (3%)
    ppermute x16, waiting for transfers between devices, swapped(): return lax.ppermute(value, ('sample', 'space'), pairs)  18 us
    ppermute x16, starting transfers between devices, swapped(): return lax.ppermute(value, ('sample', 'space'), pairs)  13.5 us
    ppermute x1, starting transfers between devices, body(): below = lax.ppermute(edge, 'space', [(i, i + 1) for i in range(spaces - 1)])  4.87 us
    pallas_call x1, Pallas kernels, body(): pl.pallas_call(local_kernel, in_specs=[vmem] * 7, out_specs=[vmem] * 9, o...  1.52 us
    pallas_call x1, Pallas kernels, body(): pl.pallas_call(inner_kernel, in_specs=[vmem] * 4 + [hbm], out_specs=[vmem...  1.41 us
    pallas_call x1, Pallas kernels, spread(): pl.pallas_call(spread_kernel, in_specs=[pl.BlockSpec(memory_space=pltpu.V...  1.41 us
    pallas_call x1, Pallas kernels, body(): pl.pallas_call(edge_kernel, in_specs=[hbm] * 4, out_specs=[vmem] * 4, out...  1.23 us
  transfers between devices with their start and end apart: 17, of which 10 were waited for; matrix products, arithmetic and copies ran while one was open for 0% of the time, Pallas kernels for 3%

profile of v2, /device:TPU:0, one launch (start us, length us, event | category | flops | bytes accessed | tf_op | source)
XLA Modules:
  0.0 43.7 jit_solution(950861396490334076)
XLA Ops:
  0.6 1.2 %edge_plane.1 = (bf16[32,1024]{1,0:T(8,128)(2,1)S(1)}, s32[8,512]{1,0:T(8,128)S(1)}, f32[8,128]{1,0:T(8,128)S(1)}, bf16[9,192,128]{2,1,0:T(8,128)(2,1)S(1)}) custom-call(bf16[8,32,1024]{2,1,0:T(8,128)(2,1)} %bitcast.11, s32[8,512]{1,0:T(8,128)} %bitcast.17, f32[8,128]{1,0:T(8,128)} %table_ref.1, bf16[9,192,128]{2,1,0:T(8,128)(2,1)} %bitcast.16), custom_call_target="tpu_custom_call" | custom-call | tf_op jit(solution)/shard_map/edge_plane/pallas_call | solution.py:292
  1.9 4.9 %collective-permute-start = (bf16[32,1024]{1,0:T(8,128)(2,1)S(1)}, bf16[32,1024]{1,0:T(8,128)(2,1)S(1)}, u32[]{:S(2)}, u32[]{:S(2)}) collective-permute-start(bf16[32,1024]{1,0:T(8,128)(2,1)S(1)} %get-tuple-element.22), channel_id=1, source_target_pairs={{0,1},{1,2},{2,3},{3,4},{4,5},{5,6},{6,7},{8,9},{9,10},{10,11},{11... | collective-permute-start | bytes 196616 | tf_op jit(solution)/shard_map/ppermute | solution.py:307
  7.5 1.4 %inner_terms.1 = (bf16[3,64,1152]{2,1,0:T(8,128)(2,1)S(1)}, bf16[3,64,1152]{2,1,0:T(8,128)(2,1)S(1)}, f32[512,128]{1,0:T(8,128)S(1)}, bf16[8,128,256]{2,1,0:T(8,128)(2,1)S(1)}) custom-call(bf16[8,32,1024]{2,1,0:T(8,128)(2,1)S(1)} %bitcast.12, s32[8,512]{1,0:T(8,128)S(1)} %get-tuple-element.24.opens_ref, f32[1,128]{1,0:T(1,128)S(1)} %bitcast.14, ...), custom_call_target="tpu_custom_call" | custom-call | tf_op jit(solution)/shard_map/inner_terms/pallas_call | solution.py:311
  8.9 1.5 %local_terms.1 = (bf16[16,1024]{1,0:T(8,128)(2,1)}, f32[472,128]{1,0:T(8,128)S(1)}, f32[472,128]{1,0:T(8,128)S(1)}, f32[472,128]{1,0:T(8,128)S(1)}, f32[472,128]...) custom-call(bf16[32,1024]{1,0:T(8,128)(2,1)S(1)} %collective-permute, ...), custom_call_target="tpu_custom_call" | custom-call | tf_op jit(solution)/shard_map/local_terms/pallas_call | solution.py:331
  10.6 0.5 %collective-permute-start.1 = (bf16[472,128]{1,0:T(8,128)(2,1)S(1)}, bf16[472,128]{1,0:T(8,128)(2,1)S(1)}, u32[]{:S(2)}, u32[]{:S(2)}) collective-permute-start(bf16[472,128]{1,0:T(8,128)(2,1)S(1)} %get-tuple-element.32), channel_id=1, source_target_pairs={{0,8},{1,9},{2,10},{3,11},{4,12},{5,13},{6,14},{7,15},{8,0},{9,1},... | collective-permute-start | bytes 362504 | tf_op jit(solution)/shard_map/ppermute | solution.py:252
  11.1 0.4 collective-permute-start.6
  11.9 3.0 %collective-permute-start.3 = (bf16[472,128]{1,0:T(8,128)(2,1)S(1)}, bf16[472,128]{1,0:T(8,128)(2,1)S(1)}, u32[]{:S(2)}, u32[]{:S(2)}) collective-permute-start(bf16[472,128]{1,0:T(8,128)(2,1)S(1)} %add_convert_fusion.5), channel_id=1, source_target_pairs={{0,17},{1,16},{2,19},{3,18},{4,21},{5,20},{6,23},{7,22},{8,25},{9,... | collective-permute-start | bytes 362504 | tf_op jit(solution)/shard_map/ppermute | solution.py:252
  15.0 0.6 %collective-permute-start.5 = (bf16[472,128]{1,0:T(8,128)(2,1)S(1)}, bf16[472,128]{1,0:T(8,128)(2,1)S(1)}, u32[]{:S(2)}, u32[]{:S(2)}) collective-permute-start(bf16[472,128]{1,0:T(8,128)(2,1)S(1)} %add_convert_fusion.4), channel_id=1, source_target_pairs={{0,16},{1,17},{2,18},{3,19},{4,20},{5,21},{6,22},{7,23},{8,9},{9,8... | collective-permute-start | bytes 362504 | tf_op jit(solution)/shard_map/ppermute | solution.py:252
  15.6 0.5 %collective-permute-start.7 = (bf16[472,128]{1,0:T(8,128)(2,1)S(1)}, bf16[472,128]{1,0:T(8,128)(2,1)S(1)}, u32[]{:S(2)}, u32[]{:S(2)}) collective-permute-start(bf16[472,128]{1,0:T(8,128)(2,1)S(1)} %add_convert_fusion.3), channel_id=1, source_target_pairs={{0,1},{1,0},{2,3},{3,2},{4,5},{5,4},{6,7},{7,6},{8,24},{9,25},{10,... | collective-permute-start | bytes 362504 | tf_op jit(solution)/shard_map/ppermute | solution.py:252
  16.1 2.5 %collective-permute-done.3 = bf16[472,128]{1,0:T(8,128)(2,1)S(1)} collective-permute-done((bf16[472,128]{1,0:T(8,128)(2,1)S(1)}, bf16[472,128]{1,0:T(8,128)(2,1)S(1)}, u32[]{:S(2)}, u32[]{:S(2)}) %collective-permute-start.3) | collective-permute-done | bytes 120864 | tf_op jit(solution)/shard_map/ppermute | solution.py:252
  18.6 2.8 %collective-permute-done.5 = bf16[472,128]{1,0:T(8,128)(2,1)S(1)} collective-permute-done((bf16[472,128]{1,0:T(8,128)(2,1)S(1)}, bf16[472,128]{1,0:T(8,128)(2,1)S(1)}, u32[]{:S(2)}, u32[]{:S(2)}) %collective-permute-start.5) | collective-permute-done | bytes 120864 | tf_op jit(solution)/shard_map/ppermute | solution.py:252
  21.5 2.5 %collective-permute-start.8 = (bf16[472,128]{1,0:T(8,128)(2,1)S(1)}, bf16[472,128]{1,0:T(8,128)(2,1)S(1)}, u32[]{:S(2)}, u32[]{:S(2)}) collective-permute-start(bf16[472,128]{1,0:T(8,128)(2,1)S(1)} %add_convert_fusion.2), channel_id=1, source_target_pairs={{0,2},{1,3},{2,0},{3,1},{4,6},{5,7},{6,4},{7,5},{8,12},{9,13},{10,... | collective-permute-start | bytes 362504 | tf_op jit(solution)/shard_map/ppermute | solution.py:252
  24.0 4.0 %collective-permute-done.8 = bf16[472,128]{1,0:T(8,128)(2,1)S(1)} collective-permute-done((bf16[472,128]{1,0:T(8,128)(2,1)S(1)}, bf16[472,128]{1,0:T(8,128)(2,1)S(1)}, u32[]{:S(2)}, u32[]{:S(2)}) %collective-permute-start.8) | collective-permute-done | bytes 120864 | tf_op jit(solution)/shard_map/ppermute | solution.py:252
  28.0 2.2 %collective-permute-start.9 = (bf16[472,128]{1,0:T(8,128)(2,1)S(1)}, bf16[472,128]{1,0:T(8,128)(2,1)S(1)}, u32[]{:S(2)}, u32[]{:S(2)}) collective-permute-start(bf16[472,128]{1,0:T(8,128)(2,1)S(1)} %add_convert_fusion.1), channel_id=1, source_target_pairs={{0,4},{1,5},{2,6},{3,7},{4,0},{5,1},{6,2},{7,3},{8,10},{9,11},{10,... | collective-permute-start | bytes 362504 | tf_op jit(solution)/shard_map/ppermute | solution.py:252
  30.2 3.6 %collective-permute-done.9 = bf16[472,128]{1,0:T(8,128)(2,1)S(1)} collective-permute-done((bf16[472,128]{1,0:T(8,128)(2,1)S(1)}, bf16[472,128]{1,0:T(8,128)(2,1)S(1)}, u32[]{:S(2)}, u32[]{:S(2)}) %collective-permute-start.9) | collective-permute-done | bytes 120864 | tf_op jit(solution)/shard_map/ppermute | solution.py:252
  33.8 1.4 %collective-permute-start.12 = (bf16[472,128]{1,0:T(8,128)(2,1)S(1)}, bf16[472,128]{1,0:T(8,128)(2,1)S(1)}, u32[]{:S(2)}, u32[]{:S(2)}) collective-permute-start(bf16[472,128]{1,0:T(8,128)(2,1)S(1)} %add_convert_fusion.refs_0_), channel_id=1, source_target_pairs={{0,17},{1,16},{2,19},{3,18},{4,21},{5,20},{6,23},{7,22},{8,25},{9,... | collective-permute-start | bytes 362504 | tf_op jit(solution)/shard_map/ppermute | solution.py:252
  35.2 0.7 %collective-permute-start.11 = (bf16[472,128]{1,0:T(8,128)(2,1)S(1)}, bf16[472,128]{1,0:T(8,128)(2,1)S(1)}, u32[]{:S(2)}, u32[]{:S(2)}) collective-permute-start(bf16[472,128]{1,0:T(8,128)(2,1)S(1)} %add_convert_fusion.refs_0_), channel_id=1, source_target_pairs={{0,16},{1,17},{2,18},{3,19},{4,20},{5,21},{6,22},{7,23},{8,9},{9,8... | collective-permute-start | bytes 362504 | tf_op jit(solution)/shard_map/ppermute | solution.py:252
  36.0 1.4 %collective-permute-start.10 = (bf16[472,128]{1,0:T(8,128)(2,1)S(1)}, bf16[472,128]{1,0:T(8,128)(2,1)S(1)}, u32[]{:S(2)}, u32[]{:S(2)}) collective-permute-start(bf16[472,128]{1,0:T(8,128)(2,1)S(1)} %add_convert_fusion.refs_0_), channel_id=1, source_target_pairs={{0,1},{1,0},{2,3},{3,2},{4,5},{5,4},{6,7},{7,6},{8,24},{9,25},{10,... | collective-permute-start | bytes 362504 | tf_op jit(solution)/shard_map/ppermute | solution.py:252
  37.4 2.3 %collective-permute-done.12.refs_3_ = bf16[472,128]{1,0:T(8,128)(2,1)S(1)} collective-permute-done((bf16[472,128]{1,0:T(8,128)(2,1)S(1)}, bf16[472,128]{1,0:T(8,128)(2,1)S(1)}, u32[]{:S(2)}, u32[]{:S(2)}) %collective-permute-start.12) | collective-permute-done | bytes 120864 | tf_op jit(solution)/shard_map/ppermute | solution.py:252
  39.7 0.5 %collective-permute-done.11.refs_2_ = bf16[472,128]{1,0:T(8,128)(2,1)S(1)} collective-permute-done((bf16[472,128]{1,0:T(8,128)(2,1)S(1)}, bf16[472,128]{1,0:T(8,128)(2,1)S(1)}, u32[]{:S(2)}, u32[]{:S(2)}) %collective-permute-start.11) | collective-permute-done | bytes 120864 | tf_op jit(solution)/shard_map/ppermute | solution.py:252
  40.2 0.8 %collective-permute-done.10.refs_1_ = bf16[472,128]{1,0:T(8,128)(2,1)S(1)} collective-permute-done((bf16[472,128]{1,0:T(8,128)(2,1)S(1)}, bf16[472,128]{1,0:T(8,128)(2,1)S(1)}, u32[]{:S(2)}, u32[]{:S(2)}) %collective-permute-start.10) | collective-permute-done | bytes 120864 | tf_op jit(solution)/shard_map/ppermute | solution.py:252
  41.0 0.5 %collective-permute-done.15.refs_6_ = bf16[472,128]{1,0:T(8,128)(2,1)S(1)} collective-permute-done((bf16[472,128]{1,0:T(8,128)(2,1)S(1)}, bf16[472,128]{1,0:T(8,128)(2,1)S(1)}, u32[]{:S(2)}, u32[]{:S(2)}) %collective-permute-start.15) | collective-permute-done | bytes 120864 | tf_op jit(solution)/shard_map/ppermute | solution.py:252
  41.5 0.8 %collective-permute-done.14.refs_5_ = bf16[472,128]{1,0:T(8,128)(2,1)S(1)} collective-permute-done((bf16[472,128]{1,0:T(8,128)(2,1)S(1)}, bf16[472,128]{1,0:T(8,128)(2,1)S(1)}, u32[]{:S(2)}, u32[]{:S(2)}) %collective-permute-start.14) | collective-permute-done | bytes 120864 | tf_op jit(solution)/shard_map/ppermute | solution.py:252
  42.3 1.4 %spread_sums.1 = (f32[8,128,256]{2,1,0:T(8,128)}, f32[1728,128]{1,0:T(8,128)}) custom-call(bf16[472,128]{1,0:T(8,128)(2,1)S(1)} %add_convert_fusion.refs_0_, bf16[472,128]{1,0:T(8,128)(2,1)S(1)} %collective-permute-done.10.refs_1_, bf16[472,128]{1,0:T(8,128)(2,1)S(1)} %collective-permute-done.11.refs_2_, ...), custom_call_target="tpu_custom_call" | custom-call | tf_op jit(solution)/shard_map/spread_sums/pallas_call | solution.py:227
  (26 shorter events, 0.9 us)
Async XLA Ops:
  0.6 6.9 %copy-start = (bf16[1,8,32,1024]{3,2,1,0:T(8,128)(2,1)S(1)}, bf16[1,8,32,1024]{3,2,1,0:T(8,128)(2,1)}, u32[]{:S(2)}) copy-start(bf16[1,8,32,1024]{3,2,1,0:T(8,128)(2,1)} %param.7) | copy-start | bytes 1572868
  1.9 7.1 %collective-permute-start = (bf16[32,1024]{1,0:T(8,128)(2,1)S(1)}, bf16[32,1024]{1,0:T(8,128)(2,1)S(1)}, u32[]{:S(2)}, u32[]{:S(2)}) collective-permute-start(bf16[32,1024]{1,0:T(8,128)(2,1)S(1)} %get-tuple-element.22), channel_id=1, source_target_pairs={{0,1},{1,2},{2,3},{3,4},{4,5},{5,6},{6,7},{8,9},{9,10},{10,11},{11... | collective-permute-start | bytes 196616 | tf_op jit(solution)/shard_map/ppermute | solution.py:307
  7.5 1.4 %copy-start.1 = (bf16[1,2,8,1024]{3,2,1,0:T(8,128)(2,1)S(1)}, bf16[1,2,8,1024]{3,2,1,0:T(8,128)(2,1)}, u32[]{:S(2)}) copy-start(bf16[1,2,8,1024]{3,2,1,0:T(8,128)(2,1)} %param.13) | copy-start | bytes 98308
  10.5 1.4 %collective-permute-start.2 = (bf16[472,128]{1,0:T(8,128)(2,1)S(1)}, bf16[472,128]{1,0:T(8,128)(2,1)S(1)}, u32[]{:S(2)}, u32[]{:S(2)}) collective-permute-start(bf16[472,128]{1,0:T(8,128)(2,1)S(1)} %get-tuple-element.34), channel_id=1, source_target_pairs={{0,8},{1,9},{2,10},{3,11},{4,12},{5,13},{6,14},{7,15},{8,0},{9,1},... | collective-permute-start | bytes 362504 | tf_op jit(solution)/shard_map/ppermute | solution.py:252
  10.6 5.6 %collective-permute-start.1 = (bf16[472,128]{1,0:T(8,128)(2,1)S(1)}, bf16[472,128]{1,0:T(8,128)(2,1)S(1)}, u32[]{:S(2)}, u32[]{:S(2)}) collective-permute-start(bf16[472,128]{1,0:T(8,128)(2,1)S(1)} %get-tuple-element.32), channel_id=1, source_target_pairs={{0,8},{1,9},{2,10},{3,11},{4,12},{5,13},{6,14},{7,15},{8,0},{9,1},... | collective-permute-start | bytes 362504 | tf_op jit(solution)/shard_map/ppermute | solution.py:252
  11.1 3.9 %collective-permute-start.4 = (bf16[472,128]{1,0:T(8,128)(2,1)S(1)}, bf16[472,128]{1,0:T(8,128)(2,1)S(1)}, u32[]{:S(2)}, u32[]{:S(2)}) collective-permute-start(bf16[472,128]{1,0:T(8,128)(2,1)S(1)} %get-tuple-element.36), channel_id=1, source_target_pairs={{0,8},{1,9},{2,10},{3,11},{4,12},{5,13},{6,14},{7,15},{8,0},{9,1},... | collective-permute-start | bytes 362504 | tf_op jit(solution)/shard_map/ppermute | solution.py:252
  11.1 4.5 %collective-permute-start.6 = (bf16[472,128]{1,0:T(8,128)(2,1)S(1)}, bf16[472,128]{1,0:T(8,128)(2,1)S(1)}, u32[]{:S(2)}, u32[]{:S(2)}) collective-permute-start(bf16[472,128]{1,0:T(8,128)(2,1)S(1)} %get-tuple-element.38), channel_id=1, source_target_pairs={{0,8},{1,9},{2,10},{3,11},{4,12},{5,13},{6,14},{7,15},{8,0},{9,1},... | collective-permute-start | bytes 362504 | tf_op jit(solution)/shard_map/ppermute | solution.py:252
  11.9 6.7 %collective-permute-start.3 = (bf16[472,128]{1,0:T(8,128)(2,1)S(1)}, bf16[472,128]{1,0:T(8,128)(2,1)S(1)}, u32[]{:S(2)}, u32[]{:S(2)}) collective-permute-start(bf16[472,128]{1,0:T(8,128)(2,1)S(1)} %add_convert_fusion.5), channel_id=1, source_target_pairs={{0,17},{1,16},{2,19},{3,18},{4,21},{5,20},{6,23},{7,22},{8,25},{9,... | collective-permute-start | bytes 362504 | tf_op jit(solution)/shard_map/ppermute | solution.py:252
  15.0 6.4 %collective-permute-start.5 = (bf16[472,128]{1,0:T(8,128)(2,1)S(1)}, bf16[472,128]{1,0:T(8,128)(2,1)S(1)}, u32[]{:S(2)}, u32[]{:S(2)}) collective-permute-start(bf16[472,128]{1,0:T(8,128)(2,1)S(1)} %add_convert_fusion.4), channel_id=1, source_target_pairs={{0,16},{1,17},{2,18},{3,19},{4,20},{5,21},{6,22},{7,23},{8,9},{9,8... | collective-permute-start | bytes 362504 | tf_op jit(solution)/shard_map/ppermute | solution.py:252
  15.6 5.8 %collective-permute-start.7 = (bf16[472,128]{1,0:T(8,128)(2,1)S(1)}, bf16[472,128]{1,0:T(8,128)(2,1)S(1)}, u32[]{:S(2)}, u32[]{:S(2)}) collective-permute-start(bf16[472,128]{1,0:T(8,128)(2,1)S(1)} %add_convert_fusion.3), channel_id=1, source_target_pairs={{0,1},{1,0},{2,3},{3,2},{4,5},{5,4},{6,7},{7,6},{8,24},{9,25},{10,... | collective-permute-start | bytes 362504 | tf_op jit(solution)/shard_map/ppermute | solution.py:252
  21.5 6.4 %collective-permute-start.8 = (bf16[472,128]{1,0:T(8,128)(2,1)S(1)}, bf16[472,128]{1,0:T(8,128)(2,1)S(1)}, u32[]{:S(2)}, u32[]{:S(2)}) collective-permute-start(bf16[472,128]{1,0:T(8,128)(2,1)S(1)} %add_convert_fusion.2), channel_id=1, source_target_pairs={{0,2},{1,3},{2,0},{3,1},{4,6},{5,7},{6,4},{7,5},{8,12},{9,13},{10,... | collective-permute-start | bytes 362504 | tf_op jit(solution)/shard_map/ppermute | solution.py:252
  28.0 5.8 %collective-permute-start.9 = (bf16[472,128]{1,0:T(8,128)(2,1)S(1)}, bf16[472,128]{1,0:T(8,128)(2,1)S(1)}, u32[]{:S(2)}, u32[]{:S(2)}) collective-permute-start(bf16[472,128]{1,0:T(8,128)(2,1)S(1)} %add_convert_fusion.1), channel_id=1, source_target_pairs={{0,4},{1,5},{2,6},{3,7},{4,0},{5,1},{6,2},{7,3},{8,10},{9,11},{10,... | collective-permute-start | bytes 362504 | tf_op jit(solution)/shard_map/ppermute | solution.py:252
  33.8 5.8 %collective-permute-start.12 = (bf16[472,128]{1,0:T(8,128)(2,1)S(1)}, bf16[472,128]{1,0:T(8,128)(2,1)S(1)}, u32[]{:S(2)}, u32[]{:S(2)}) collective-permute-start(bf16[472,128]{1,0:T(8,128)(2,1)S(1)} %add_convert_fusion.refs_0_), channel_id=1, source_target_pairs={{0,17},{1,16},{2,19},{3,18},{4,21},{5,20},{6,23},{7,22},{8,25},{9,... | collective-permute-start | bytes 362504 | tf_op jit(solution)/shard_map/ppermute | solution.py:252
  35.2 4.9 %collective-permute-start.11 = (bf16[472,128]{1,0:T(8,128)(2,1)S(1)}, bf16[472,128]{1,0:T(8,128)(2,1)S(1)}, u32[]{:S(2)}, u32[]{:S(2)}) collective-permute-start(bf16[472,128]{1,0:T(8,128)(2,1)S(1)} %add_convert_fusion.refs_0_), channel_id=1, source_target_pairs={{0,16},{1,17},{2,18},{3,19},{4,20},{5,21},{6,22},{7,23},{8,9},{9,8... | collective-permute-start | bytes 362504 | tf_op jit(solution)/shard_map/ppermute | solution.py:252
  36.0 5.0 %collective-permute-start.10 = (bf16[472,128]{1,0:T(8,128)(2,1)S(1)}, bf16[472,128]{1,0:T(8,128)(2,1)S(1)}, u32[]{:S(2)}, u32[]{:S(2)}) collective-permute-start(bf16[472,128]{1,0:T(8,128)(2,1)S(1)} %add_convert_fusion.refs_0_), channel_id=1, source_target_pairs={{0,1},{1,0},{2,3},{3,2},{4,5},{5,4},{6,7},{7,6},{8,24},{9,25},{10,... | collective-permute-start | bytes 362504 | tf_op jit(solution)/shard_map/ppermute | solution.py:252
  37.4 3.6 %collective-permute-start.13 = (bf16[472,128]{1,0:T(8,128)(2,1)S(1)}, bf16[472,128]{1,0:T(8,128)(2,1)S(1)}, u32[]{:S(2)}, u32[]{:S(2)}) collective-permute-start(bf16[472,128]{1,0:T(8,128)(2,1)S(1)} %add_convert_fusion.refs_0_), channel_id=1, source_target_pairs={{0,8},{1,9},{2,10},{3,11},{4,12},{5,13},{6,14},{7,15},{8,0},{9,1},... | collective-permute-start | bytes 362504 | tf_op jit(solution)/shard_map/ppermute | solution.py:252
  39.6 1.3 %collective-permute-start.16 = (bf16[472,128]{1,0:T(8,128)(2,1)S(1)}, bf16[472,128]{1,0:T(8,128)(2,1)S(1)}, u32[]{:S(2)}, u32[]{:S(2)}) collective-permute-start(bf16[472,128]{1,0:T(8,128)(2,1)S(1)} %collective-permute-done.12.refs_3_), channel_id=1, source_target_pairs={{0,8},{1,9},{2,10},{3,11},{4,12},{5,13},{6,14},{7,15},{8,0},{9,1},... | collective-permute-start | bytes 362504 | tf_op jit(solution)/shard_map/ppermute | solution.py:252
  40.1 1.3 %collective-permute-start.15 = (bf16[472,128]{1,0:T(8,128)(2,1)S(1)}, bf16[472,128]{1,0:T(8,128)(2,1)S(1)}, u32[]{:S(2)}, u32[]{:S(2)}) collective-permute-start(bf16[472,128]{1,0:T(8,128)(2,1)S(1)} %collective-permute-done.11.refs_2_), channel_id=1, source_target_pairs={{0,8},{1,9},{2,10},{3,11},{4,12},{5,13},{6,14},{7,15},{8,0},{9,1},... | collective-permute-start | bytes 362504 | tf_op jit(solution)/shard_map/ppermute | solution.py:252
  40.9 1.3 %collective-permute-start.14 = (bf16[472,128]{1,0:T(8,128)(2,1)S(1)}, bf16[472,128]{1,0:T(8,128)(2,1)S(1)}, u32[]{:S(2)}, u32[]{:S(2)}) collective-permute-start(bf16[472,128]{1,0:T(8,128)(2,1)S(1)} %collective-permute-done.10.refs_1_), channel_id=1, source_target_pairs={{0,8},{1,9},{2,10},{3,11},{4,12},{5,13},{6,14},{7,15},{8,0},{9,1},... | collective-permute-start | bytes 362504 | tf_op jit(solution)/shard_map/ppermute | solution.py:252

commit v3 on v2

--- a/solution.py
+++ b/solution.py
@@ -23,7 +23,7 @@
     return lax.broadcasted_iota(jnp.int32, shape, dim)
 
 
-def masked_rows(acts, opens):
+def open_rows(opens):
     planes = opens.shape[0]
     cells = ROWS * CELLS
     own = (iota((ROWS, cells), 1) // CELLS) == iota((ROWS, cells), 0)
@@ -33,8 +33,7 @@
     pick = ((iota((cells, 128), 0) % CELLS) == iota((cells, 128), 1)).astype(F32).astype(BF16)
     by_cell = jnp.dot(spread, pick, preferred_element_type=F32).astype(BF16)
     widen = (iota((128, WIDE), 0) == (iota((128, WIDE), 1) // C0)).astype(F32).astype(BF16)
-    mask = jnp.dot(by_cell, widen, preferred_element_type=F32).astype(BF16)
-    return acts * mask
+    return jnp.dot(by_cell, widen, preferred_element_type=F32).astype(BF16)
 
 
 def edge_kernel(
@@ -43,15 +42,16 @@
     plane = pltpu.make_async_copy(acts_ref.at[DEPTH - 1], plane_ref, sems.at[0])
     cells = pltpu.make_async_copy(opens_ref, cells_ref, sems.at[1])
     table = pltpu.make_async_copy(table_ref, bias_ref, sems.at[2])
+    cells.start()
     plane.start()
-    cells.start()
     table.start()
     early = pltpu.make_async_copy(w1_hbm, w1_ref, sems.at[3])
     early.start()
     cells.wait()
+    mask = open_rows(cells_ref[DEPTH - 1 :])
+    plane.wait()
+    edge_ref[...] = plane_ref[...] * mask
     table.wait()
-    plane.wait()
-    edge_ref[...] = masked_rows(plane_ref[...], cells_ref[DEPTH - 1 :])
     early.wait()
 
 
@@ -91,7 +91,7 @@
 ):
     fetch = pltpu.make_async_copy(w2_hbm, w2_ref, sem)
     fetch.start()
-    field = masked_rows(acts_ref[...].reshape(DEPTH * ROWS, WIDE), opens_ref[...])
+    field = acts_ref[...].reshape(DEPTH * ROWS, WIDE) * open_rows(opens_ref[...])
     half = 3 * 64
     r = iota((2 * half, DEPTH * ROWS), 0)
     par = (r >= half).astype(jnp.int32)
@@ -182,8 +182,8 @@
     for a in range(3):
         for b in range(3):
             grad = lax.dot_general(
-                rows_of(a, b), delta, (((0,), (0,)), ((), ())), preferred_element_type=F32
-            )
+                delta, rows_of(a, b), (((0,), (0,)), ((), ())), preferred_element_type=F32
+            ).T
             at = (a * 3 + b) * 3 * C0
             early_ref[at : at + 3 * C0] = grad[C0:]
 
@@ -203,43 +203,44 @@
 
 
 def spread_kernel(*refs):
-    deep_ref, early_ref, wide_ref, low_ref, sems = refs[8:]
+    deep_in, deep_out, wide_out, low_out, wide_ref, low_ref, sems = refs[8:]
     copies = []
+
+    def send(source, target):
+        copies.append(pltpu.make_async_copy(source, target, sems.at[len(copies)]))
+        copies[-1].start()
+
     for k in range(8):
         chunk = chunk_of(k % 4, k // 4)
         wide_ref[k, :, :128] = refs[k][:C1].astype(F32)
         wide_ref[k, :, 128:] = refs[k][C1 : 2 * C1].astype(F32)
-        copies.append(pltpu.make_async_copy(wide_ref.at[k], deep_ref.at[chunk], sems.at[2 * k]))
-        copies[-1].start()
+        send(wide_ref.at[k], wide_out.at[chunk])
         low_ref[k] = refs[k][2 * C1 :].astype(F32)
         at = pl.multiple_of(chunk * EARLY_ROWS, 8)
-        copies.append(
-            pltpu.make_async_copy(
-                low_ref.at[k], early_ref.at[pl.ds(at, EARLY_ROWS), :], sems.at[2 * k + 1]
-            )
-        )
-        copies[-1].start()
+        send(low_ref.at[k], low_out.at[pl.ds(at, EARLY_ROWS), :])
+    send(deep_in, deep_out)
     for copy in copies:
         copy.wait()
 
 
-def spread(chunks):
+def spread(chunks, deep):
     return pl.pallas_call(
         spread_kernel,
-        in_specs=[pl.BlockSpec(memory_space=pltpu.VMEM)] * 8,
-        out_specs=[pl.BlockSpec(memory_space=pltpu.HBM)] * 2,
+        in_specs=[pl.BlockSpec(memory_space=pltpu.VMEM)] * 9,
+        out_specs=[pl.BlockSpec(memory_space=pltpu.HBM)] * 3,
         out_shape=[
+            jax.ShapeDtypeStruct(deep.shape, BF16),
             jax.ShapeDtypeStruct((8, C1, C2), F32),
             jax.ShapeDtypeStruct((27 * C0, C1), F32),
         ],
         scratch_shapes=[
             pltpu.VMEM((8, C1, C2), F32),
             pltpu.VMEM((8, EARLY_ROWS, 128), F32),
-            pltpu.SemaphoreType.DMA((16,)),
+            pltpu.SemaphoreType.DMA((17,)),
         ],
         compiler_params=pltpu.CompilerParams(vmem_limit_bytes=VMEM_BYTES),
         name="spread_sums",
-    )(*chunks)
+    )(*chunks, deep)
 
 
 def swapped(value, flips):
@@ -345,7 +346,7 @@
         compiler_params=params,
         name="local_terms",
     )(below, early, *inner, cotangent.reshape(DEPTH // 4 * ROWS // 4, CELLS // 4 * C2))
-    grad_deep, grad_early = spread(total(chunks[:4], chunks[4:]))
+    deep, grad_deep, grad_early = spread(total(chunks[:4], chunks[4:]), deep)
     return (
         deep.reshape(1, DEPTH // 4, ROWS // 4, CELLS // 4 * C2),
         grad_deep.reshape(w_deep.shape),

time: 43.8 us -> 43.6 us (level)
  no operation moved by 1% of the time
where the time goes in v3:
time: 43.6 us; the launch traced here: 43.4 us
  starting transfers between devices  18.4 us (42%)
  waiting for transfers between devices  18 us (41%)
  Pallas kernels  5.3 us (12%)
  between operations  1.39 us (3%)
    ppermute x16, waiting for transfers between devices, swapped(): return lax.ppermute(value, ('sample', 'space'), pairs)  18 us
    ppermute x16, starting transfers between devices, swapped(): return lax.ppermute(value, ('sample', 'space'), pairs)  13.5 us
    ppermute x1, starting transfers between devices, body(): below = lax.ppermute(edge, 'space', [(i, i + 1) for i in range(spaces - 1)])  4.87 us
    pallas_call x1, Pallas kernels, spread(): pl.pallas_call(spread_kernel, in_specs=[pl.BlockSpec(memory_space=pltpu.V...  1.42 us
    pallas_call x1, Pallas kernels, body(): pl.pallas_call(inner_kernel, in_specs=[vmem] * 4 + [hbm], out_specs=[vmem...  1.41 us
    pallas_call x1, Pallas kernels, body(): pl.pallas_call(local_kernel, in_specs=[vmem] * 7, out_specs=[vmem] * 9, o...  1.3 us
    pallas_call x1, Pallas kernels, body(): pl.pallas_call(edge_kernel, in_specs=[hbm] * 4, out_specs=[vmem] * 4, out...  1.17 us
  transfers between devices with their start and end apart: 17, of which 10 were waited for; matrix products, arithmetic and copies ran while one was open for 0% of the time, Pallas kernels for 3%

profile of v3, /device:TPU:0, one launch (start us, length us, event | category | flops | bytes accessed | tf_op | source)
XLA Modules:
  0.0 43.4 jit_solution(17576310169737608762)
XLA Ops:
  0.6 1.2 %edge_plane.1 = (bf16[32,1024]{1,0:T(8,128)(2,1)S(1)}, s32[8,512]{1,0:T(8,128)S(1)}, f32[8,128]{1,0:T(8,128)S(1)}, bf16[9,192,128]{2,1,0:T(8,128)(2,1)S(1)}) custom-call(bf16[8,32,1024]{2,1,0:T(8,128)(2,1)} %bitcast.11, s32[8,512]{1,0:T(8,128)} %bitcast.17, f32[8,128]{1,0:T(8,128)} %table_ref.1, bf16[9,192,128]{2,1,0:T(8,128)(2,1)} %bitcast.16), custom_call_target="tpu_custom_call" | custom-call | tf_op jit(solution)/shard_map/edge_plane/pallas_call | solution.py:293
  1.8 4.9 %collective-permute-start = (bf16[32,1024]{1,0:T(8,128)(2,1)S(1)}, bf16[32,1024]{1,0:T(8,128)(2,1)S(1)}, u32[]{:S(2)}, u32[]{:S(2)}) collective-permute-start(bf16[32,1024]{1,0:T(8,128)(2,1)S(1)} %get-tuple-element.23), channel_id=1, source_target_pairs={{0,1},{1,2},{2,3},{3,4},{4,5},{5,6},{6,7},{8,9},{9,10},{10,11},{11... | collective-permute-start | bytes 196616 | tf_op jit(solution)/shard_map/ppermute | solution.py:308
  7.5 1.4 %inner_terms.1 = (bf16[3,64,1152]{2,1,0:T(8,128)(2,1)S(1)}, bf16[3,64,1152]{2,1,0:T(8,128)(2,1)S(1)}, f32[512,128]{1,0:T(8,128)S(1)}, bf16[8,128,256]{2,1,0:T(8,128)(2,1)S(1)}) custom-call(bf16[8,32,1024]{2,1,0:T(8,128)(2,1)S(1)} %bitcast.12, s32[8,512]{1,0:T(8,128)S(1)} %get-tuple-element.25.opens_ref, f32[1,128]{1,0:T(1,128)S(1)} %bitcast.14, ...), custom_call_target="tpu_custom_call" | custom-call | tf_op jit(solution)/shard_map/inner_terms/pallas_call | solution.py:312
  8.9 1.3 %local_terms.1 = (bf16[16,1024]{1,0:T(8,128)(2,1)S(1)}, f32[472,128]{1,0:T(8,128)S(1)}, f32[472,128]{1,0:T(8,128)S(1)}, f32[472,128]{1,0:T(8,128)S(1)}, f32[472,...) custom-call(bf16[32,1024]{1,0:T(8,128)(2,1)S(1)} %collective-permute, ...), custom_call_target="tpu_custom_call" | custom-call | tf_op jit(solution)/shard_map/local_terms/pallas_call | solution.py:332
  10.3 0.5 %collective-permute-start.1 = (bf16[472,128]{1,0:T(8,128)(2,1)S(1)}, bf16[472,128]{1,0:T(8,128)(2,1)S(1)}, u32[]{:S(2)}, u32[]{:S(2)}) collective-permute-start(bf16[472,128]{1,0:T(8,128)(2,1)S(1)} %get-tuple-element.32), channel_id=1, source_target_pairs={{0,8},{1,9},{2,10},{3,11},{4,12},{5,13},{6,14},{7,15},{8,0},{9,1},... | collective-permute-start | bytes 362504 | tf_op jit(solution)/shard_map/ppermute | solution.py:253
  10.9 0.4 collective-permute-start.6
  11.6 3.0 %collective-permute-start.3 = (bf16[472,128]{1,0:T(8,128)(2,1)S(1)}, bf16[472,128]{1,0:T(8,128)(2,1)S(1)}, u32[]{:S(2)}, u32[]{:S(2)}) collective-permute-start(bf16[472,128]{1,0:T(8,128)(2,1)S(1)} %add_convert_fusion.5), channel_id=1, source_target_pairs={{0,17},{1,16},{2,19},{3,18},{4,21},{5,20},{6,23},{7,22},{8,25},{9,... | collective-permute-start | bytes 362504 | tf_op jit(solution)/shard_map/ppermute | solution.py:253
  14.7 0.6 %collective-permute-start.5 = (bf16[472,128]{1,0:T(8,128)(2,1)S(1)}, bf16[472,128]{1,0:T(8,128)(2,1)S(1)}, u32[]{:S(2)}, u32[]{:S(2)}) collective-permute-start(bf16[472,128]{1,0:T(8,128)(2,1)S(1)} %add_convert_fusion.4), channel_id=1, source_target_pairs={{0,16},{1,17},{2,18},{3,19},{4,20},{5,21},{6,22},{7,23},{8,9},{9,8... | collective-permute-start | bytes 362504 | tf_op jit(solution)/shard_map/ppermute | solution.py:253
  15.4 0.5 %collective-permute-start.7 = (bf16[472,128]{1,0:T(8,128)(2,1)S(1)}, bf16[472,128]{1,0:T(8,128)(2,1)S(1)}, u32[]{:S(2)}, u32[]{:S(2)}) collective-permute-start(bf16[472,128]{1,0:T(8,128)(2,1)S(1)} %add_convert_fusion.3), channel_id=1, source_target_pairs={{0,1},{1,0},{2,3},{3,2},{4,5},{5,4},{6,7},{7,6},{8,24},{9,25},{10,... | collective-permute-start | bytes 362504 | tf_op jit(solution)/shard_map/ppermute | solution.py:253
  15.9 2.5 %collective-permute-done.3 = bf16[472,128]{1,0:T(8,128)(2,1)S(1)} collective-permute-done((bf16[472,128]{1,0:T(8,128)(2,1)S(1)}, bf16[472,128]{1,0:T(8,128)(2,1)S(1)}, u32[]{:S(2)}, u32[]{:S(2)}) %collective-permute-start.3) | collective-permute-done | bytes 120864 | tf_op jit(solution)/shard_map/ppermute | solution.py:253
  18.4 2.8 %collective-permute-done.5 = bf16[472,128]{1,0:T(8,128)(2,1)S(1)} collective-permute-done((bf16[472,128]{1,0:T(8,128)(2,1)S(1)}, bf16[472,128]{1,0:T(8,128)(2,1)S(1)}, u32[]{:S(2)}, u32[]{:S(2)}) %collective-permute-start.5) | collective-permute-done | bytes 120864 | tf_op jit(solution)/shard_map/ppermute | solution.py:253
  21.2 2.5 %collective-permute-start.8 = (bf16[472,128]{1,0:T(8,128)(2,1)S(1)}, bf16[472,128]{1,0:T(8,128)(2,1)S(1)}, u32[]{:S(2)}, u32[]{:S(2)}) collective-permute-start(bf16[472,128]{1,0:T(8,128)(2,1)S(1)} %add_convert_fusion.2), channel_id=1, source_target_pairs={{0,2},{1,3},{2,0},{3,1},{4,6},{5,7},{6,4},{7,5},{8,12},{9,13},{10,... | collective-permute-start | bytes 362504 | tf_op jit(solution)/shard_map/ppermute | solution.py:253
  23.7 4.0 %collective-permute-done.8 = bf16[472,128]{1,0:T(8,128)(2,1)S(1)} collective-permute-done((bf16[472,128]{1,0:T(8,128)(2,1)S(1)}, bf16[472,128]{1,0:T(8,128)(2,1)S(1)}, u32[]{:S(2)}, u32[]{:S(2)}) %collective-permute-start.8) | collective-permute-done | bytes 120864 | tf_op jit(solution)/shard_map/ppermute | solution.py:253
  27.7 2.2 %collective-permute-start.9 = (bf16[472,128]{1,0:T(8,128)(2,1)S(1)}, bf16[472,128]{1,0:T(8,128)(2,1)S(1)}, u32[]{:S(2)}, u32[]{:S(2)}) collective-permute-start(bf16[472,128]{1,0:T(8,128)(2,1)S(1)} %add_convert_fusion.1), channel_id=1, source_target_pairs={{0,4},{1,5},{2,6},{3,7},{4,0},{5,1},{6,2},{7,3},{8,10},{9,11},{10,... | collective-permute-start | bytes 362504 | tf_op jit(solution)/shard_map/ppermute | solution.py:253
  29.9 3.6 %collective-permute-done.9 = bf16[472,128]{1,0:T(8,128)(2,1)S(1)} collective-permute-done((bf16[472,128]{1,0:T(8,128)(2,1)S(1)}, bf16[472,128]{1,0:T(8,128)(2,1)S(1)}, u32[]{:S(2)}, u32[]{:S(2)}) %collective-permute-start.9) | collective-permute-done | bytes 120864 | tf_op jit(solution)/shard_map/ppermute | solution.py:253
  33.5 1.4 %collective-permute-start.12 = (bf16[472,128]{1,0:T(8,128)(2,1)S(1)}, bf16[472,128]{1,0:T(8,128)(2,1)S(1)}, u32[]{:S(2)}, u32[]{:S(2)}) collective-permute-start(bf16[472,128]{1,0:T(8,128)(2,1)S(1)} %add_convert_fusion.refs_0_), channel_id=1, source_target_pairs={{0,17},{1,16},{2,19},{3,18},{4,21},{5,20},{6,23},{7,22},{8,25},{9,... | collective-permute-start | bytes 362504 | tf_op jit(solution)/shard_map/ppermute | solution.py:253
  35.0 0.7 %collective-permute-start.11 = (bf16[472,128]{1,0:T(8,128)(2,1)S(1)}, bf16[472,128]{1,0:T(8,128)(2,1)S(1)}, u32[]{:S(2)}, u32[]{:S(2)}) collective-permute-start(bf16[472,128]{1,0:T(8,128)(2,1)S(1)} %add_convert_fusion.refs_0_), channel_id=1, source_target_pairs={{0,16},{1,17},{2,18},{3,19},{4,20},{5,21},{6,22},{7,23},{8,9},{9,8... | collective-permute-start | bytes 362504 | tf_op jit(solution)/shard_map/ppermute | solution.py:253
  35.7 1.4 %collective-permute-start.10 = (bf16[472,128]{1,0:T(8,128)(2,1)S(1)}, bf16[472,128]{1,0:T(8,128)(2,1)S(1)}, u32[]{:S(2)}, u32[]{:S(2)}) collective-permute-start(bf16[472,128]{1,0:T(8,128)(2,1)S(1)} %add_convert_fusion.refs_0_), channel_id=1, source_target_pairs={{0,1},{1,0},{2,3},{3,2},{4,5},{5,4},{6,7},{7,6},{8,24},{9,25},{10,... | collective-permute-start | bytes 362504 | tf_op jit(solution)/shard_map/ppermute | solution.py:253
  37.1 2.3 %collective-permute-done.12.refs_3_ = bf16[472,128]{1,0:T(8,128)(2,1)S(1)} collective-permute-done((bf16[472,128]{1,0:T(8,128)(2,1)S(1)}, bf16[472,128]{1,0:T(8,128)(2,1)S(1)}, u32[]{:S(2)}, u32[]{:S(2)}) %collective-permute-start.12) | collective-permute-done | bytes 120864 | tf_op jit(solution)/shard_map/ppermute | solution.py:253
  39.4 0.5 %collective-permute-done.11.refs_2_ = bf16[472,128]{1,0:T(8,128)(2,1)S(1)} collective-permute-done((bf16[472,128]{1,0:T(8,128)(2,1)S(1)}, bf16[472,128]{1,0:T(8,128)(2,1)S(1)}, u32[]{:S(2)}, u32[]{:S(2)}) %collective-permute-start.11) | collective-permute-done | bytes 120864 | tf_op jit(solution)/shard_map/ppermute | solution.py:253
  39.9 0.8 %collective-permute-done.10.refs_1_ = bf16[472,128]{1,0:T(8,128)(2,1)S(1)} collective-permute-done((bf16[472,128]{1,0:T(8,128)(2,1)S(1)}, bf16[472,128]{1,0:T(8,128)(2,1)S(1)}, u32[]{:S(2)}, u32[]{:S(2)}) %collective-permute-start.10) | collective-permute-done | bytes 120864 | tf_op jit(solution)/shard_map/ppermute | solution.py:253
  40.7 0.5 %collective-permute-done.15.refs_6_ = bf16[472,128]{1,0:T(8,128)(2,1)S(1)} collective-permute-done((bf16[472,128]{1,0:T(8,128)(2,1)S(1)}, bf16[472,128]{1,0:T(8,128)(2,1)S(1)}, u32[]{:S(2)}, u32[]{:S(2)}) %collective-permute-start.15) | collective-permute-done | bytes 120864 | tf_op jit(solution)/shard_map/ppermute | solution.py:253
  41.2 0.8 %collective-permute-done.14.refs_5_ = bf16[472,128]{1,0:T(8,128)(2,1)S(1)} collective-permute-done((bf16[472,128]{1,0:T(8,128)(2,1)S(1)}, bf16[472,128]{1,0:T(8,128)(2,1)S(1)}, u32[]{:S(2)}, u32[]{:S(2)}) %collective-permute-start.14) | collective-permute-done | bytes 120864 | tf_op jit(solution)/shard_map/ppermute | solution.py:253
  42.0 1.4 %spread_sums.1 = (bf16[16,1024]{1,0:T(8,128)(2,1)}, f32[8,128,256]{2,1,0:T(8,128)}, f32[1728,128]{1,0:T(8,128)}) custom-call(bf16[472,128]{1,0:T(8,128)(2,1)S(1)} %add_convert_fusion.refs_0_, bf16[472,128]{1,0:T(8,128)(2,1)S(1)} %collective-permute-done.10.refs_1_, bf16[472,128]{1,0:T(8,128)(2,1)S(1)} %collective-permute-done.11.refs_2_, ...), custom_call_target="tpu_custom_call" | custom-call | tf_op jit(solution)/shard_map/spread_sums/pallas_call | solution.py:227
  (26 shorter events, 0.9 us)
Async XLA Ops:
  0.6 6.8 %copy-start = (bf16[1,8,32,1024]{3,2,1,0:T(8,128)(2,1)S(1)}, bf16[1,8,32,1024]{3,2,1,0:T(8,128)(2,1)}, u32[]{:S(2)}) copy-start(bf16[1,8,32,1024]{3,2,1,0:T(8,128)(2,1)} %param.7) | copy-start | bytes 1572868
  1.8 7.1 %collective-permute-start = (bf16[32,1024]{1,0:T(8,128)(2,1)S(1)}, bf16[32,1024]{1,0:T(8,128)(2,1)S(1)}, u32[]{:S(2)}, u32[]{:S(2)}) collective-permute-start(bf16[32,1024]{1,0:T(8,128)(2,1)S(1)} %get-tuple-element.23), channel_id=1, source_target_pairs={{0,1},{1,2},{2,3},{3,4},{4,5},{5,6},{6,7},{8,9},{9,10},{10,11},{11... | collective-permute-start | bytes 196616 | tf_op jit(solution)/shard_map/ppermute | solution.py:308
  7.5 1.4 %copy-start.1 = (bf16[1,2,8,1024]{3,2,1,0:T(8,128)(2,1)S(1)}, bf16[1,2,8,1024]{3,2,1,0:T(8,128)(2,1)}, u32[]{:S(2)}) copy-start(bf16[1,2,8,1024]{3,2,1,0:T(8,128)(2,1)} %param.13) | copy-start | bytes 98308
  10.2 1.4 %collective-permute-start.2 = (bf16[472,128]{1,0:T(8,128)(2,1)S(1)}, bf16[472,128]{1,0:T(8,128)(2,1)S(1)}, u32[]{:S(2)}, u32[]{:S(2)}) collective-permute-start(bf16[472,128]{1,0:T(8,128)(2,1)S(1)} %get-tuple-element.34), channel_id=1, source_target_pairs={{0,8},{1,9},{2,10},{3,11},{4,12},{5,13},{6,14},{7,15},{8,0},{9,1},... | collective-permute-start | bytes 362504 | tf_op jit(solution)/shard_map/ppermute | solution.py:253
  10.3 5.6 %collective-permute-start.1 = (bf16[472,128]{1,0:T(8,128)(2,1)S(1)}, bf16[472,128]{1,0:T(8,128)(2,1)S(1)}, u32[]{:S(2)}, u32[]{:S(2)}) collective-permute-start(bf16[472,128]{1,0:T(8,128)(2,1)S(1)} %get-tuple-element.32), channel_id=1, source_target_pairs={{0,8},{1,9},{2,10},{3,11},{4,12},{5,13},{6,14},{7,15},{8,0},{9,1},... | collective-permute-start | bytes 362504 | tf_op jit(solution)/shard_map/ppermute | solution.py:253
  10.8 3.9 %collective-permute-start.4 = (bf16[472,128]{1,0:T(8,128)(2,1)S(1)}, bf16[472,128]{1,0:T(8,128)(2,1)S(1)}, u32[]{:S(2)}, u32[]{:S(2)}) collective-permute-start(bf16[472,128]{1,0:T(8,128)(2,1)S(1)} %get-tuple-element.36), channel_id=1, source_target_pairs={{0,8},{1,9},{2,10},{3,11},{4,12},{5,13},{6,14},{7,15},{8,0},{9,1},... | collective-permute-start | bytes 362504 | tf_op jit(solution)/shard_map/ppermute | solution.py:253
  10.9 4.5 %collective-permute-start.6 = (bf16[472,128]{1,0:T(8,128)(2,1)S(1)}, bf16[472,128]{1,0:T(8,128)(2,1)S(1)}, u32[]{:S(2)}, u32[]{:S(2)}) collective-permute-start(bf16[472,128]{1,0:T(8,128)(2,1)S(1)} %get-tuple-element.38), channel_id=1, source_target_pairs={{0,8},{1,9},{2,10},{3,11},{4,12},{5,13},{6,14},{7,15},{8,0},{9,1},... | collective-permute-start | bytes 362504 | tf_op jit(solution)/shard_map/ppermute | solution.py:253
  11.6 6.7 %collective-permute-start.3 = (bf16[472,128]{1,0:T(8,128)(2,1)S(1)}, bf16[472,128]{1,0:T(8,128)(2,1)S(1)}, u32[]{:S(2)}, u32[]{:S(2)}) collective-permute-start(bf16[472,128]{1,0:T(8,128)(2,1)S(1)} %add_convert_fusion.5), channel_id=1, source_target_pairs={{0,17},{1,16},{2,19},{3,18},{4,21},{5,20},{6,23},{7,22},{8,25},{9,... | collective-permute-start | bytes 362504 | tf_op jit(solution)/shard_map/ppermute | solution.py:253
  14.7 6.4 %collective-permute-start.5 = (bf16[472,128]{1,0:T(8,128)(2,1)S(1)}, bf16[472,128]{1,0:T(8,128)(2,1)S(1)}, u32[]{:S(2)}, u32[]{:S(2)}) collective-permute-start(bf16[472,128]{1,0:T(8,128)(2,1)S(1)} %add_convert_fusion.4), channel_id=1, source_target_pairs={{0,16},{1,17},{2,18},{3,19},{4,20},{5,21},{6,22},{7,23},{8,9},{9,8... | collective-permute-start | bytes 362504 | tf_op jit(solution)/shard_map/ppermute | solution.py:253
  15.4 5.8 %collective-permute-start.7 = (bf16[472,128]{1,0:T(8,128)(2,1)S(1)}, bf16[472,128]{1,0:T(8,128)(2,1)S(1)}, u32[]{:S(2)}, u32[]{:S(2)}) collective-permute-start(bf16[472,128]{1,0:T(8,128)(2,1)S(1)} %add_convert_fusion.3), channel_id=1, source_target_pairs={{0,1},{1,0},{2,3},{3,2},{4,5},{5,4},{6,7},{7,6},{8,24},{9,25},{10,... | collective-permute-start | bytes 362504 | tf_op jit(solution)/shard_map/ppermute | solution.py:253
  21.2 6.4 %collective-permute-start.8 = (bf16[472,128]{1,0:T(8,128)(2,1)S(1)}, bf16[472,128]{1,0:T(8,128)(2,1)S(1)}, u32[]{:S(2)}, u32[]{:S(2)}) collective-permute-start(bf16[472,128]{1,0:T(8,128)(2,1)S(1)} %add_convert_fusion.2), channel_id=1, source_target_pairs={{0,2},{1,3},{2,0},{3,1},{4,6},{5,7},{6,4},{7,5},{8,12},{9,13},{10,... | collective-permute-start | bytes 362504 | tf_op jit(solution)/shard_map/ppermute | solution.py:253
  27.7 5.8 %collective-permute-start.9 = (bf16[472,128]{1,0:T(8,128)(2,1)S(1)}, bf16[472,128]{1,0:T(8,128)(2,1)S(1)}, u32[]{:S(2)}, u32[]{:S(2)}) collective-permute-start(bf16[472,128]{1,0:T(8,128)(2,1)S(1)} %add_convert_fusion.1), channel_id=1, source_target_pairs={{0,4},{1,5},{2,6},{3,7},{4,0},{5,1},{6,2},{7,3},{8,10},{9,11},{10,... | collective-permute-start | bytes 362504 | tf_op jit(solution)/shard_map/ppermute | solution.py:253
  33.5 5.8 %collective-permute-start.12 = (bf16[472,128]{1,0:T(8,128)(2,1)S(1)}, bf16[472,128]{1,0:T(8,128)(2,1)S(1)}, u32[]{:S(2)}, u32[]{:S(2)}) collective-permute-start(bf16[472,128]{1,0:T(8,128)(2,1)S(1)} %add_convert_fusion.refs_0_), channel_id=1, source_target_pairs={{0,17},{1,16},{2,19},{3,18},{4,21},{5,20},{6,23},{7,22},{8,25},{9,... | collective-permute-start | bytes 362504 | tf_op jit(solution)/shard_map/ppermute | solution.py:253
  35.0 4.9 %collective-permute-start.11 = (bf16[472,128]{1,0:T(8,128)(2,1)S(1)}, bf16[472,128]{1,0:T(8,128)(2,1)S(1)}, u32[]{:S(2)}, u32[]{:S(2)}) collective-permute-start(bf16[472,128]{1,0:T(8,128)(2,1)S(1)} %add_convert_fusion.refs_0_), channel_id=1, source_target_pairs={{0,16},{1,17},{2,18},{3,19},{4,20},{5,21},{6,22},{7,23},{8,9},{9,8... | collective-permute-start | bytes 362504 | tf_op jit(solution)/shard_map/ppermute | solution.py:253
  35.7 5.0 %collective-permute-start.10 = (bf16[472,128]{1,0:T(8,128)(2,1)S(1)}, bf16[472,128]{1,0:T(8,128)(2,1)S(1)}, u32[]{:S(2)}, u32[]{:S(2)}) collective-permute-start(bf16[472,128]{1,0:T(8,128)(2,1)S(1)} %add_convert_fusion.refs_0_), channel_id=1, source_target_pairs={{0,1},{1,0},{2,3},{3,2},{4,5},{5,4},{6,7},{7,6},{8,24},{9,25},{10,... | collective-permute-start | bytes 362504 | tf_op jit(solution)/shard_map/ppermute | solution.py:253
  37.1 3.6 %collective-permute-start.13 = (bf16[472,128]{1,0:T(8,128)(2,1)S(1)}, bf16[472,128]{1,0:T(8,128)(2,1)S(1)}, u32[]{:S(2)}, u32[]{:S(2)}) collective-permute-start(bf16[472,128]{1,0:T(8,128)(2,1)S(1)} %add_convert_fusion.refs_0_), channel_id=1, source_target_pairs={{0,8},{1,9},{2,10},{3,11},{4,12},{5,13},{6,14},{7,15},{8,0},{9,1},... | collective-permute-start | bytes 362504 | tf_op jit(solution)/shard_map/ppermute | solution.py:253
  39.4 1.3 %collective-permute-start.16 = (bf16[472,128]{1,0:T(8,128)(2,1)S(1)}, bf16[472,128]{1,0:T(8,128)(2,1)S(1)}, u32[]{:S(2)}, u32[]{:S(2)}) collective-permute-start(bf16[472,128]{1,0:T(8,128)(2,1)S(1)} %collective-permute-done.12.refs_3_), channel_id=1, source_target_pairs={{0,8},{1,9},{2,10},{3,11},{4,12},{5,13},{6,14},{7,15},{8,0},{9,1},... | collective-permute-start | bytes 362504 | tf_op jit(solution)/shard_map/ppermute | solution.py:253
  39.8 1.3 %collective-permute-start.15 = (bf16[472,128]{1,0:T(8,128)(2,1)S(1)}, bf16[472,128]{1,0:T(8,128)(2,1)S(1)}, u32[]{:S(2)}, u32[]{:S(2)}) collective-permute-start(bf16[472,128]{1,0:T(8,128)(2,1)S(1)} %collective-permute-done.11.refs_2_), channel_id=1, source_target_pairs={{0,8},{1,9},{2,10},{3,11},{4,12},{5,13},{6,14},{7,15},{8,0},{9,1},... | collective-permute-start | bytes 362504 | tf_op jit(solution)/shard_map/ppermute | solution.py:253
  40.7 1.3 %collective-permute-start.14 = (bf16[472,128]{1,0:T(8,128)(2,1)S(1)}, bf16[472,128]{1,0:T(8,128)(2,1)S(1)}, u32[]{:S(2)}, u32[]{:S(2)}) collective-permute-start(bf16[472,128]{1,0:T(8,128)(2,1)S(1)} %collective-permute-done.10.refs_1_), channel_id=1, source_target_pairs={{0,8},{1,9},{2,10},{3,11},{4,12},{5,13},{6,14},{7,15},{8,0},{9,1},... | collective-permute-start | bytes 362504 | tf_op jit(solution)/shard_map/ppermute | solution.py:253

commit v4 on v3

--- a/solution.py
+++ b/solution.py
@@ -37,7 +37,9 @@
 
 
 def edge_kernel(
-    acts_ref, opens_ref, table_ref, w1_hbm, edge_ref, cells_ref, bias_ref, w1_ref, plane_ref, sems
+    acts_ref, opens_ref, table_ref, w1_hbm, cot_hbm,
+    edge_ref, cells_ref, bias_ref, w1_ref, cot_ref,
+    plane_ref, sems,
 ):
     plane = pltpu.make_async_copy(acts_ref.at[DEPTH - 1], plane_ref, sems.at[0])
     cells = pltpu.make_async_copy(opens_ref, cells_ref, sems.at[1])
@@ -47,12 +49,15 @@
     table.start()
     early = pltpu.make_async_copy(w1_hbm, w1_ref, sems.at[3])
     early.start()
+    cot = pltpu.make_async_copy(cot_hbm, cot_ref, sems.at[4])
+    cot.start()
     cells.wait()
     mask = open_rows(cells_ref[DEPTH - 1 :])
     plane.wait()
     edge_ref[...] = plane_ref[...] * mask
     table.wait()
     early.wait()
+    cot.wait()
 
 
 def places():
@@ -84,9 +89,51 @@
     return jnp.concatenate([jnp.zeros((C0, C1), BF16), w], axis=0)
 
 
+def blocks(parts):
+    return jnp.concatenate(
+        [ref[b, top : top + n, (x + 1) * PAIR : (x + 2) * PAIR] for x in range(CELLS // 2) for ref, b, top, n in parts],
+        axis=0,
+    )
+
+
+def pair_weight(w):
+    here = jnp.concatenate([w[C0 : 2 * C0], jnp.zeros((C0, C1), BF16)], axis=1)
+    return jnp.concatenate([here, jnp.concatenate([w[2 * C0 :], w[:C0]], axis=1)], axis=0)
+
+
+def by_twos(taps):
+    return [taps[k : k + 2] for k in range(0, len(taps), 2)]
+
+
+def convolved(rows, weights, n):
+    out = jnp.zeros((rows[0].shape[0], 2 * C1), F32)
+    for taps in by_twos(list(zip(rows, weights))):
+        left = jnp.concatenate([r for r, _ in taps], axis=1)
+        right = jnp.concatenate([pair_weight(w) for _, w in taps], axis=0)
+        out = out + jnp.dot(left, right, preferred_element_type=F32)
+    ahead = jnp.concatenate([jnp.zeros((n, C1), F32), out[:-n, C1:]], axis=0)
+    return out[:, :C1] + ahead
+
+
+TAPS = [(a, b, c) for a in range(2) for b in range(2) for c in range(2)]
+
+
+def pieces(tap):
+    a, b, c = tap
+    return [
+        (2 * x + c) * 64 + (2 * z + a) * 16 + b * 8
+        for x in range(CELLS // 4)
+        for z in range(DEPTH // 4)
+    ]
+
+
+def upstream(cot_ref):
+    return jnp.concatenate([cot_ref[:, x * C2 : (x + 1) * C2] for x in range(CELLS // 4)], axis=0)
+
+
 def inner_kernel(
-    acts_ref, opens_ref, bias_ref, w1_ref, w2_hbm,
-    even_ref, odd_ref, pre_ref, w2_ref,
+    acts_ref, opens_ref, bias_ref, w1_ref, cot_ref, w2_hbm,
+    even_ref, odd_ref, pre_ref, w2_ref, back_ref,
     sem,
 ):
     fetch = pltpu.make_async_copy(w2_hbm, w2_ref, sem)
@@ -106,31 +153,39 @@
             ref[b, :, :PAIR] = jnp.zeros((64, PAIR), BF16)
             ref[b, :, PAIR:] = rows[top + b * 64 : top + (b + 1) * 64]
     pre = bias_ref[...]
-    for a, ref in ((1, even_ref), (2, odd_ref)):
-        for b in range(3):
-            w = tap_weight(w1_ref[a * 3 + b])
-            pre = pre + jnp.dot(windows([(ref, b, 0, 64)]), w, preferred_element_type=F32)
-    over = jnp.zeros((8 * 48, C1), F32)
-    for b in range(3):
-        w = tap_weight(w1_ref[b])
-        over = over + jnp.dot(windows([(odd_ref, b, 0, 48)]), w, preferred_element_type=F32)
+    pre = pre + convolved(
+        [blocks([(ref, b, 0, 64)]) for ref in (even_ref, odd_ref) for b in range(3)],
+        [w1_ref[k] for k in range(3, 9)],
+        64,
+    )
+    over = convolved(
+        [blocks([(odd_ref, b, 0, 48)]) for b in range(3)], [w1_ref[b] for b in range(3)], 48
+    )
     for x in range(8):
         pre_ref[x * 64 : x * 64 + 16] = pre[x * 64 : x * 64 + 16]
         pre_ref[x * 64 + 16 : (x + 1) * 64] = (
             pre[x * 64 + 16 : (x + 1) * 64] + over[x * 48 : (x + 1) * 48]
         )
     fetch.wait()
+    cot = upstream(cot_ref)
+    for t, tap in enumerate(TAPS):
+        back = lax.dot_general(cot, w2_ref[t], (((1,), (1,)), ((), ())), preferred_element_type=F32)
+        for k, at in enumerate(pieces(tap)):
+            back_ref[at : at + 8] = back[k * 8 : (k + 1) * 8]
 
 
 def local_kernel(
-    below_ref, first_ref, even_ref, odd_ref, pre_ref, w2_ref, cot_ref,
+    across_ref, beside_ref, first_ref, even_ref, odd_ref, pre_ref, w2_ref, back_ref, cot_ref,
     deep_ref, keep0_ref, keep1_ref, keep2_ref, keep3_ref, send0_ref, send1_ref, send2_ref, send3_ref,
     under_ref, patch_ref, early_ref,
 ):
     r = iota((48, ROWS), 0)
     y = 2 * row_of_slot(r % 16) + r // 16 - 1
     pick = (iota(r.shape, 1) == y).astype(F32).astype(BF16)
-    rows = jnp.dot(pick, below_ref[...], preferred_element_type=F32).astype(BF16)
+    place = lax.axis_index("space")
+    across = jnp.where(place > 0, across_ref[...], 0)
+    below = jnp.where(place % 2 == 1, beside_ref[...], across)
+    rows = jnp.dot(pick, below, preferred_element_type=F32).astype(BF16)
     for b in range(3):
         under_ref[b, :, :PAIR] = jnp.zeros((16, PAIR), BF16)
         under_ref[b, :, PAIR:] = rows[b * 16 : (b + 1) * 16]
@@ -157,27 +212,16 @@
 
     hidden = jnp.where(pre > 0, pre, SLOPE * pre)
 
-    def piece(xs, zs, a, b, c):
-        return (2 * xs + c) * 64 + (2 * zs + a) * 16 + b * 8
-
-    pieces = [(xs, zs) for xs in range(CELLS // 4) for zs in range(DEPTH // 4)]
-    taps = [(a, b, c) for a in range(2) for b in range(2) for c in range(2)]
-    cot = jnp.concatenate([cot_ref[:, x * C2 : (x + 1) * C2] for x in range(CELLS // 4)], axis=0)
+    cot = upstream(cot_ref)
     out = jnp.zeros((64, C2), F32)
-    delta_at = {}
-    for t, (a, b, c) in enumerate(taps):
-        starts = [piece(xs, zs, a, b, c) for xs, zs in pieces]
-        patch = jnp.concatenate([hidden[at : at + 8] for at in starts], axis=0).astype(BF16)
+    for t, tap in enumerate(TAPS):
+        patch = jnp.concatenate([hidden[at : at + 8] for at in pieces(tap)], axis=0).astype(BF16)
         patch_ref[t] = patch
         out = out + jnp.dot(patch, w2_ref[t], preferred_element_type=F32)
-        back = lax.dot_general(cot, w2_ref[t], (((1,), (1,)), ((), ())), preferred_element_type=F32)
-        for k, at in enumerate(starts):
-            delta_at[at] = back[k * 8 : (k + 1) * 8]
     out = out.astype(BF16)
     for x in range(CELLS // 4):
         deep_ref[:, x * C2 : (x + 1) * C2] = out[x * 16 : (x + 1) * 16]
-    back = jnp.concatenate([delta_at[at] for at in sorted(delta_at)], axis=0)
-    delta = (back * jnp.where(pre > 0, 1.0, SLOPE)).astype(BF16)
+    delta = (back_ref[...] * jnp.where(pre > 0, 1.0, SLOPE)).astype(BF16)
 
     for a in range(3):
         for b in range(3):
@@ -280,6 +324,22 @@
     return [near[m] for m in range(4)] + [far[m] for m in range(4)]
 
 
+def neighbours_planes(edge):
+    samples, spaces = lax.axis_size("sample"), lax.axis_size("space")
+
+    def partner(i, j):
+        k = j - 1 if j % 2 == 0 else j + 1
+        return (i, k) if 0 <= k < spaces else (i ^ 1, j)
+
+    places = [(i, j) for i in range(samples) for j in range(spaces)]
+    across = [[i * spaces + j for i, j in to] for to in (places, [partner(i, j) for i, j in places])]
+    beside = [i * spaces + (j ^ 1) for i, j in places]
+    return (
+        lax.ppermute(edge, ("sample", "space"), list(zip(*across))),
+        lax.ppermute(edge, ("sample", "space"), list(zip(across[0], beside))),
+    )
+
+
 def in_hbm(value):
     return pltpu.with_memory_space_constraint(value, pltpu.HBM)
 
@@ -290,34 +350,42 @@
     opens = open_cells[0]
     vmem = pl.BlockSpec(memory_space=pltpu.VMEM)
     hbm = pl.BlockSpec(memory_space=pltpu.HBM)
-    edge, opens, table, early = pl.pallas_call(
+    flat_cot = cotangent.reshape(DEPTH // 4 * ROWS // 4, CELLS // 4 * C2)
+    edge, opens, table, early, cot = pl.pallas_call(
         edge_kernel,
-        in_specs=[hbm] * 4,
-        out_specs=[vmem] * 4,
+        in_specs=[hbm] * 5,
+        out_specs=[vmem] * 5,
         out_shape=[
             jax.ShapeDtypeStruct((ROWS, WIDE), BF16),
             jax.ShapeDtypeStruct(opens.shape, opens.dtype),
             jax.ShapeDtypeStruct(bias_table.shape, bias_table.dtype),
             jax.ShapeDtypeStruct((9, 3 * C0, C1), BF16),
-        ],
-        scratch_shapes=[pltpu.VMEM((ROWS, WIDE), BF16), pltpu.SemaphoreType.DMA((4,))],
+            jax.ShapeDtypeStruct(flat_cot.shape, BF16),
+        ],
+        scratch_shapes=[pltpu.VMEM((ROWS, WIDE), BF16), pltpu.SemaphoreType.DMA((5,))],
         compiler_params=params,
         name="edge_plane",
-    )(in_hbm(acts), in_hbm(opens), in_hbm(bias_table), in_hbm(w_early.reshape(9, 3 * C0, C1)))
-    spaces = lax.axis_size("space")
-    below = lax.ppermute(edge, "space", [(i, i + 1) for i in range(spaces - 1)])
+    )(
+        in_hbm(acts),
+        in_hbm(opens),
+        in_hbm(bias_table),
+        in_hbm(w_early.reshape(9, 3 * C0, C1)),
+        in_hbm(flat_cot),
+    )
+    belows = neighbours_planes(edge)
     chosen = jnp.arange(bias_table.shape[0], dtype=jnp.int32)[:, None] == wind_class[0]
     bias = jnp.sum(jnp.where(chosen, table, jnp.zeros_like(table)), axis=0, keepdims=True)
     pair_rows = jax.ShapeDtypeStruct((3, 64, WIDE + PAIR), BF16)
     inner = pl.pallas_call(
         inner_kernel,
-        in_specs=[vmem] * 4 + [hbm],
-        out_specs=[vmem] * 4,
+        in_specs=[vmem] * 5 + [hbm],
+        out_specs=[vmem] * 5,
         out_shape=[
             pair_rows,
             pair_rows,
             jax.ShapeDtypeStruct((512, C1), F32),
             jax.ShapeDtypeStruct((8, C1, C2), BF16),
+            jax.ShapeDtypeStruct((512, C1), F32),
         ],
         scratch_shapes=[pltpu.SemaphoreType.DMA],
         compiler_params=params,
@@ -327,11 +395,12 @@
         opens,
         bias,
         early,
+        cot,
         in_hbm(w_deep.reshape(8, C1, C2)),
     )
     deep, *chunks = pl.pallas_call(
         local_kernel,
-        in_specs=[vmem] * 7,
+        in_specs=[vmem] * 9,
         out_specs=[vmem] * 9,
         out_shape=[
             jax.ShapeDtypeStruct((DEPTH // 4 * ROWS // 4, CELLS // 4 * C2), BF16),
@@ -345,7 +414,7 @@
         ],
         compiler_params=params,
         name="local_terms",
-    )(below, early, *inner, cotangent.reshape(DEPTH // 4 * ROWS // 4, CELLS // 4 * C2))
+    )(*belows, early, *inner, cot)
     deep, grad_deep, grad_early = spread(total(chunks[:4], chunks[4:]), deep)
     return (
         deep.reshape(1, DEPTH // 4, ROWS // 4, CELLS // 4 * C2),

time: 43.6 us -> 43 us (0.986)
  starting transfers between devices: 18.4 us -> 17.3 us
  waiting for transfers between devices: 18 us -> 18.6 us
    ppermute x1 -> x2, starting transfers between devices: 4.87 us -> 3.03 us  [the longest x1 3.03 us: neighbours_planes(): lax.ppermute(edge, ('sample', 'space'), list(zip(across[0], beside)))]
    ppermute x16, starting transfers between devices: 13.5 us -> 14.2 us  [swapped(): return lax.ppermute(value, ('sample', 'space'), pairs)]
    ppermute x1 -> x2, waiting for transfers between devices: 0.01 us -> 0.73 us  [the longest x1 0.73 us: neighbours_planes(): lax.ppermute(edge, ('sample', 'space'), list(zip(across[0], beside)))]
  transfers between devices with their start and end apart: 17 -> 18, of which waited for: 10 -> 12; matrix products, arithmetic and copies ran while one was open for 0% -> 0% of each run, Pallas kernels for 3% -> 4%
where the time goes in v4:
time: 43 us; the launch traced here: 42.9 us
  waiting for transfers between devices  18.6 us (43%)
  starting transfers between devices  17.3 us (40%)
  Pallas kernels  5.27 us (12%)
  between operations  1.37 us (3%)
    ppermute x16, waiting for transfers between devices, swapped(): return lax.ppermute(value, ('sample', 'space'), pairs)  17.9 us
    ppermute x16, starting transfers between devices, swapped(): return lax.ppermute(value, ('sample', 'space'), pairs)  14.2 us
    ppermute x1, starting transfers between devices, neighbours_planes(): lax.ppermute(edge, ('sample', 'space'), list(zip(across[0], beside)))  3.03 us
    pallas_call x1, Pallas kernels, body(): pl.pallas_call(inner_kernel, in_specs=[vmem] * 5 + [hbm], out_specs=[vmem...  1.61 us
    pallas_call x1, Pallas kernels, spread(): pl.pallas_call(spread_kernel, in_specs=[pl.BlockSpec(memory_space=pltpu.V...  1.42 us
    pallas_call x1, Pallas kernels, body(): pl.pallas_call(edge_kernel, in_specs=[hbm] * 5, out_specs=[vmem] * 5, out...  1.18 us
    pallas_call x1, Pallas kernels, body(): pl.pallas_call(local_kernel, in_specs=[vmem] * 9, out_specs=[vmem] * 9, o...  1.06 us
  transfers between devices with their start and end apart: 18, of which 12 were waited for; matrix products, arithmetic and copies ran while one was open for 0% of the time, Pallas kernels for 4%

profile of v4, /device:TPU:0, one launch (start us, length us, event | category | flops | bytes accessed | tf_op | source)
XLA Modules:
  0.0 42.9 jit_solution(2897969966171074385)
XLA Ops:
  0.6 1.2 %edge_plane.1 = (bf16[32,1024]{1,0:T(8,128)(2,1)S(1)}, s32[8,512]{1,0:T(8,128)S(1)}, f32[8,128]{1,0:T(8,128)S(1)}, bf16[9,192,128]{2,1,0:T(8,128)(2,1)S(1)}, bf16[16,1024]{1,0:T(8,128)(2,1)S(1)}) custom-call(bf16[8,32,1024]{2,1,0:T(8,128)(2,1)} %bitcast.11, s32[8,512]{1,0:T(8,128)} %bitcast.17, f32[8,128]{1,0:T(8,128)} %table_ref.1, ...), custom_call_target="tpu_custom_call" | custom-call | tf_op jit(solution)/shard_map/edge_plane/pallas_call | solution.py:354
  1.8 3.0 %collective-permute-start.1 = (bf16[32,1024]{1,0:T(8,128)(2,1)S(1)}, bf16[32,1024]{1,0:T(8,128)(2,1)S(1)}, u32[]{:S(2)}, u32[]{:S(2)}) collective-permute-start(bf16[32,1024]{1,0:T(8,128)(2,1)S(1)} %get-tuple-element.25), channel_id=1, source_target_pairs={{0,1},{1,0},{2,3},{3,2},{4,5},{5,4},{6,7},{7,6},{8,9},{9,8},{10,11... | collective-permute-start | bytes 196616 | tf_op jit(solution)/shard_map/ppermute | solution.py:339
  5.6 1.6 %inner_terms.1 = (bf16[3,64,1152]{2,1,0:T(8,128)(2,1)S(1)}, bf16[3,64,1152]{2,1,0:T(8,128)(2,1)S(1)}, f32[512,128]{1,0:T(8,128)S(1)}, bf16[8,128,256]{2,1,0:T(8,128)(2,1)S(1)}, f32[512,128]{1,0:T(8,128)S(1)}) custom-call(bf16[8,32,1024]{2,1,0:T(8,128)(2,1)S(1)} %bitcast.12, s32[8,512]{1,0:T(8,128)S(1)} %get-tuple-element.27.opens_ref, ...), custom_call_target="tpu_custom_call" | custom-call | tf_op jit(solution)/shard_map/inner_terms/pallas_call | solution.py:379
  7.2 0.7 %collective-permute-done.1.beside_ref = bf16[32,1024]{1,0:T(8,128)(2,1)S(1)} collective-permute-done((bf16[32,1024]{1,0:T(8,128)(2,1)S(1)}, bf16[32,1024]{1,0:T(8,128)(2,1)S(1)}, u32[]{:S(2)}, u32[]{:S(2)}) %collective-permute-start.1) | collective-permute-done | bytes 65568 | tf_op jit(solution)/shard_map/ppermute | solution.py:339
  8.0 1.1 %local_terms.1 = (bf16[16,1024]{1,0:T(8,128)(2,1)S(1)}, f32[472,128]{1,0:T(8,128)S(1)}, f32[472,128]{1,0:T(8,128)S(1)}, f32[472,128]{1,0:T(8,128)S(1)}, f32[472,...) custom-call(bf16[32,1024]{1,0:T(8,128)(2,1)S(1)} %collective-permute, ...), custom_call_target="tpu_custom_call" | custom-call | tf_op jit(solution)/shard_map/local_terms/pallas_call | solution.py:401
  9.1 0.5 %collective-permute-start.2 = (bf16[472,128]{1,0:T(8,128)(2,1)S(1)}, bf16[472,128]{1,0:T(8,128)(2,1)S(1)}, u32[]{:S(2)}, u32[]{:S(2)}) collective-permute-start(bf16[472,128]{1,0:T(8,128)(2,1)S(1)} %get-tuple-element.36), channel_id=1, source_target_pairs={{0,8},{1,9},{2,10},{3,11},{4,12},{5,13},{6,14},{7,15},{8,0},{9,1},... | collective-permute-start | bytes 362504 | tf_op jit(solution)/shard_map/ppermute | solution.py:297
  10.5 3.6 %collective-permute-start.4 = (bf16[472,128]{1,0:T(8,128)(2,1)S(1)}, bf16[472,128]{1,0:T(8,128)(2,1)S(1)}, u32[]{:S(2)}, u32[]{:S(2)}) collective-permute-start(bf16[472,128]{1,0:T(8,128)(2,1)S(1)} %add_convert_fusion.5), channel_id=1, source_target_pairs={{0,17},{1,16},{2,19},{3,18},{4,21},{5,20},{6,23},{7,22},{8,25},{9,... | collective-permute-start | bytes 362504 | tf_op jit(solution)/shard_map/ppermute | solution.py:297
  14.1 0.5 %collective-permute-start.6 = (bf16[472,128]{1,0:T(8,128)(2,1)S(1)}, bf16[472,128]{1,0:T(8,128)(2,1)S(1)}, u32[]{:S(2)}, u32[]{:S(2)}) collective-permute-start(bf16[472,128]{1,0:T(8,128)(2,1)S(1)} %add_convert_fusion.4), channel_id=1, source_target_pairs={{0,16},{1,17},{2,18},{3,19},{4,20},{5,21},{6,22},{7,23},{8,9},{9,8... | collective-permute-start | bytes 362504 | tf_op jit(solution)/shard_map/ppermute | solution.py:297
  14.6 0.6 %collective-permute-start.8 = (bf16[472,128]{1,0:T(8,128)(2,1)S(1)}, bf16[472,128]{1,0:T(8,128)(2,1)S(1)}, u32[]{:S(2)}, u32[]{:S(2)}) collective-permute-start(bf16[472,128]{1,0:T(8,128)(2,1)S(1)} %add_convert_fusion.3), channel_id=1, source_target_pairs={{0,1},{1,0},{2,3},{3,2},{4,5},{5,4},{6,7},{7,6},{8,24},{9,25},{10,... | collective-permute-start | bytes 362504 | tf_op jit(solution)/shard_map/ppermute | solution.py:297
  15.2 2.5 %collective-permute-done.4 = bf16[472,128]{1,0:T(8,128)(2,1)S(1)} collective-permute-done((bf16[472,128]{1,0:T(8,128)(2,1)S(1)}, bf16[472,128]{1,0:T(8,128)(2,1)S(1)}, u32[]{:S(2)}, u32[]{:S(2)}) %collective-permute-start.4) | collective-permute-done | bytes 120864 | tf_op jit(solution)/shard_map/ppermute | solution.py:297
  17.7 2.6 %collective-permute-done.6 = bf16[472,128]{1,0:T(8,128)(2,1)S(1)} collective-permute-done((bf16[472,128]{1,0:T(8,128)(2,1)S(1)}, bf16[472,128]{1,0:T(8,128)(2,1)S(1)}, u32[]{:S(2)}, u32[]{:S(2)}) %collective-permute-start.6) | collective-permute-done | bytes 120864 | tf_op jit(solution)/shard_map/ppermute | solution.py:297
  20.4 2.7 %collective-permute-start.9 = (bf16[472,128]{1,0:T(8,128)(2,1)S(1)}, bf16[472,128]{1,0:T(8,128)(2,1)S(1)}, u32[]{:S(2)}, u32[]{:S(2)}) collective-permute-start(bf16[472,128]{1,0:T(8,128)(2,1)S(1)} %add_convert_fusion.2), channel_id=1, source_target_pairs={{0,2},{1,3},{2,0},{3,1},{4,6},{5,7},{6,4},{7,5},{8,12},{9,13},{10,... | collective-permute-start | bytes 362504 | tf_op jit(solution)/shard_map/ppermute | solution.py:297
  23.2 4.0 %collective-permute-done.9 = bf16[472,128]{1,0:T(8,128)(2,1)S(1)} collective-permute-done((bf16[472,128]{1,0:T(8,128)(2,1)S(1)}, bf16[472,128]{1,0:T(8,128)(2,1)S(1)}, u32[]{:S(2)}, u32[]{:S(2)}) %collective-permute-start.9) | collective-permute-done | bytes 120864 | tf_op jit(solution)/shard_map/ppermute | solution.py:297
  27.1 2.2 %collective-permute-start.10 = (bf16[472,128]{1,0:T(8,128)(2,1)S(1)}, bf16[472,128]{1,0:T(8,128)(2,1)S(1)}, u32[]{:S(2)}, u32[]{:S(2)}) collective-permute-start(bf16[472,128]{1,0:T(8,128)(2,1)S(1)} %add_convert_fusion.1), channel_id=1, source_target_pairs={{0,4},{1,5},{2,6},{3,7},{4,0},{5,1},{6,2},{7,3},{8,10},{9,11},{10,... | collective-permute-start | bytes 362504 | tf_op jit(solution)/shard_map/ppermute | solution.py:297
  29.4 3.6 %collective-permute-done.10 = bf16[472,128]{1,0:T(8,128)(2,1)S(1)} collective-permute-done((bf16[472,128]{1,0:T(8,128)(2,1)S(1)}, bf16[472,128]{1,0:T(8,128)(2,1)S(1)}, u32[]{:S(2)}, u32[]{:S(2)}) %collective-permute-start.10) | collective-permute-done | bytes 120864 | tf_op jit(solution)/shard_map/ppermute | solution.py:297
  33.0 1.3 %collective-permute-start.13 = (bf16[472,128]{1,0:T(8,128)(2,1)S(1)}, bf16[472,128]{1,0:T(8,128)(2,1)S(1)}, u32[]{:S(2)}, u32[]{:S(2)}) collective-permute-start(bf16[472,128]{1,0:T(8,128)(2,1)S(1)} %add_convert_fusion.refs_0_), channel_id=1, source_target_pairs={{0,17},{1,16},{2,19},{3,18},{4,21},{5,20},{6,23},{7,22},{8,25},{9,... | collective-permute-start | bytes 362504 | tf_op jit(solution)/shard_map/ppermute | solution.py:297
  34.3 0.6 %collective-permute-start.12 = (bf16[472,128]{1,0:T(8,128)(2,1)S(1)}, bf16[472,128]{1,0:T(8,128)(2,1)S(1)}, u32[]{:S(2)}, u32[]{:S(2)}) collective-permute-start(bf16[472,128]{1,0:T(8,128)(2,1)S(1)} %add_convert_fusion.refs_0_), channel_id=1, source_target_pairs={{0,16},{1,17},{2,18},{3,19},{4,20},{5,21},{6,22},{7,23},{8,9},{9,8... | collective-permute-start | bytes 362504 | tf_op jit(solution)/shard_map/ppermute | solution.py:297
  34.9 1.6 %collective-permute-start.11 = (bf16[472,128]{1,0:T(8,128)(2,1)S(1)}, bf16[472,128]{1,0:T(8,128)(2,1)S(1)}, u32[]{:S(2)}, u32[]{:S(2)}) collective-permute-start(bf16[472,128]{1,0:T(8,128)(2,1)S(1)} %add_convert_fusion.refs_0_), channel_id=1, source_target_pairs={{0,1},{1,0},{2,3},{3,2},{4,5},{5,4},{6,7},{7,6},{8,24},{9,25},{10,... | collective-permute-start | bytes 362504 | tf_op jit(solution)/shard_map/ppermute | solution.py:297
  36.6 2.3 %collective-permute-done.13.refs_3_ = bf16[472,128]{1,0:T(8,128)(2,1)S(1)} collective-permute-done((bf16[472,128]{1,0:T(8,128)(2,1)S(1)}, bf16[472,128]{1,0:T(8,128)(2,1)S(1)}, u32[]{:S(2)}, u32[]{:S(2)}) %collective-permute-start.13) | collective-permute-done | bytes 120864 | tf_op jit(solution)/shard_map/ppermute | solution.py:297
  38.9 0.5 %collective-permute-done.12.refs_2_ = bf16[472,128]{1,0:T(8,128)(2,1)S(1)} collective-permute-done((bf16[472,128]{1,0:T(8,128)(2,1)S(1)}, bf16[472,128]{1,0:T(8,128)(2,1)S(1)}, u32[]{:S(2)}, u32[]{:S(2)}) %collective-permute-start.12) | collective-permute-done | bytes 120864 | tf_op jit(solution)/shard_map/ppermute | solution.py:297
  39.4 0.7 %collective-permute-done.11.refs_1_ = bf16[472,128]{1,0:T(8,128)(2,1)S(1)} collective-permute-done((bf16[472,128]{1,0:T(8,128)(2,1)S(1)}, bf16[472,128]{1,0:T(8,128)(2,1)S(1)}, u32[]{:S(2)}, u32[]{:S(2)}) %collective-permute-start.11) | collective-permute-done | bytes 120864 | tf_op jit(solution)/shard_map/ppermute | solution.py:297
  40.2 0.5 %collective-permute-done.16.refs_6_ = bf16[472,128]{1,0:T(8,128)(2,1)S(1)} collective-permute-done((bf16[472,128]{1,0:T(8,128)(2,1)S(1)}, bf16[472,128]{1,0:T(8,128)(2,1)S(1)}, u32[]{:S(2)}, u32[]{:S(2)}) %collective-permute-start.16) | collective-permute-done | bytes 120864 | tf_op jit(solution)/shard_map/ppermute | solution.py:297
  40.7 0.8 %collective-permute-done.15.refs_5_ = bf16[472,128]{1,0:T(8,128)(2,1)S(1)} collective-permute-done((bf16[472,128]{1,0:T(8,128)(2,1)S(1)}, bf16[472,128]{1,0:T(8,128)(2,1)S(1)}, u32[]{:S(2)}, u32[]{:S(2)}) %collective-permute-start.15) | collective-permute-done | bytes 120864 | tf_op jit(solution)/shard_map/ppermute | solution.py:297
  41.5 1.4 %spread_sums.1 = (bf16[16,1024]{1,0:T(8,128)(2,1)}, f32[8,128,256]{2,1,0:T(8,128)}, f32[1728,128]{1,0:T(8,128)}) custom-call(bf16[472,128]{1,0:T(8,128)(2,1)S(1)} %add_convert_fusion.refs_0_, bf16[472,128]{1,0:T(8,128)(2,1)S(1)} %collective-permute-done.11.refs_1_, bf16[472,128]{1,0:T(8,128)(2,1)S(1)} %collective-permute-done.12.refs_2_, ...), custom_call_target="tpu_custom_call" | custom-call | tf_op jit(solution)/shard_map/spread_sums/pallas_call | solution.py:271
  (26 shorter events, 1.3 us)
Async XLA Ops:
  0.6 5.0 %copy-start = (bf16[1,8,32,1024]{3,2,1,0:T(8,128)(2,1)S(1)}, bf16[1,8,32,1024]{3,2,1,0:T(8,128)(2,1)}, u32[]{:S(2)}) copy-start(bf16[1,8,32,1024]{3,2,1,0:T(8,128)(2,1)} %param.7) | copy-start | bytes 1572868
  1.8 6.1 %collective-permute-start.1 = (bf16[32,1024]{1,0:T(8,128)(2,1)S(1)}, bf16[32,1024]{1,0:T(8,128)(2,1)S(1)}, u32[]{:S(2)}, u32[]{:S(2)}) collective-permute-start(bf16[32,1024]{1,0:T(8,128)(2,1)S(1)} %get-tuple-element.25), channel_id=1, source_target_pairs={{0,1},{1,0},{2,3},{3,2},{4,5},{5,4},{6,7},{7,6},{8,9},{9,8},{10,11... | collective-permute-start | bytes 196616 | tf_op jit(solution)/shard_map/ppermute | solution.py:339
  4.9 3.1 %collective-permute-start = (bf16[32,1024]{1,0:T(8,128)(2,1)S(1)}, bf16[32,1024]{1,0:T(8,128)(2,1)S(1)}, u32[]{:S(2)}, u32[]{:S(2)}) collective-permute-start(bf16[32,1024]{1,0:T(8,128)(2,1)S(1)} %get-tuple-element.25), channel_id=1, source_target_pairs={{0,8},{1,2},{2,1},{3,4},{4,3},{5,6},{6,5},{7,15},{8,0},{9,10},{10,... | collective-permute-start | bytes 196616 | tf_op jit(solution)/shard_map/ppermute | solution.py:338
  9.0 1.4 %collective-permute-start.3 = (bf16[472,128]{1,0:T(8,128)(2,1)S(1)}, bf16[472,128]{1,0:T(8,128)(2,1)S(1)}, u32[]{:S(2)}, u32[]{:S(2)}) collective-permute-start(bf16[472,128]{1,0:T(8,128)(2,1)S(1)} %get-tuple-element.38), channel_id=1, source_target_pairs={{0,8},{1,9},{2,10},{3,11},{4,12},{5,13},{6,14},{7,15},{8,0},{9,1},... | collective-permute-start | bytes 362504 | tf_op jit(solution)/shard_map/ppermute | solution.py:297
  9.1 6.1 %collective-permute-start.2 = (bf16[472,128]{1,0:T(8,128)(2,1)S(1)}, bf16[472,128]{1,0:T(8,128)(2,1)S(1)}, u32[]{:S(2)}, u32[]{:S(2)}) collective-permute-start(bf16[472,128]{1,0:T(8,128)(2,1)S(1)} %get-tuple-element.36), channel_id=1, source_target_pairs={{0,8},{1,9},{2,10},{3,11},{4,12},{5,13},{6,14},{7,15},{8,0},{9,1},... | collective-permute-start | bytes 362504 | tf_op jit(solution)/shard_map/ppermute | solution.py:297
  9.6 4.4 %collective-permute-start.5 = (bf16[472,128]{1,0:T(8,128)(2,1)S(1)}, bf16[472,128]{1,0:T(8,128)(2,1)S(1)}, u32[]{:S(2)}, u32[]{:S(2)}) collective-permute-start(bf16[472,128]{1,0:T(8,128)(2,1)S(1)} %get-tuple-element.40), channel_id=1, source_target_pairs={{0,8},{1,9},{2,10},{3,11},{4,12},{5,13},{6,14},{7,15},{8,0},{9,1},... | collective-permute-start | bytes 362504 | tf_op jit(solution)/shard_map/ppermute | solution.py:297
  9.7 4.9 %collective-permute-start.7 = (bf16[472,128]{1,0:T(8,128)(2,1)S(1)}, bf16[472,128]{1,0:T(8,128)(2,1)S(1)}, u32[]{:S(2)}, u32[]{:S(2)}) collective-permute-start(bf16[472,128]{1,0:T(8,128)(2,1)S(1)} %get-tuple-element.42), channel_id=1, source_target_pairs={{0,8},{1,9},{2,10},{3,11},{4,12},{5,13},{6,14},{7,15},{8,0},{9,1},... | collective-permute-start | bytes 362504 | tf_op jit(solution)/shard_map/ppermute | solution.py:297
  10.5 7.3 %collective-permute-start.4 = (bf16[472,128]{1,0:T(8,128)(2,1)S(1)}, bf16[472,128]{1,0:T(8,128)(2,1)S(1)}, u32[]{:S(2)}, u32[]{:S(2)}) collective-permute-start(bf16[472,128]{1,0:T(8,128)(2,1)S(1)} %add_convert_fusion.5), channel_id=1, source_target_pairs={{0,17},{1,16},{2,19},{3,18},{4,21},{5,20},{6,23},{7,22},{8,25},{9,... | collective-permute-start | bytes 362504 | tf_op jit(solution)/shard_map/ppermute | solution.py:297
  14.1 6.3 %collective-permute-start.6 = (bf16[472,128]{1,0:T(8,128)(2,1)S(1)}, bf16[472,128]{1,0:T(8,128)(2,1)S(1)}, u32[]{:S(2)}, u32[]{:S(2)}) collective-permute-start(bf16[472,128]{1,0:T(8,128)(2,1)S(1)} %add_convert_fusion.4), channel_id=1, source_target_pairs={{0,16},{1,17},{2,18},{3,19},{4,20},{5,21},{6,22},{7,23},{8,9},{9,8... | collective-permute-start | bytes 362504 | tf_op jit(solution)/shard_map/ppermute | solution.py:297
  14.6 5.8 %collective-permute-start.8 = (bf16[472,128]{1,0:T(8,128)(2,1)S(1)}, bf16[472,128]{1,0:T(8,128)(2,1)S(1)}, u32[]{:S(2)}, u32[]{:S(2)}) collective-permute-start(bf16[472,128]{1,0:T(8,128)(2,1)S(1)} %add_convert_fusion.3), channel_id=1, source_target_pairs={{0,1},{1,0},{2,3},{3,2},{4,5},{5,4},{6,7},{7,6},{8,24},{9,25},{10,... | collective-permute-start | bytes 362504 | tf_op jit(solution)/shard_map/ppermute | solution.py:297
  20.4 6.7 %collective-permute-start.9 = (bf16[472,128]{1,0:T(8,128)(2,1)S(1)}, bf16[472,128]{1,0:T(8,128)(2,1)S(1)}, u32[]{:S(2)}, u32[]{:S(2)}) collective-permute-start(bf16[472,128]{1,0:T(8,128)(2,1)S(1)} %add_convert_fusion.2), channel_id=1, source_target_pairs={{0,2},{1,3},{2,0},{3,1},{4,6},{5,7},{6,4},{7,5},{8,12},{9,13},{10,... | collective-permute-start | bytes 362504 | tf_op jit(solution)/shard_map/ppermute | solution.py:297
  27.1 5.8 %collective-permute-start.10 = (bf16[472,128]{1,0:T(8,128)(2,1)S(1)}, bf16[472,128]{1,0:T(8,128)(2,1)S(1)}, u32[]{:S(2)}, u32[]{:S(2)}) collective-permute-start(bf16[472,128]{1,0:T(8,128)(2,1)S(1)} %add_convert_fusion.1), channel_id=1, source_target_pairs={{0,4},{1,5},{2,6},{3,7},{4,0},{5,1},{6,2},{7,3},{8,10},{9,11},{10,... | collective-permute-start | bytes 362504 | tf_op jit(solution)/shard_map/ppermute | solution.py:297
  33.0 5.9 %collective-permute-start.13 = (bf16[472,128]{1,0:T(8,128)(2,1)S(1)}, bf16[472,128]{1,0:T(8,128)(2,1)S(1)}, u32[]{:S(2)}, u32[]{:S(2)}) collective-permute-start(bf16[472,128]{1,0:T(8,128)(2,1)S(1)} %add_convert_fusion.refs_0_), channel_id=1, source_target_pairs={{0,17},{1,16},{2,19},{3,18},{4,21},{5,20},{6,23},{7,22},{8,25},{9,... | collective-permute-start | bytes 362504 | tf_op jit(solution)/shard_map/ppermute | solution.py:297
  34.3 5.1 %collective-permute-start.12 = (bf16[472,128]{1,0:T(8,128)(2,1)S(1)}, bf16[472,128]{1,0:T(8,128)(2,1)S(1)}, u32[]{:S(2)}, u32[]{:S(2)}) collective-permute-start(bf16[472,128]{1,0:T(8,128)(2,1)S(1)} %add_convert_fusion.refs_0_), channel_id=1, source_target_pairs={{0,16},{1,17},{2,18},{3,19},{4,20},{5,21},{6,22},{7,23},{8,9},{9,8... | collective-permute-start | bytes 362504 | tf_op jit(solution)/shard_map/ppermute | solution.py:297
  34.9 5.2 %collective-permute-start.11 = (bf16[472,128]{1,0:T(8,128)(2,1)S(1)}, bf16[472,128]{1,0:T(8,128)(2,1)S(1)}, u32[]{:S(2)}, u32[]{:S(2)}) collective-permute-start(bf16[472,128]{1,0:T(8,128)(2,1)S(1)} %add_convert_fusion.refs_0_), channel_id=1, source_target_pairs={{0,1},{1,0},{2,3},{3,2},{4,5},{5,4},{6,7},{7,6},{8,24},{9,25},{10,... | collective-permute-start | bytes 362504 | tf_op jit(solution)/shard_map/ppermute | solution.py:297
  36.6 3.6 %collective-permute-start.14 = (bf16[472,128]{1,0:T(8,128)(2,1)S(1)}, bf16[472,128]{1,0:T(8,128)(2,1)S(1)}, u32[]{:S(2)}, u32[]{:S(2)}) collective-permute-start(bf16[472,128]{1,0:T(8,128)(2,1)S(1)} %add_convert_fusion.refs_0_), channel_id=1, source_target_pairs={{0,8},{1,9},{2,10},{3,11},{4,12},{5,13},{6,14},{7,15},{8,0},{9,1},... | collective-permute-start | bytes 362504 | tf_op jit(solution)/shard_map/ppermute | solution.py:297
  38.9 1.3 %collective-permute-start.17 = (bf16[472,128]{1,0:T(8,128)(2,1)S(1)}, bf16[472,128]{1,0:T(8,128)(2,1)S(1)}, u32[]{:S(2)}, u32[]{:S(2)}) collective-permute-start(bf16[472,128]{1,0:T(8,128)(2,1)S(1)} %collective-permute-done.13.refs_3_), channel_id=1, source_target_pairs={{0,8},{1,9},{2,10},{3,11},{4,12},{5,13},{6,14},{7,15},{8,0},{9,1},... | collective-permute-start | bytes 362504 | tf_op jit(solution)/shard_map/ppermute | solution.py:297
  39.4 1.3 %collective-permute-start.16 = (bf16[472,128]{1,0:T(8,128)(2,1)S(1)}, bf16[472,128]{1,0:T(8,128)(2,1)S(1)}, u32[]{:S(2)}, u32[]{:S(2)}) collective-permute-start(bf16[472,128]{1,0:T(8,128)(2,1)S(1)} %collective-permute-done.12.refs_2_), channel_id=1, source_target_pairs={{0,8},{1,9},{2,10},{3,11},{4,12},{5,13},{6,14},{7,15},{8,0},{9,1},... | collective-permute-start | bytes 362504 | tf_op jit(solution)/shard_map/ppermute | solution.py:297
  40.1 1.3 %collective-permute-start.15 = (bf16[472,128]{1,0:T(8,128)(2,1)S(1)}, bf16[472,128]{1,0:T(8,128)(2,1)S(1)}, u32[]{:S(2)}, u32[]{:S(2)}) collective-permute-start(bf16[472,128]{1,0:T(8,128)(2,1)S(1)} %collective-permute-done.11.refs_1_), channel_id=1, source_target_pairs={{0,8},{1,9},{2,10},{3,11},{4,12},{5,13},{6,14},{7,15},{8,0},{9,1},... | collective-permute-start | bytes 362504 | tf_op jit(solution)/shard_map/ppermute | solution.py:297

commit v5 on v4

--- a/solution.py
+++ b/solution.py
@@ -1,3 +1,5 @@
+import functools
+
 import jax
 import jax.numpy as jnp
 from jax import lax
@@ -246,45 +248,47 @@
             ref[2 * C1 :] = early.astype(kind)
 
 
-def spread_kernel(*refs):
-    deep_in, deep_out, wide_out, low_out, wide_ref, low_ref, sems = refs[8:]
+def spread_kernel(names, *refs):
+    wide_out, low_out, wide_ref, low_ref, sems = refs[-5:]
     copies = []
 
     def send(source, target):
         copies.append(pltpu.make_async_copy(source, target, sems.at[len(copies)]))
         copies[-1].start()
 
-    for k in range(8):
-        chunk = chunk_of(k % 4, k // 4)
+    for k, name in enumerate(names):
+        chunk = chunk_of(name % 4, name // 4)
         wide_ref[k, :, :128] = refs[k][:C1].astype(F32)
         wide_ref[k, :, 128:] = refs[k][C1 : 2 * C1].astype(F32)
         send(wide_ref.at[k], wide_out.at[chunk])
         low_ref[k] = refs[k][2 * C1 :].astype(F32)
         at = pl.multiple_of(chunk * EARLY_ROWS, 8)
         send(low_ref.at[k], low_out.at[pl.ds(at, EARLY_ROWS), :])
-    send(deep_in, deep_out)
     for copy in copies:
         copy.wait()
 
 
-def spread(chunks, deep):
+def spread(chunks, names, into=()):
+    vmem = pl.BlockSpec(memory_space=pltpu.VMEM)
+    hbm = pl.BlockSpec(memory_space=pltpu.HBM)
+    count = len(names)
     return pl.pallas_call(
-        spread_kernel,
-        in_specs=[pl.BlockSpec(memory_space=pltpu.VMEM)] * 9,
-        out_specs=[pl.BlockSpec(memory_space=pltpu.HBM)] * 3,
+        functools.partial(spread_kernel, names),
+        in_specs=[vmem] * count + [hbm] * len(into),
+        out_specs=[hbm] * 2,
         out_shape=[
-            jax.ShapeDtypeStruct(deep.shape, BF16),
             jax.ShapeDtypeStruct((8, C1, C2), F32),
             jax.ShapeDtypeStruct((27 * C0, C1), F32),
         ],
+        input_output_aliases={count: 0, count + 1: 1} if into else {},
         scratch_shapes=[
-            pltpu.VMEM((8, C1, C2), F32),
-            pltpu.VMEM((8, EARLY_ROWS, 128), F32),
-            pltpu.SemaphoreType.DMA((17,)),
+            pltpu.VMEM((count, C1, C2), F32),
+            pltpu.VMEM((count, EARLY_ROWS, 128), F32),
+            pltpu.SemaphoreType.DMA((2 * count,)),
         ],
         compiler_params=pltpu.CompilerParams(vmem_limit_bytes=VMEM_BYTES),
         name="spread_sums",
-    )(*chunks, deep)
+    )(*[chunks[k] for k in names], *into)
 
 
 def swapped(value, flips):
@@ -302,12 +306,12 @@
 
 
 def total(keep, send):
-    got = {m: swapped(send[m], SIBLING) for m in (3, 2, 1, 0)}
+    got = {m: swapped(send[m], SIBLING) for m in (1, 2, 3, 0)}
     quad = {}
-    for m in (3, 2, 1):
+    for m in (1, 2, 3):
         quad[m] = swapped((keep[m] + got[m].astype(F32)).astype(BF16), QUAD[m])
     mine = keep[0] + got[0].astype(F32)
-    for m in (3, 2, 1):
+    for m in (1, 2, 3):
         mine = mine + quad[m].astype(F32)
     rest = []
     for axis, bit in (("space", 2), ("sample", 4)):
@@ -318,7 +322,7 @@
         own = mine.astype(BF16)
         mine = own.astype(F32) + swapped(own, flips).astype(F32)
     near = {0: mine.astype(BF16)}
-    for m in (3, 2, 1):
+    for m in (3, 1, 2):
         near[m] = swapped(near[0], QUAD[m])
     far = {m: swapped(near[m], SIBLING) for m in range(4)}
     return [near[m] for m in range(4)] + [far[m] for m in range(4)]
@@ -415,7 +419,10 @@
         compiler_params=params,
         name="local_terms",
     )(*belows, early, *inner, cot)
-    deep, grad_deep, grad_early = spread(total(chunks[:4], chunks[4:]), deep)
+    sums, grads = total(chunks[:4], chunks[4:]), ()
+    for names in ((0, 3, 1, 2, 4, 7), (5, 6)):
+        grads = spread(sums, names, grads)
+    grad_deep, grad_early = grads
     return (
         deep.reshape(1, DEPTH // 4, ROWS // 4, CELLS // 4 * C2),
         grad_deep.reshape(w_deep.shape),

time: 43 us -> 42.4 us (0.986)
  waiting for transfers between devices: 18.6 us -> 16.8 us
  Pallas kernels: 5.27 us -> 6.06 us
    ppermute x16, waiting for transfers between devices: 17.9 us -> 16 us  [swapped(): return lax.ppermute(value, ('sample', 'space'), pairs)]
    pallas_call x1 -> x2, Pallas kernels: 1.42 us -> 2.04 us  [spread(): pl.pallas_call(functools.partial(spread_kernel, names), in_specs=[vmem] *...]
  transfers between devices with their start and end apart: 18 -> 18, of which waited for: 12 -> 11; matrix products, arithmetic and copies ran while one was open for 0% -> 0% of each run, Pallas kernels for 4% -> 7%
where the time goes in v5:
time: 42.4 us; the launch traced here: 42 us
  starting transfers between devices  17.5 us (41%)
  waiting for transfers between devices  16.8 us (40%)
  Pallas kernels  6.06 us (14%)
  between operations  1.37 us (3%)
    ppermute x16, waiting for transfers between devices, swapped(): return lax.ppermute(value, ('sample', 'space'), pairs)  16 us
    ppermute x16, starting transfers between devices, swapped(): return lax.ppermute(value, ('sample', 'space'), pairs)  14.4 us
    ppermute x1, starting transfers between devices, neighbours_planes(): lax.ppermute(edge, ('sample', 'space'), list(zip(across[0], beside)))  3.03 us
    pallas_call x2, Pallas kernels, spread(): pl.pallas_call(functools.partial(spread_kernel, names), in_specs=[vmem] *...  2.04 us
    pallas_call x1, Pallas kernels, body(): pl.pallas_call(inner_kernel, in_specs=[vmem] * 5 + [hbm], out_specs=[vmem...  1.61 us
    pallas_call x1, Pallas kernels, body(): pl.pallas_call(local_kernel, in_specs=[vmem] * 9, out_specs=[vmem] * 9, o...  1.23 us
    pallas_call x1, Pallas kernels, body(): pl.pallas_call(edge_kernel, in_specs=[hbm] * 5, out_specs=[vmem] * 5, out...  1.18 us
  transfers between devices with their start and end apart: 18, of which 11 were waited for; matrix products, arithmetic and copies ran while one was open for 0% of the time, Pallas kernels for 7%

profile of v5, /device:TPU:0, one launch (start us, length us, event | category | flops | bytes accessed | tf_op | source)
XLA Modules:
  0.0 42.0 jit_solution(954062116154977270)
XLA Ops:
  0.6 1.2 %edge_plane.1 = (bf16[32,1024]{1,0:T(8,128)(2,1)S(1)}, s32[8,512]{1,0:T(8,128)S(1)}, f32[8,128]{1,0:T(8,128)S(1)}, bf16[9,192,128]{2,1,0:T(8,128)(2,1)S(1)}, bf16[16,1024]{1,0:T(8,128)(2,1)S(1)}) custom-call(bf16[8,32,1024]{2,1,0:T(8,128)(2,1)} %bitcast.11, s32[8,512]{1,0:T(8,128)} %bitcast.19, f32[8,128]{1,0:T(8,128)} %table_ref.1, ...), custom_call_target="tpu_custom_call" | custom-call | tf_op jit(solution)/shard_map/edge_plane/pallas_call | solution.py:358
  1.8 3.0 %collective-permute-start.1 = (bf16[32,1024]{1,0:T(8,128)(2,1)S(1)}, bf16[32,1024]{1,0:T(8,128)(2,1)S(1)}, u32[]{:S(2)}, u32[]{:S(2)}) collective-permute-start(bf16[32,1024]{1,0:T(8,128)(2,1)S(1)} %get-tuple-element.26), channel_id=1, source_target_pairs={{0,1},{1,0},{2,3},{3,2},{4,5},{5,4},{6,7},{7,6},{8,9},{9,8},{10,11... | collective-permute-start | bytes 196616 | tf_op jit(solution)/shard_map/ppermute | solution.py:343
  5.6 1.6 %inner_terms.1 = (bf16[3,64,1152]{2,1,0:T(8,128)(2,1)S(1)}, bf16[3,64,1152]{2,1,0:T(8,128)(2,1)S(1)}, f32[512,128]{1,0:T(8,128)S(1)}, bf16[8,128,256]{2,1,0:T(8,128)(2,1)S(1)}, f32[512,128]{1,0:T(8,128)S(1)}) custom-call(bf16[8,32,1024]{2,1,0:T(8,128)(2,1)S(1)} %bitcast.12, s32[8,512]{1,0:T(8,128)S(1)} %get-tuple-element.28.opens_ref, ...), custom_call_target="tpu_custom_call" | custom-call | tf_op jit(solution)/shard_map/inner_terms/pallas_call | solution.py:383
  7.2 0.7 %collective-permute-done.1.beside_ref = bf16[32,1024]{1,0:T(8,128)(2,1)S(1)} collective-permute-done((bf16[32,1024]{1,0:T(8,128)(2,1)S(1)}, bf16[32,1024]{1,0:T(8,128)(2,1)S(1)}, u32[]{:S(2)}, u32[]{:S(2)}) %collective-permute-start.1) | collective-permute-done | bytes 65568 | tf_op jit(solution)/shard_map/ppermute | solution.py:343
  8.0 1.2 %local_terms.1 = (bf16[16,1024]{1,0:T(8,128)(2,1)}, f32[472,128]{1,0:T(8,128)S(1)}, f32[472,128]{1,0:T(8,128)S(1)}, f32[472,128]{1,0:T(8,128)S(1)}, f32[472,128]...) custom-call(bf16[32,1024]{1,0:T(8,128)(2,1)S(1)} %collective-permute, ...), custom_call_target="tpu_custom_call" | custom-call | tf_op jit(solution)/shard_map/local_terms/pallas_call | solution.py:405
  9.2 0.5 %collective-permute-start.2 = (bf16[472,128]{1,0:T(8,128)(2,1)S(1)}, bf16[472,128]{1,0:T(8,128)(2,1)S(1)}, u32[]{:S(2)}, u32[]{:S(2)}) collective-permute-start(bf16[472,128]{1,0:T(8,128)(2,1)S(1)} %get-tuple-element.38), channel_id=1, source_target_pairs={{0,8},{1,9},{2,10},{3,11},{4,12},{5,13},{6,14},{7,15},{8,0},{9,1},... | collective-permute-start | bytes 362504 | tf_op jit(solution)/shard_map/ppermute | solution.py:301
  9.7 0.5 %collective-permute-start.7 = (bf16[472,128]{1,0:T(8,128)(2,1)S(1)}, bf16[472,128]{1,0:T(8,128)(2,1)S(1)}, u32[]{:S(2)}, u32[]{:S(2)}) collective-permute-start(bf16[472,128]{1,0:T(8,128)(2,1)S(1)} %get-tuple-element.44), channel_id=1, source_target_pairs={{0,8},{1,9},{2,10},{3,11},{4,12},{5,13},{6,14},{7,15},{8,0},{9,1},... | collective-permute-start | bytes 362504 | tf_op jit(solution)/shard_map/ppermute | solution.py:301
  10.6 2.5 %collective-permute-start.4 = (bf16[472,128]{1,0:T(8,128)(2,1)S(1)}, bf16[472,128]{1,0:T(8,128)(2,1)S(1)}, u32[]{:S(2)}, u32[]{:S(2)}) collective-permute-start(bf16[472,128]{1,0:T(8,128)(2,1)S(1)} %add_convert_fusion.5), channel_id=1, source_target_pairs={{0,1},{1,0},{2,3},{3,2},{4,5},{5,4},{6,7},{7,6},{8,24},{9,25},{10,... | collective-permute-start | bytes 362504 | tf_op jit(solution)/shard_map/ppermute | solution.py:301
  13.1 1.7 %collective-permute-start.6 = (bf16[472,128]{1,0:T(8,128)(2,1)S(1)}, bf16[472,128]{1,0:T(8,128)(2,1)S(1)}, u32[]{:S(2)}, u32[]{:S(2)}) collective-permute-start(bf16[472,128]{1,0:T(8,128)(2,1)S(1)} %add_convert_fusion.4), channel_id=1, source_target_pairs={{0,16},{1,17},{2,18},{3,19},{4,20},{5,21},{6,22},{7,23},{8,9},{9,8... | collective-permute-start | bytes 362504 | tf_op jit(solution)/shard_map/ppermute | solution.py:301
  15.2 1.2 %collective-permute-done.4 = bf16[472,128]{1,0:T(8,128)(2,1)S(1)} collective-permute-done((bf16[472,128]{1,0:T(8,128)(2,1)S(1)}, bf16[472,128]{1,0:T(8,128)(2,1)S(1)}, u32[]{:S(2)}, u32[]{:S(2)}) %collective-permute-start.4) | collective-permute-done | bytes 120864 | tf_op jit(solution)/shard_map/ppermute | solution.py:301
  16.3 2.9 %collective-permute-done.6 = bf16[472,128]{1,0:T(8,128)(2,1)S(1)} collective-permute-done((bf16[472,128]{1,0:T(8,128)(2,1)S(1)}, bf16[472,128]{1,0:T(8,128)(2,1)S(1)}, u32[]{:S(2)}, u32[]{:S(2)}) %collective-permute-start.6) | collective-permute-done | bytes 120864 | tf_op jit(solution)/shard_map/ppermute | solution.py:301
  19.3 1.4 %collective-permute-done.8 = bf16[472,128]{1,0:T(8,128)(2,1)S(1)} collective-permute-done((bf16[472,128]{1,0:T(8,128)(2,1)S(1)}, bf16[472,128]{1,0:T(8,128)(2,1)S(1)}, u32[]{:S(2)}, u32[]{:S(2)}) %collective-permute-start.8) | collective-permute-done | bytes 120864 | tf_op jit(solution)/shard_map/ppermute | solution.py:301
  20.8 2.7 %collective-permute-start.9 = (bf16[472,128]{1,0:T(8,128)(2,1)S(1)}, bf16[472,128]{1,0:T(8,128)(2,1)S(1)}, u32[]{:S(2)}, u32[]{:S(2)}) collective-permute-start(bf16[472,128]{1,0:T(8,128)(2,1)S(1)} %add_convert_fusion.2), channel_id=1, source_target_pairs={{0,2},{1,3},{2,0},{3,1},{4,6},{5,7},{6,4},{7,5},{8,12},{9,13},{10,... | collective-permute-start | bytes 362504 | tf_op jit(solution)/shard_map/ppermute | solution.py:301
  23.4 3.3 %collective-permute-done.9 = bf16[472,128]{1,0:T(8,128)(2,1)S(1)} collective-permute-done((bf16[472,128]{1,0:T(8,128)(2,1)S(1)}, bf16[472,128]{1,0:T(8,128)(2,1)S(1)}, u32[]{:S(2)}, u32[]{:S(2)}) %collective-permute-start.9) | collective-permute-done | bytes 120864 | tf_op jit(solution)/shard_map/ppermute | solution.py:301
  26.8 2.6 %collective-permute-start.10 = (bf16[472,128]{1,0:T(8,128)(2,1)S(1)}, bf16[472,128]{1,0:T(8,128)(2,1)S(1)}, u32[]{:S(2)}, u32[]{:S(2)}) collective-permute-start(bf16[472,128]{1,0:T(8,128)(2,1)S(1)} %add_convert_fusion.1), channel_id=1, source_target_pairs={{0,4},{1,5},{2,6},{3,7},{4,0},{5,1},{6,2},{7,3},{8,10},{9,11},{10,... | collective-permute-start | bytes 362504 | tf_op jit(solution)/shard_map/ppermute | solution.py:301
  29.4 3.2 %collective-permute-done.10 = bf16[472,128]{1,0:T(8,128)(2,1)S(1)} collective-permute-done((bf16[472,128]{1,0:T(8,128)(2,1)S(1)}, bf16[472,128]{1,0:T(8,128)(2,1)S(1)}, u32[]{:S(2)}, u32[]{:S(2)}) %collective-permute-start.10) | collective-permute-done | bytes 120864 | tf_op jit(solution)/shard_map/ppermute | solution.py:301
  32.6 1.6 %collective-permute-start.15 = (bf16[472,128]{1,0:T(8,128)(2,1)S(1)}, bf16[472,128]{1,0:T(8,128)(2,1)S(1)}, u32[]{:S(2)}, u32[]{:S(2)}) collective-permute-start(bf16[472,128]{1,0:T(8,128)(2,1)S(1)} %add_convert_fusion.refs_0_), channel_id=1, source_target_pairs={{0,17},{1,16},{2,19},{3,18},{4,21},{5,20},{6,23},{7,22},{8,25},{9,... | collective-permute-start | bytes 362504 | tf_op jit(solution)/shard_map/ppermute | solution.py:301
  34.3 0.7 %collective-permute-start.13 = (bf16[472,128]{1,0:T(8,128)(2,1)S(1)}, bf16[472,128]{1,0:T(8,128)(2,1)S(1)}, u32[]{:S(2)}, u32[]{:S(2)}) collective-permute-start(bf16[472,128]{1,0:T(8,128)(2,1)S(1)} %add_convert_fusion.refs_0_), channel_id=1, source_target_pairs={{0,16},{1,17},{2,18},{3,19},{4,20},{5,21},{6,22},{7,23},{8,9},{9,8... | collective-permute-start | bytes 362504 | tf_op jit(solution)/shard_map/ppermute | solution.py:301
  35.0 1.2 %collective-permute-start.11 = (bf16[472,128]{1,0:T(8,128)(2,1)S(1)}, bf16[472,128]{1,0:T(8,128)(2,1)S(1)}, u32[]{:S(2)}, u32[]{:S(2)}) collective-permute-start(bf16[472,128]{1,0:T(8,128)(2,1)S(1)} %add_convert_fusion.refs_0_), channel_id=1, source_target_pairs={{0,1},{1,0},{2,3},{3,2},{4,5},{5,4},{6,7},{7,6},{8,24},{9,25},{10,... | collective-permute-start | bytes 362504 | tf_op jit(solution)/shard_map/ppermute | solution.py:301
  36.2 2.3 %collective-permute-done.15.refs_1_ = bf16[472,128]{1,0:T(8,128)(2,1)S(1)} collective-permute-done((bf16[472,128]{1,0:T(8,128)(2,1)S(1)}, bf16[472,128]{1,0:T(8,128)(2,1)S(1)}, u32[]{:S(2)}, u32[]{:S(2)}) %collective-permute-start.15) | collective-permute-done | bytes 120864 | tf_op jit(solution)/shard_map/ppermute | solution.py:301
  38.5 0.7 %collective-permute-done.13.refs_3_ = bf16[472,128]{1,0:T(8,128)(2,1)S(1)} collective-permute-done((bf16[472,128]{1,0:T(8,128)(2,1)S(1)}, bf16[472,128]{1,0:T(8,128)(2,1)S(1)}, u32[]{:S(2)}, u32[]{:S(2)}) %collective-permute-start.13) | collective-permute-done | bytes 120864 | tf_op jit(solution)/shard_map/ppermute | solution.py:301
  39.1 0.7 %collective-permute-done.11.refs_2_ = bf16[472,128]{1,0:T(8,128)(2,1)S(1)} collective-permute-done((bf16[472,128]{1,0:T(8,128)(2,1)S(1)}, bf16[472,128]{1,0:T(8,128)(2,1)S(1)}, u32[]{:S(2)}, u32[]{:S(2)}) %collective-permute-start.11) | collective-permute-done | bytes 120864 | tf_op jit(solution)/shard_map/ppermute | solution.py:301
  39.9 1.2 %spread_sums.2 = (f32[8,128,256]{2,1,0:T(8,128)}, f32[1728,128]{1,0:T(8,128)}) custom-call(bf16[472,128]{1,0:T(8,128)(2,1)S(1)} %add_convert_fusion.refs_0_, bf16[472,128]{1,0:T(8,128)(2,1)S(1)} %collective-permute-done.15.refs_1_, bf16[472,128]{1,0:T(8,128)(2,1)S(1)} %collective-permute-done.11.refs_2_, ...), custom_call_target="tpu_custom_call" | custom-call | tf_op jit(solution)/shard_map/spread_sums/pallas_call | solution.py:275
  41.2 0.8 %spread_sums.3 = (f32[8,128,256]{2,1,0:T(8,128)}, f32[1728,128]{1,0:T(8,128)}) custom-call(bf16[472,128]{1,0:T(8,128)(2,1)S(1)} %collective-permute-done.12.refs_0_, bf16[472,128]{1,0:T(8,128)(2,1)S(1)} %collective-permute-done.14.refs_1_, f32[8,128,256]{2,1,0:T(8,128)} %get-tuple-element.45.refs_2_, ...), custom_call_target="tpu_custom_call", output_to_operand_aliasing={{0}: (2, {}), {1}: (3, {})} | custom-call | tf_op jit(solution)/shard_map/spread_sums/pallas_call | solution.py:275
  (27 shorter events, 1.1 us)
Async XLA Ops:
  0.6 5.0 %copy-start = (bf16[1,8,32,1024]{3,2,1,0:T(8,128)(2,1)S(1)}, bf16[1,8,32,1024]{3,2,1,0:T(8,128)(2,1)}, u32[]{:S(2)}) copy-start(bf16[1,8,32,1024]{3,2,1,0:T(8,128)(2,1)} %param.7) | copy-start | bytes 1572868
  1.8 6.1 %collective-permute-start.1 = (bf16[32,1024]{1,0:T(8,128)(2,1)S(1)}, bf16[32,1024]{1,0:T(8,128)(2,1)S(1)}, u32[]{:S(2)}, u32[]{:S(2)}) collective-permute-start(bf16[32,1024]{1,0:T(8,128)(2,1)S(1)} %get-tuple-element.26), channel_id=1, source_target_pairs={{0,1},{1,0},{2,3},{3,2},{4,5},{5,4},{6,7},{7,6},{8,9},{9,8},{10,11... | collective-permute-start | bytes 196616 | tf_op jit(solution)/shard_map/ppermute | solution.py:343
  4.9 3.1 %collective-permute-start = (bf16[32,1024]{1,0:T(8,128)(2,1)S(1)}, bf16[32,1024]{1,0:T(8,128)(2,1)S(1)}, u32[]{:S(2)}, u32[]{:S(2)}) collective-permute-start(bf16[32,1024]{1,0:T(8,128)(2,1)S(1)} %get-tuple-element.26), channel_id=1, source_target_pairs={{0,8},{1,2},{2,1},{3,4},{4,3},{5,6},{6,5},{7,15},{8,0},{9,10},{10,... | collective-permute-start | bytes 196616 | tf_op jit(solution)/shard_map/ppermute | solution.py:342
  9.2 1.3 %collective-permute-start.3 = (bf16[472,128]{1,0:T(8,128)(2,1)S(1)}, bf16[472,128]{1,0:T(8,128)(2,1)S(1)}, u32[]{:S(2)}, u32[]{:S(2)}) collective-permute-start(bf16[472,128]{1,0:T(8,128)(2,1)S(1)} %get-tuple-element.40), channel_id=1, source_target_pairs={{0,8},{1,9},{2,10},{3,11},{4,12},{5,13},{6,14},{7,15},{8,0},{9,1},... | collective-permute-start | bytes 362504 | tf_op jit(solution)/shard_map/ppermute | solution.py:301
  9.2 6.0 %collective-permute-start.2 = (bf16[472,128]{1,0:T(8,128)(2,1)S(1)}, bf16[472,128]{1,0:T(8,128)(2,1)S(1)}, u32[]{:S(2)}, u32[]{:S(2)}) collective-permute-start(bf16[472,128]{1,0:T(8,128)(2,1)S(1)} %get-tuple-element.38), channel_id=1, source_target_pairs={{0,8},{1,9},{2,10},{3,11},{4,12},{5,13},{6,14},{7,15},{8,0},{9,1},... | collective-permute-start | bytes 362504 | tf_op jit(solution)/shard_map/ppermute | solution.py:301
  9.7 3.4 %collective-permute-start.5 = (bf16[472,128]{1,0:T(8,128)(2,1)S(1)}, bf16[472,128]{1,0:T(8,128)(2,1)S(1)}, u32[]{:S(2)}, u32[]{:S(2)}) collective-permute-start(bf16[472,128]{1,0:T(8,128)(2,1)S(1)} %get-tuple-element.42), channel_id=1, source_target_pairs={{0,8},{1,9},{2,10},{3,11},{4,12},{5,13},{6,14},{7,15},{8,0},{9,1},... | collective-permute-start | bytes 362504 | tf_op jit(solution)/shard_map/ppermute | solution.py:301
  9.7 5.1 %collective-permute-start.7 = (bf16[472,128]{1,0:T(8,128)(2,1)S(1)}, bf16[472,128]{1,0:T(8,128)(2,1)S(1)}, u32[]{:S(2)}, u32[]{:S(2)}) collective-permute-start(bf16[472,128]{1,0:T(8,128)(2,1)S(1)} %get-tuple-element.44), channel_id=1, source_target_pairs={{0,8},{1,9},{2,10},{3,11},{4,12},{5,13},{6,14},{7,15},{8,0},{9,1},... | collective-permute-start | bytes 362504 | tf_op jit(solution)/shard_map/ppermute | solution.py:301
  10.6 5.8 %collective-permute-start.4 = (bf16[472,128]{1,0:T(8,128)(2,1)S(1)}, bf16[472,128]{1,0:T(8,128)(2,1)S(1)}, u32[]{:S(2)}, u32[]{:S(2)}) collective-permute-start(bf16[472,128]{1,0:T(8,128)(2,1)S(1)} %add_convert_fusion.5), channel_id=1, source_target_pairs={{0,1},{1,0},{2,3},{3,2},{4,5},{5,4},{6,7},{7,6},{8,24},{9,25},{10,... | collective-permute-start | bytes 362504 | tf_op jit(solution)/shard_map/ppermute | solution.py:301
  13.1 6.1 %collective-permute-start.6 = (bf16[472,128]{1,0:T(8,128)(2,1)S(1)}, bf16[472,128]{1,0:T(8,128)(2,1)S(1)}, u32[]{:S(2)}, u32[]{:S(2)}) collective-permute-start(bf16[472,128]{1,0:T(8,128)(2,1)S(1)} %add_convert_fusion.4), channel_id=1, source_target_pairs={{0,16},{1,17},{2,18},{3,19},{4,20},{5,21},{6,22},{7,23},{8,9},{9,8... | collective-permute-start | bytes 362504 | tf_op jit(solution)/shard_map/ppermute | solution.py:301
  14.8 5.8 %collective-permute-start.8 = (bf16[472,128]{1,0:T(8,128)(2,1)S(1)}, bf16[472,128]{1,0:T(8,128)(2,1)S(1)}, u32[]{:S(2)}, u32[]{:S(2)}) collective-permute-start(bf16[472,128]{1,0:T(8,128)(2,1)S(1)} %add_convert_fusion.3), channel_id=1, source_target_pairs={{0,17},{1,16},{2,19},{3,18},{4,21},{5,20},{6,23},{7,22},{8,25},{9,... | collective-permute-start | bytes 362504 | tf_op jit(solution)/shard_map/ppermute | solution.py:301
  20.8 6.0 %collective-permute-start.9 = (bf16[472,128]{1,0:T(8,128)(2,1)S(1)}, bf16[472,128]{1,0:T(8,128)(2,1)S(1)}, u32[]{:S(2)}, u32[]{:S(2)}) collective-permute-start(bf16[472,128]{1,0:T(8,128)(2,1)S(1)} %add_convert_fusion.2), channel_id=1, source_target_pairs={{0,2},{1,3},{2,0},{3,1},{4,6},{5,7},{6,4},{7,5},{8,12},{9,13},{10,... | collective-permute-start | bytes 362504 | tf_op jit(solution)/shard_map/ppermute | solution.py:301
  26.8 5.8 %collective-permute-start.10 = (bf16[472,128]{1,0:T(8,128)(2,1)S(1)}, bf16[472,128]{1,0:T(8,128)(2,1)S(1)}, u32[]{:S(2)}, u32[]{:S(2)}) collective-permute-start(bf16[472,128]{1,0:T(8,128)(2,1)S(1)} %add_convert_fusion.1), channel_id=1, source_target_pairs={{0,4},{1,5},{2,6},{3,7},{4,0},{5,1},{6,2},{7,3},{8,10},{9,11},{10,... | collective-permute-start | bytes 362504 | tf_op jit(solution)/shard_map/ppermute | solution.py:301
  32.6 5.8 %collective-permute-start.15 = (bf16[472,128]{1,0:T(8,128)(2,1)S(1)}, bf16[472,128]{1,0:T(8,128)(2,1)S(1)}, u32[]{:S(2)}, u32[]{:S(2)}) collective-permute-start(bf16[472,128]{1,0:T(8,128)(2,1)S(1)} %add_convert_fusion.refs_0_), channel_id=1, source_target_pairs={{0,17},{1,16},{2,19},{3,18},{4,21},{5,20},{6,23},{7,22},{8,25},{9,... | collective-permute-start | bytes 362504 | tf_op jit(solution)/shard_map/ppermute | solution.py:301
  34.3 4.9 %collective-permute-start.13 = (bf16[472,128]{1,0:T(8,128)(2,1)S(1)}, bf16[472,128]{1,0:T(8,128)(2,1)S(1)}, u32[]{:S(2)}, u32[]{:S(2)}) collective-permute-start(bf16[472,128]{1,0:T(8,128)(2,1)S(1)} %add_convert_fusion.refs_0_), channel_id=1, source_target_pairs={{0,16},{1,17},{2,18},{3,19},{4,20},{5,21},{6,22},{7,23},{8,9},{9,8... | collective-permute-start | bytes 362504 | tf_op jit(solution)/shard_map/ppermute | solution.py:301
  35.0 4.9 %collective-permute-start.11 = (bf16[472,128]{1,0:T(8,128)(2,1)S(1)}, bf16[472,128]{1,0:T(8,128)(2,1)S(1)}, u32[]{:S(2)}, u32[]{:S(2)}) collective-permute-start(bf16[472,128]{1,0:T(8,128)(2,1)S(1)} %add_convert_fusion.refs_0_), channel_id=1, source_target_pairs={{0,1},{1,0},{2,3},{3,2},{4,5},{5,4},{6,7},{7,6},{8,24},{9,25},{10,... | collective-permute-start | bytes 362504 | tf_op jit(solution)/shard_map/ppermute | solution.py:301
  36.2 3.6 %collective-permute-start.16 = (bf16[472,128]{1,0:T(8,128)(2,1)S(1)}, bf16[472,128]{1,0:T(8,128)(2,1)S(1)}, u32[]{:S(2)}, u32[]{:S(2)}) collective-permute-start(bf16[472,128]{1,0:T(8,128)(2,1)S(1)} %add_convert_fusion.refs_0_), channel_id=1, source_target_pairs={{0,8},{1,9},{2,10},{3,11},{4,12},{5,13},{6,14},{7,15},{8,0},{9,1},... | collective-permute-start | bytes 362504 | tf_op jit(solution)/shard_map/ppermute | solution.py:301
  38.5 1.4 %collective-permute-start.17 = (bf16[472,128]{1,0:T(8,128)(2,1)S(1)}, bf16[472,128]{1,0:T(8,128)(2,1)S(1)}, u32[]{:S(2)}, u32[]{:S(2)}) collective-permute-start(bf16[472,128]{1,0:T(8,128)(2,1)S(1)} %collective-permute-done.15.refs_1_), channel_id=1, source_target_pairs={{0,8},{1,9},{2,10},{3,11},{4,12},{5,13},{6,14},{7,15},{8,0},{9,1},... | collective-permute-start | bytes 362504 | tf_op jit(solution)/shard_map/ppermute | solution.py:301
  39.1 1.9 %collective-permute-start.14 = (bf16[472,128]{1,0:T(8,128)(2,1)S(1)}, bf16[472,128]{1,0:T(8,128)(2,1)S(1)}, u32[]{:S(2)}, u32[]{:S(2)}) collective-permute-start(bf16[472,128]{1,0:T(8,128)(2,1)S(1)} %collective-permute-done.13.refs_3_), channel_id=1, source_target_pairs={{0,8},{1,9},{2,10},{3,11},{4,12},{5,13},{6,14},{7,15},{8,0},{9,1},... | collective-permute-start | bytes 362504 | tf_op jit(solution)/shard_map/ppermute | solution.py:301
  39.8 1.3 %collective-permute-start.12 = (bf16[472,128]{1,0:T(8,128)(2,1)S(1)}, bf16[472,128]{1,0:T(8,128)(2,1)S(1)}, u32[]{:S(2)}, u32[]{:S(2)}) collective-permute-start(bf16[472,128]{1,0:T(8,128)(2,1)S(1)} %collective-permute-done.11.refs_2_), channel_id=1, source_target_pairs={{0,8},{1,9},{2,10},{3,11},{4,12},{5,13},{6,14},{7,15},{8,0},{9,1},... | collective-permute-start | bytes 362504 | tf_op jit(solution)/shard_map/ppermute | solution.py:301

commit v6 on v5

--- a/solution.py
+++ b/solution.py
@@ -248,8 +248,8 @@
             ref[2 * C1 :] = early.astype(kind)
 
 
-def spread_kernel(names, *refs):
-    wide_out, low_out, wide_ref, low_ref, sems = refs[-5:]
+def spread_kernel(names, whole, *refs):
+    wide_out, low_out, *whole_out, wide_ref, low_ref, sems = refs[-5 - whole :]
     copies = []
 
     def send(source, target):
@@ -264,31 +264,34 @@
         low_ref[k] = refs[k][2 * C1 :].astype(F32)
         at = pl.multiple_of(chunk * EARLY_ROWS, 8)
         send(low_ref.at[k], low_out.at[pl.ds(at, EARLY_ROWS), :])
+    for source, target in zip(refs[len(names) :], whole_out):
+        send(source, target)
     for copy in copies:
         copy.wait()
 
 
-def spread(chunks, names, into=()):
+def spread(chunks, names, into=(), whole=()):
     vmem = pl.BlockSpec(memory_space=pltpu.VMEM)
     hbm = pl.BlockSpec(memory_space=pltpu.HBM)
     count = len(names)
     return pl.pallas_call(
-        functools.partial(spread_kernel, names),
-        in_specs=[vmem] * count + [hbm] * len(into),
-        out_specs=[hbm] * 2,
+        functools.partial(spread_kernel, names, len(whole)),
+        in_specs=[vmem] * (count + len(whole)) + [hbm] * len(into),
+        out_specs=[hbm] * (2 + len(whole)),
         out_shape=[
             jax.ShapeDtypeStruct((8, C1, C2), F32),
             jax.ShapeDtypeStruct((27 * C0, C1), F32),
-        ],
+        ]
+        + [jax.ShapeDtypeStruct(value.shape, value.dtype) for value in whole],
         input_output_aliases={count: 0, count + 1: 1} if into else {},
         scratch_shapes=[
             pltpu.VMEM((count, C1, C2), F32),
             pltpu.VMEM((count, EARLY_ROWS, 128), F32),
-            pltpu.SemaphoreType.DMA((2 * count,)),
+            pltpu.SemaphoreType.DMA((2 * count + len(whole),)),
         ],
         compiler_params=pltpu.CompilerParams(vmem_limit_bytes=VMEM_BYTES),
         name="spread_sums",
-    )(*[chunks[k] for k in names], *into)
+    )(*[chunks[k] for k in names], *whole, *into)
 
 
 def swapped(value, flips):
@@ -419,10 +422,9 @@
         compiler_params=params,
         name="local_terms",
     )(*belows, early, *inner, cot)
-    sums, grads = total(chunks[:4], chunks[4:]), ()
-    for names in ((0, 3, 1, 2, 4, 7), (5, 6)):
-        grads = spread(sums, names, grads)
-    grad_deep, grad_early = grads
+    sums = total(chunks[:4], chunks[4:])
+    *grads, deep = spread(sums, (0, 3, 1, 2, 4, 7), whole=(deep,))
+    grad_deep, grad_early = spread(sums, (5, 6), grads)
     return (
         deep.reshape(1, DEPTH // 4, ROWS // 4, CELLS // 4 * C2),
         grad_deep.reshape(w_deep.shape),

time: 42.4 us -> 42.3 us (level)
  no operation moved by 1% of the time
where the time goes in v6:
time: 42.3 us; the launch traced here: 41.9 us
  starting transfers between devices  17.5 us (41%)
  waiting for transfers between devices  16.7 us (39%)
  Pallas kernels  5.91 us (14%)
  between operations  1.39 us (3%)
    ppermute x16, waiting for transfers between devices, swapped(): return lax.ppermute(value, ('sample', 'space'), pairs)  16 us
    ppermute x16, starting transfers between devices, swapped(): return lax.ppermute(value, ('sample', 'space'), pairs)  14.5 us
    ppermute x1, starting transfers between devices, neighbours_planes(): lax.ppermute(edge, ('sample', 'space'), list(zip(across[0], beside)))  3.03 us
    pallas_call x2, Pallas kernels, spread(): pl.pallas_call(functools.partial(spread_kernel, names, len(whole)), in_sp...  2.05 us
    pallas_call x1, Pallas kernels, body(): pl.pallas_call(inner_kernel, in_specs=[vmem] * 5 + [hbm], out_specs=[vmem...  1.61 us
    pallas_call x1, Pallas kernels, body(): pl.pallas_call(edge_kernel, in_specs=[hbm] * 5, out_specs=[vmem] * 5, out...  1.18 us
    pallas_call x1, Pallas kernels, body(): pl.pallas_call(local_kernel, in_specs=[vmem] * 9, out_specs=[vmem] * 9, o...  1.06 us
  transfers between devices with their start and end apart: 18, of which 11 were waited for; matrix products, arithmetic and copies ran while one was open for 0% of the time, Pallas kernels for 7%

profile of v6, /device:TPU:0, one launch (start us, length us, event | category | flops | bytes accessed | tf_op | source)
XLA Modules:
  0.0 41.9 jit_solution(14442180943923328434)
XLA Ops:
  0.6 1.2 %edge_plane.1 = (bf16[32,1024]{1,0:T(8,128)(2,1)S(1)}, s32[8,512]{1,0:T(8,128)S(1)}, f32[8,128]{1,0:T(8,128)S(1)}, bf16[9,192,128]{2,1,0:T(8,128)(2,1)S(1)}, bf16[16,1024]{1,0:T(8,128)(2,1)S(1)}) custom-call(bf16[8,32,1024]{2,1,0:T(8,128)(2,1)} %bitcast.11, s32[8,512]{1,0:T(8,128)} %bitcast.19, f32[8,128]{1,0:T(8,128)} %table_ref.1, ...), custom_call_target="tpu_custom_call" | custom-call | tf_op jit(solution)/shard_map/edge_plane/pallas_call | solution.py:361
  1.8 3.0 %collective-permute-start.1 = (bf16[32,1024]{1,0:T(8,128)(2,1)S(1)}, bf16[32,1024]{1,0:T(8,128)(2,1)S(1)}, u32[]{:S(2)}, u32[]{:S(2)}) collective-permute-start(bf16[32,1024]{1,0:T(8,128)(2,1)S(1)} %get-tuple-element.27), channel_id=1, source_target_pairs={{0,1},{1,0},{2,3},{3,2},{4,5},{5,4},{6,7},{7,6},{8,9},{9,8},{10,11... | collective-permute-start | bytes 196616 | tf_op jit(solution)/shard_map/ppermute | solution.py:346
  5.6 1.6 %inner_terms.1 = (bf16[3,64,1152]{2,1,0:T(8,128)(2,1)S(1)}, bf16[3,64,1152]{2,1,0:T(8,128)(2,1)S(1)}, f32[512,128]{1,0:T(8,128)S(1)}, bf16[8,128,256]{2,1,0:T(8,128)(2,1)S(1)}, f32[512,128]{1,0:T(8,128)S(1)}) custom-call(bf16[8,32,1024]{2,1,0:T(8,128)(2,1)S(1)} %bitcast.12, s32[8,512]{1,0:T(8,128)S(1)} %get-tuple-element.29.opens_ref, ...), custom_call_target="tpu_custom_call" | custom-call | tf_op jit(solution)/shard_map/inner_terms/pallas_call | solution.py:386
  7.2 0.7 %collective-permute-done.1.beside_ref = bf16[32,1024]{1,0:T(8,128)(2,1)S(1)} collective-permute-done((bf16[32,1024]{1,0:T(8,128)(2,1)S(1)}, bf16[32,1024]{1,0:T(8,128)(2,1)S(1)}, u32[]{:S(2)}, u32[]{:S(2)}) %collective-permute-start.1) | collective-permute-done | bytes 65568 | tf_op jit(solution)/shard_map/ppermute | solution.py:346
  8.0 1.1 %local_terms.1 = (bf16[16,1024]{1,0:T(8,128)(2,1)S(1)}, f32[472,128]{1,0:T(8,128)S(1)}, f32[472,128]{1,0:T(8,128)S(1)}, f32[472,128]{1,0:T(8,128)S(1)}, f32[472,...) custom-call(bf16[32,1024]{1,0:T(8,128)(2,1)S(1)} %collective-permute, ...), custom_call_target="tpu_custom_call" | custom-call | tf_op jit(solution)/shard_map/local_terms/pallas_call | solution.py:408
  9.1 0.5 %collective-permute-start.2 = (bf16[472,128]{1,0:T(8,128)(2,1)S(1)}, bf16[472,128]{1,0:T(8,128)(2,1)S(1)}, u32[]{:S(2)}, u32[]{:S(2)}) collective-permute-start(bf16[472,128]{1,0:T(8,128)(2,1)S(1)} %get-tuple-element.38), channel_id=1, source_target_pairs={{0,8},{1,9},{2,10},{3,11},{4,12},{5,13},{6,14},{7,15},{8,0},{9,1},... | collective-permute-start | bytes 362504 | tf_op jit(solution)/shard_map/ppermute | solution.py:304
  9.7 0.4 %collective-permute-start.7 = (bf16[472,128]{1,0:T(8,128)(2,1)S(1)}, bf16[472,128]{1,0:T(8,128)(2,1)S(1)}, u32[]{:S(2)}, u32[]{:S(2)}) collective-permute-start(bf16[472,128]{1,0:T(8,128)(2,1)S(1)} %get-tuple-element.44), channel_id=1, source_target_pairs={{0,8},{1,9},{2,10},{3,11},{4,12},{5,13},{6,14},{7,15},{8,0},{9,1},... | collective-permute-start | bytes 362504 | tf_op jit(solution)/shard_map/ppermute | solution.py:304
  10.5 2.5 %collective-permute-start.4 = (bf16[472,128]{1,0:T(8,128)(2,1)S(1)}, bf16[472,128]{1,0:T(8,128)(2,1)S(1)}, u32[]{:S(2)}, u32[]{:S(2)}) collective-permute-start(bf16[472,128]{1,0:T(8,128)(2,1)S(1)} %add_convert_fusion.5), channel_id=1, source_target_pairs={{0,1},{1,0},{2,3},{3,2},{4,5},{5,4},{6,7},{7,6},{8,24},{9,25},{10,... | collective-permute-start | bytes 362504 | tf_op jit(solution)/shard_map/ppermute | solution.py:304
  13.0 1.7 %collective-permute-start.6 = (bf16[472,128]{1,0:T(8,128)(2,1)S(1)}, bf16[472,128]{1,0:T(8,128)(2,1)S(1)}, u32[]{:S(2)}, u32[]{:S(2)}) collective-permute-start(bf16[472,128]{1,0:T(8,128)(2,1)S(1)} %add_convert_fusion.4), channel_id=1, source_target_pairs={{0,16},{1,17},{2,18},{3,19},{4,20},{5,21},{6,22},{7,23},{8,9},{9,8... | collective-permute-start | bytes 362504 | tf_op jit(solution)/shard_map/ppermute | solution.py:304
  15.1 1.2 %collective-permute-done.4 = bf16[472,128]{1,0:T(8,128)(2,1)S(1)} collective-permute-done((bf16[472,128]{1,0:T(8,128)(2,1)S(1)}, bf16[472,128]{1,0:T(8,128)(2,1)S(1)}, u32[]{:S(2)}, u32[]{:S(2)}) %collective-permute-start.4) | collective-permute-done | bytes 120864 | tf_op jit(solution)/shard_map/ppermute | solution.py:304
  16.2 2.9 %collective-permute-done.6 = bf16[472,128]{1,0:T(8,128)(2,1)S(1)} collective-permute-done((bf16[472,128]{1,0:T(8,128)(2,1)S(1)}, bf16[472,128]{1,0:T(8,128)(2,1)S(1)}, u32[]{:S(2)}, u32[]{:S(2)}) %collective-permute-start.6) | collective-permute-done | bytes 120864 | tf_op jit(solution)/shard_map/ppermute | solution.py:304
  19.2 1.4 %collective-permute-done.8 = bf16[472,128]{1,0:T(8,128)(2,1)S(1)} collective-permute-done((bf16[472,128]{1,0:T(8,128)(2,1)S(1)}, bf16[472,128]{1,0:T(8,128)(2,1)S(1)}, u32[]{:S(2)}, u32[]{:S(2)}) %collective-permute-start.8) | collective-permute-done | bytes 120864 | tf_op jit(solution)/shard_map/ppermute | solution.py:304
  20.7 2.7 %collective-permute-start.9 = (bf16[472,128]{1,0:T(8,128)(2,1)S(1)}, bf16[472,128]{1,0:T(8,128)(2,1)S(1)}, u32[]{:S(2)}, u32[]{:S(2)}) collective-permute-start(bf16[472,128]{1,0:T(8,128)(2,1)S(1)} %add_convert_fusion.2), channel_id=1, source_target_pairs={{0,2},{1,3},{2,0},{3,1},{4,6},{5,7},{6,4},{7,5},{8,12},{9,13},{10,... | collective-permute-start | bytes 362504 | tf_op jit(solution)/shard_map/ppermute | solution.py:304
  23.4 3.3 %collective-permute-done.9 = bf16[472,128]{1,0:T(8,128)(2,1)S(1)} collective-permute-done((bf16[472,128]{1,0:T(8,128)(2,1)S(1)}, bf16[472,128]{1,0:T(8,128)(2,1)S(1)}, u32[]{:S(2)}, u32[]{:S(2)}) %collective-permute-start.9) | collective-permute-done | bytes 120864 | tf_op jit(solution)/shard_map/ppermute | solution.py:304
  26.7 2.6 %collective-permute-start.10 = (bf16[472,128]{1,0:T(8,128)(2,1)S(1)}, bf16[472,128]{1,0:T(8,128)(2,1)S(1)}, u32[]{:S(2)}, u32[]{:S(2)}) collective-permute-start(bf16[472,128]{1,0:T(8,128)(2,1)S(1)} %add_convert_fusion.1), channel_id=1, source_target_pairs={{0,4},{1,5},{2,6},{3,7},{4,0},{5,1},{6,2},{7,3},{8,10},{9,11},{10,... | collective-permute-start | bytes 362504 | tf_op jit(solution)/shard_map/ppermute | solution.py:304
  29.3 3.2 %collective-permute-done.10 = bf16[472,128]{1,0:T(8,128)(2,1)S(1)} collective-permute-done((bf16[472,128]{1,0:T(8,128)(2,1)S(1)}, bf16[472,128]{1,0:T(8,128)(2,1)S(1)}, u32[]{:S(2)}, u32[]{:S(2)}) %collective-permute-start.10) | collective-permute-done | bytes 120864 | tf_op jit(solution)/shard_map/ppermute | solution.py:304
  32.6 1.6 %collective-permute-start.11 = (bf16[472,128]{1,0:T(8,128)(2,1)S(1)}, bf16[472,128]{1,0:T(8,128)(2,1)S(1)}, u32[]{:S(2)}, u32[]{:S(2)}) collective-permute-start(bf16[472,128]{1,0:T(8,128)(2,1)S(1)} %add_convert_fusion.refs_0_), channel_id=1, source_target_pairs={{0,17},{1,16},{2,19},{3,18},{4,21},{5,20},{6,23},{7,22},{8,25},{9,... | collective-permute-start | bytes 362504 | tf_op jit(solution)/shard_map/ppermute | solution.py:304
  34.2 0.7 %collective-permute-start.13 = (bf16[472,128]{1,0:T(8,128)(2,1)S(1)}, bf16[472,128]{1,0:T(8,128)(2,1)S(1)}, u32[]{:S(2)}, u32[]{:S(2)}) collective-permute-start(bf16[472,128]{1,0:T(8,128)(2,1)S(1)} %add_convert_fusion.refs_0_), channel_id=1, source_target_pairs={{0,16},{1,17},{2,18},{3,19},{4,20},{5,21},{6,22},{7,23},{8,9},{9,8... | collective-permute-start | bytes 362504 | tf_op jit(solution)/shard_map/ppermute | solution.py:304
  34.9 1.2 %collective-permute-start.12 = (bf16[472,128]{1,0:T(8,128)(2,1)S(1)}, bf16[472,128]{1,0:T(8,128)(2,1)S(1)}, u32[]{:S(2)}, u32[]{:S(2)}) collective-permute-start(bf16[472,128]{1,0:T(8,128)(2,1)S(1)} %add_convert_fusion.refs_0_), channel_id=1, source_target_pairs={{0,1},{1,0},{2,3},{3,2},{4,5},{5,4},{6,7},{7,6},{8,24},{9,25},{10,... | collective-permute-start | bytes 362504 | tf_op jit(solution)/shard_map/ppermute | solution.py:304
  36.1 2.3 %collective-permute-done.11.refs_1_ = bf16[472,128]{1,0:T(8,128)(2,1)S(1)} collective-permute-done((bf16[472,128]{1,0:T(8,128)(2,1)S(1)}, bf16[472,128]{1,0:T(8,128)(2,1)S(1)}, u32[]{:S(2)}, u32[]{:S(2)}) %collective-permute-start.11) | collective-permute-done | bytes 120864 | tf_op jit(solution)/shard_map/ppermute | solution.py:304
  38.4 0.7 %collective-permute-done.13.refs_3_ = bf16[472,128]{1,0:T(8,128)(2,1)S(1)} collective-permute-done((bf16[472,128]{1,0:T(8,128)(2,1)S(1)}, bf16[472,128]{1,0:T(8,128)(2,1)S(1)}, u32[]{:S(2)}, u32[]{:S(2)}) %collective-permute-start.13) | collective-permute-done | bytes 120864 | tf_op jit(solution)/shard_map/ppermute | solution.py:304
  39.1 0.7 %collective-permute-done.12.refs_2_ = bf16[472,128]{1,0:T(8,128)(2,1)S(1)} collective-permute-done((bf16[472,128]{1,0:T(8,128)(2,1)S(1)}, bf16[472,128]{1,0:T(8,128)(2,1)S(1)}, u32[]{:S(2)}, u32[]{:S(2)}) %collective-permute-start.12) | collective-permute-done | bytes 120864 | tf_op jit(solution)/shard_map/ppermute | solution.py:304
  39.8 1.2 %spread_sums.2 = (f32[8,128,256]{2,1,0:T(8,128)}, f32[1728,128]{1,0:T(8,128)}, bf16[16,1024]{1,0:T(8,128)(2,1)}) custom-call(bf16[472,128]{1,0:T(8,128)(2,1)S(1)} %add_convert_fusion.refs_0_, bf16[472,128]{1,0:T(8,128)(2,1)S(1)} %collective-permute-done.11.refs_1_, bf16[472,128]{1,0:T(8,128)(2,1)S(1)} %collective-permute-done.12.refs_2_, ...), custom_call_target="tpu_custom_call" | custom-call | tf_op jit(solution)/shard_map/spread_sums/pallas_call | solution.py:277
  41.1 0.8 %spread_sums.3 = (f32[8,128,256]{2,1,0:T(8,128)}, f32[1728,128]{1,0:T(8,128)}) custom-call(bf16[472,128]{1,0:T(8,128)(2,1)S(1)} %collective-permute-done.16.refs_0_, bf16[472,128]{1,0:T(8,128)(2,1)S(1)} %collective-permute-done.17.refs_1_, f32[8,128,256]{2,1,0:T(8,128)} %get-tuple-element.47.refs_2_, ...), custom_call_target="tpu_custom_call", output_to_operand_aliasing={{0}: (2, {}), {1}: (3, {})} | custom-call | tf_op jit(solution)/shard_map/spread_sums/pallas_call | solution.py:277
  (27 shorter events, 1.2 us)
Async XLA Ops:
  0.6 5.0 %copy-start = (bf16[1,8,32,1024]{3,2,1,0:T(8,128)(2,1)S(1)}, bf16[1,8,32,1024]{3,2,1,0:T(8,128)(2,1)}, u32[]{:S(2)}) copy-start(bf16[1,8,32,1024]{3,2,1,0:T(8,128)(2,1)} %param.7) | copy-start | bytes 1572868
  1.8 6.1 %collective-permute-start.1 = (bf16[32,1024]{1,0:T(8,128)(2,1)S(1)}, bf16[32,1024]{1,0:T(8,128)(2,1)S(1)}, u32[]{:S(2)}, u32[]{:S(2)}) collective-permute-start(bf16[32,1024]{1,0:T(8,128)(2,1)S(1)} %get-tuple-element.27), channel_id=1, source_target_pairs={{0,1},{1,0},{2,3},{3,2},{4,5},{5,4},{6,7},{7,6},{8,9},{9,8},{10,11... | collective-permute-start | bytes 196616 | tf_op jit(solution)/shard_map/ppermute | solution.py:346
  4.9 3.1 %collective-permute-start = (bf16[32,1024]{1,0:T(8,128)(2,1)S(1)}, bf16[32,1024]{1,0:T(8,128)(2,1)S(1)}, u32[]{:S(2)}, u32[]{:S(2)}) collective-permute-start(bf16[32,1024]{1,0:T(8,128)(2,1)S(1)} %get-tuple-element.27), channel_id=1, source_target_pairs={{0,8},{1,2},{2,1},{3,4},{4,3},{5,6},{6,5},{7,15},{8,0},{9,10},{10,... | collective-permute-start | bytes 196616 | tf_op jit(solution)/shard_map/ppermute | solution.py:345
  9.0 1.4 %collective-permute-start.3 = (bf16[472,128]{1,0:T(8,128)(2,1)S(1)}, bf16[472,128]{1,0:T(8,128)(2,1)S(1)}, u32[]{:S(2)}, u32[]{:S(2)}) collective-permute-start(bf16[472,128]{1,0:T(8,128)(2,1)S(1)} %get-tuple-element.40), channel_id=1, source_target_pairs={{0,8},{1,9},{2,10},{3,11},{4,12},{5,13},{6,14},{7,15},{8,0},{9,1},... | collective-permute-start | bytes 362504 | tf_op jit(solution)/shard_map/ppermute | solution.py:304
  9.1 6.0 %collective-permute-start.2 = (bf16[472,128]{1,0:T(8,128)(2,1)S(1)}, bf16[472,128]{1,0:T(8,128)(2,1)S(1)}, u32[]{:S(2)}, u32[]{:S(2)}) collective-permute-start(bf16[472,128]{1,0:T(8,128)(2,1)S(1)} %get-tuple-element.38), channel_id=1, source_target_pairs={{0,8},{1,9},{2,10},{3,11},{4,12},{5,13},{6,14},{7,15},{8,0},{9,1},... | collective-permute-start | bytes 362504 | tf_op jit(solution)/shard_map/ppermute | solution.py:304
  9.6 3.4 %collective-permute-start.5 = (bf16[472,128]{1,0:T(8,128)(2,1)S(1)}, bf16[472,128]{1,0:T(8,128)(2,1)S(1)}, u32[]{:S(2)}, u32[]{:S(2)}) collective-permute-start(bf16[472,128]{1,0:T(8,128)(2,1)S(1)} %get-tuple-element.42), channel_id=1, source_target_pairs={{0,8},{1,9},{2,10},{3,11},{4,12},{5,13},{6,14},{7,15},{8,0},{9,1},... | collective-permute-start | bytes 362504 | tf_op jit(solution)/shard_map/ppermute | solution.py:304
  9.7 5.0 %collective-permute-start.7 = (bf16[472,128]{1,0:T(8,128)(2,1)S(1)}, bf16[472,128]{1,0:T(8,128)(2,1)S(1)}, u32[]{:S(2)}, u32[]{:S(2)}) collective-permute-start(bf16[472,128]{1,0:T(8,128)(2,1)S(1)} %get-tuple-element.44), channel_id=1, source_target_pairs={{0,8},{1,9},{2,10},{3,11},{4,12},{5,13},{6,14},{7,15},{8,0},{9,1},... | collective-permute-start | bytes 362504 | tf_op jit(solution)/shard_map/ppermute | solution.py:304
  10.5 5.8 %collective-permute-start.4 = (bf16[472,128]{1,0:T(8,128)(2,1)S(1)}, bf16[472,128]{1,0:T(8,128)(2,1)S(1)}, u32[]{:S(2)}, u32[]{:S(2)}) collective-permute-start(bf16[472,128]{1,0:T(8,128)(2,1)S(1)} %add_convert_fusion.5), channel_id=1, source_target_pairs={{0,1},{1,0},{2,3},{3,2},{4,5},{5,4},{6,7},{7,6},{8,24},{9,25},{10,... | collective-permute-start | bytes 362504 | tf_op jit(solution)/shard_map/ppermute | solution.py:304
  13.0 6.1 %collective-permute-start.6 = (bf16[472,128]{1,0:T(8,128)(2,1)S(1)}, bf16[472,128]{1,0:T(8,128)(2,1)S(1)}, u32[]{:S(2)}, u32[]{:S(2)}) collective-permute-start(bf16[472,128]{1,0:T(8,128)(2,1)S(1)} %add_convert_fusion.4), channel_id=1, source_target_pairs={{0,16},{1,17},{2,18},{3,19},{4,20},{5,21},{6,22},{7,23},{8,9},{9,8... | collective-permute-start | bytes 362504 | tf_op jit(solution)/shard_map/ppermute | solution.py:304
  14.7 5.8 %collective-permute-start.8 = (bf16[472,128]{1,0:T(8,128)(2,1)S(1)}, bf16[472,128]{1,0:T(8,128)(2,1)S(1)}, u32[]{:S(2)}, u32[]{:S(2)}) collective-permute-start(bf16[472,128]{1,0:T(8,128)(2,1)S(1)} %add_convert_fusion.3), channel_id=1, source_target_pairs={{0,17},{1,16},{2,19},{3,18},{4,21},{5,20},{6,23},{7,22},{8,25},{9,... | collective-permute-start | bytes 362504 | tf_op jit(solution)/shard_map/ppermute | solution.py:304
  20.7 6.0 %collective-permute-start.9 = (bf16[472,128]{1,0:T(8,128)(2,1)S(1)}, bf16[472,128]{1,0:T(8,128)(2,1)S(1)}, u32[]{:S(2)}, u32[]{:S(2)}) collective-permute-start(bf16[472,128]{1,0:T(8,128)(2,1)S(1)} %add_convert_fusion.2), channel_id=1, source_target_pairs={{0,2},{1,3},{2,0},{3,1},{4,6},{5,7},{6,4},{7,5},{8,12},{9,13},{10,... | collective-permute-start | bytes 362504 | tf_op jit(solution)/shard_map/ppermute | solution.py:304
  26.7 5.8 %collective-permute-start.10 = (bf16[472,128]{1,0:T(8,128)(2,1)S(1)}, bf16[472,128]{1,0:T(8,128)(2,1)S(1)}, u32[]{:S(2)}, u32[]{:S(2)}) collective-permute-start(bf16[472,128]{1,0:T(8,128)(2,1)S(1)} %add_convert_fusion.1), channel_id=1, source_target_pairs={{0,4},{1,5},{2,6},{3,7},{4,0},{5,1},{6,2},{7,3},{8,10},{9,11},{10,... | collective-permute-start | bytes 362504 | tf_op jit(solution)/shard_map/ppermute | solution.py:304
  32.6 5.8 %collective-permute-start.11 = (bf16[472,128]{1,0:T(8,128)(2,1)S(1)}, bf16[472,128]{1,0:T(8,128)(2,1)S(1)}, u32[]{:S(2)}, u32[]{:S(2)}) collective-permute-start(bf16[472,128]{1,0:T(8,128)(2,1)S(1)} %add_convert_fusion.refs_0_), channel_id=1, source_target_pairs={{0,17},{1,16},{2,19},{3,18},{4,21},{5,20},{6,23},{7,22},{8,25},{9,... | collective-permute-start | bytes 362504 | tf_op jit(solution)/shard_map/ppermute | solution.py:304
  34.2 4.9 %collective-permute-start.13 = (bf16[472,128]{1,0:T(8,128)(2,1)S(1)}, bf16[472,128]{1,0:T(8,128)(2,1)S(1)}, u32[]{:S(2)}, u32[]{:S(2)}) collective-permute-start(bf16[472,128]{1,0:T(8,128)(2,1)S(1)} %add_convert_fusion.refs_0_), channel_id=1, source_target_pairs={{0,16},{1,17},{2,18},{3,19},{4,20},{5,21},{6,22},{7,23},{8,9},{9,8... | collective-permute-start | bytes 362504 | tf_op jit(solution)/shard_map/ppermute | solution.py:304
  34.9 4.9 %collective-permute-start.12 = (bf16[472,128]{1,0:T(8,128)(2,1)S(1)}, bf16[472,128]{1,0:T(8,128)(2,1)S(1)}, u32[]{:S(2)}, u32[]{:S(2)}) collective-permute-start(bf16[472,128]{1,0:T(8,128)(2,1)S(1)} %add_convert_fusion.refs_0_), channel_id=1, source_target_pairs={{0,1},{1,0},{2,3},{3,2},{4,5},{5,4},{6,7},{7,6},{8,24},{9,25},{10,... | collective-permute-start | bytes 362504 | tf_op jit(solution)/shard_map/ppermute | solution.py:304
  36.1 3.6 %collective-permute-start.14 = (bf16[472,128]{1,0:T(8,128)(2,1)S(1)}, bf16[472,128]{1,0:T(8,128)(2,1)S(1)}, u32[]{:S(2)}, u32[]{:S(2)}) collective-permute-start(bf16[472,128]{1,0:T(8,128)(2,1)S(1)} %add_convert_fusion.refs_0_), channel_id=1, source_target_pairs={{0,8},{1,9},{2,10},{3,11},{4,12},{5,13},{6,14},{7,15},{8,0},{9,1},... | collective-permute-start | bytes 362504 | tf_op jit(solution)/shard_map/ppermute | solution.py:304
  38.4 1.4 %collective-permute-start.15 = (bf16[472,128]{1,0:T(8,128)(2,1)S(1)}, bf16[472,128]{1,0:T(8,128)(2,1)S(1)}, u32[]{:S(2)}, u32[]{:S(2)}) collective-permute-start(bf16[472,128]{1,0:T(8,128)(2,1)S(1)} %collective-permute-done.11.refs_1_), channel_id=1, source_target_pairs={{0,8},{1,9},{2,10},{3,11},{4,12},{5,13},{6,14},{7,15},{8,0},{9,1},... | collective-permute-start | bytes 362504 | tf_op jit(solution)/shard_map/ppermute | solution.py:304
  39.1 1.9 %collective-permute-start.17 = (bf16[472,128]{1,0:T(8,128)(2,1)S(1)}, bf16[472,128]{1,0:T(8,128)(2,1)S(1)}, u32[]{:S(2)}, u32[]{:S(2)}) collective-permute-start(bf16[472,128]{1,0:T(8,128)(2,1)S(1)} %collective-permute-done.13.refs_3_), channel_id=1, source_target_pairs={{0,8},{1,9},{2,10},{3,11},{4,12},{5,13},{6,14},{7,15},{8,0},{9,1},... | collective-permute-start | bytes 362504 | tf_op jit(solution)/shard_map/ppermute | solution.py:304
  39.7 1.3 %collective-permute-start.16 = (bf16[472,128]{1,0:T(8,128)(2,1)S(1)}, bf16[472,128]{1,0:T(8,128)(2,1)S(1)}, u32[]{:S(2)}, u32[]{:S(2)}) collective-permute-start(bf16[472,128]{1,0:T(8,128)(2,1)S(1)} %collective-permute-done.12.refs_2_), channel_id=1, source_target_pairs={{0,8},{1,9},{2,10},{3,11},{4,12},{5,13},{6,14},{7,15},{8,0},{9,1},... | collective-permute-start | bytes 362504 | tf_op jit(solution)/shard_map/ppermute | solution.py:304

commit v7 on v6

--- a/solution.py
+++ b/solution.py
@@ -25,23 +25,27 @@
     return lax.broadcasted_iota(jnp.int32, shape, dim)
 
 
-def open_rows(opens):
-    planes = opens.shape[0]
+def mask_tables():
     cells = ROWS * CELLS
     own = (iota((ROWS, cells), 1) // CELLS) == iota((ROWS, cells), 0)
+    pick = ((iota((cells, 128), 0) % CELLS) == iota((cells, 128), 1)).astype(F32).astype(BF16)
+    widen = (iota((128, WIDE), 0) == (iota((128, WIDE), 1) // C0)).astype(F32).astype(BF16)
+    return own, pick, widen
+
+
+def open_rows(opens, tables):
+    own, pick, widen = tables
     spread = jnp.concatenate(
-        [jnp.where(own, opens[z : z + 1, :], 0).astype(F32).astype(BF16) for z in range(planes)], axis=0
-    )
-    pick = ((iota((cells, 128), 0) % CELLS) == iota((cells, 128), 1)).astype(F32).astype(BF16)
+        [jnp.where(own, opens[z : z + 1, :], 0).astype(F32).astype(BF16) for z in range(opens.shape[0])], axis=0
+    )
     by_cell = jnp.dot(spread, pick, preferred_element_type=F32).astype(BF16)
-    widen = (iota((128, WIDE), 0) == (iota((128, WIDE), 1) // C0)).astype(F32).astype(BF16)
     return jnp.dot(by_cell, widen, preferred_element_type=F32).astype(BF16)
 
 
 def edge_kernel(
     acts_ref, opens_ref, table_ref, w1_hbm, cot_hbm,
     edge_ref, cells_ref, bias_ref, w1_ref, cot_ref,
-    plane_ref, sems,
+    plane_ref, pick_ref, widen_ref, sems,
 ):
     plane = pltpu.make_async_copy(acts_ref.at[DEPTH - 1], plane_ref, sems.at[0])
     cells = pltpu.make_async_copy(opens_ref, cells_ref, sems.at[1])
@@ -53,8 +57,9 @@
     early.start()
     cot = pltpu.make_async_copy(cot_hbm, cot_ref, sems.at[4])
     cot.start()
+    pick_ref[...], widen_ref[...] = mask_tables()[1:]
     cells.wait()
-    mask = open_rows(cells_ref[DEPTH - 1 :])
+    mask = open_rows(cells_ref[DEPTH - 1 :], (mask_tables()[0], pick_ref[...], widen_ref[...]))
     plane.wait()
     edge_ref[...] = plane_ref[...] * mask
     table.wait()
@@ -140,7 +145,7 @@
 ):
     fetch = pltpu.make_async_copy(w2_hbm, w2_ref, sem)
     fetch.start()
-    field = acts_ref[...].reshape(DEPTH * ROWS, WIDE) * open_rows(opens_ref[...])
+    field = acts_ref[...].reshape(DEPTH * ROWS, WIDE) * open_rows(opens_ref[...], mask_tables())
     half = 3 * 64
     r = iota((2 * half, DEPTH * ROWS), 0)
     par = (r >= half).astype(jnp.int32)
@@ -369,7 +374,12 @@
             jax.ShapeDtypeStruct((9, 3 * C0, C1), BF16),
             jax.ShapeDtypeStruct(flat_cot.shape, BF16),
         ],
-        scratch_shapes=[pltpu.VMEM((ROWS, WIDE), BF16), pltpu.SemaphoreType.DMA((5,))],
+        scratch_shapes=[
+            pltpu.VMEM((ROWS, WIDE), BF16),
+            pltpu.VMEM((ROWS * CELLS, 128), BF16),
+            pltpu.VMEM((128, WIDE), BF16),
+            pltpu.SemaphoreType.DMA((5,)),
+        ],
         compiler_params=params,
         name="edge_plane",
     )(

time: 42.3 us -> 42.3 us (level)
  no operation moved by 1% of the time
where the time goes in v7:
time: 42.3 us; the launch traced here: 41.9 us
  starting transfers between devices  17.5 us (41%)
  waiting for transfers between devices  16.7 us (39%)
  Pallas kernels  5.91 us (14%)
  between operations  1.39 us (3%)
    ppermute x16, waiting for transfers between devices, swapped(): return lax.ppermute(value, ('sample', 'space'), pairs)  16 us
    ppermute x16, starting transfers between devices, swapped(): return lax.ppermute(value, ('sample', 'space'), pairs)  14.5 us
    ppermute x1, starting transfers between devices, neighbours_planes(): lax.ppermute(edge, ('sample', 'space'), list(zip(across[0], beside)))  3.03 us
    pallas_call x2, Pallas kernels, spread(): pl.pallas_call(functools.partial(spread_kernel, names, len(whole)), in_sp...  2.05 us
    pallas_call x1, Pallas kernels, body(): pl.pallas_call(inner_kernel, in_specs=[vmem] * 5 + [hbm], out_specs=[vmem...  1.61 us
    pallas_call x1, Pallas kernels, body(): pl.pallas_call(edge_kernel, in_specs=[hbm] * 5, out_specs=[vmem] * 5, out...  1.18 us
    pallas_call x1, Pallas kernels, body(): pl.pallas_call(local_kernel, in_specs=[vmem] * 9, out_specs=[vmem] * 9, o...  1.06 us
  transfers between devices with their start and end apart: 18, of which 11 were waited for; matrix products, arithmetic and copies ran while one was open for 0% of the time, Pallas kernels for 7%

profile of v7, /device:TPU:0, one launch (start us, length us, event | category | flops | bytes accessed | tf_op | source)
XLA Modules:
  0.0 41.9 jit_solution(3881604831222724386)
XLA Ops:
  0.6 1.2 %edge_plane.1 = (bf16[32,1024]{1,0:T(8,128)(2,1)S(1)}, s32[8,512]{1,0:T(8,128)S(1)}, f32[8,128]{1,0:T(8,128)S(1)}, bf16[9,192,128]{2,1,0:T(8,128)(2,1)S(1)}, bf16[16,1024]{1,0:T(8,128)(2,1)S(1)}) custom-call(bf16[8,32,1024]{2,1,0:T(8,128)(2,1)} %bitcast.11, s32[8,512]{1,0:T(8,128)} %bitcast.19, f32[8,128]{1,0:T(8,128)} %table_ref.1, ...), custom_call_target="tpu_custom_call" | custom-call | tf_op jit(solution)/shard_map/edge_plane/pallas_call | solution.py:366
  1.8 3.0 %collective-permute-start.1 = (bf16[32,1024]{1,0:T(8,128)(2,1)S(1)}, bf16[32,1024]{1,0:T(8,128)(2,1)S(1)}, u32[]{:S(2)}, u32[]{:S(2)}) collective-permute-start(bf16[32,1024]{1,0:T(8,128)(2,1)S(1)} %get-tuple-element.27), channel_id=1, source_target_pairs={{0,1},{1,0},{2,3},{3,2},{4,5},{5,4},{6,7},{7,6},{8,9},{9,8},{10,11... | collective-permute-start | bytes 196616 | tf_op jit(solution)/shard_map/ppermute | solution.py:351
  5.6 1.6 %inner_terms.1 = (bf16[3,64,1152]{2,1,0:T(8,128)(2,1)S(1)}, bf16[3,64,1152]{2,1,0:T(8,128)(2,1)S(1)}, f32[512,128]{1,0:T(8,128)S(1)}, bf16[8,128,256]{2,1,0:T(8,128)(2,1)S(1)}, f32[512,128]{1,0:T(8,128)S(1)}) custom-call(bf16[8,32,1024]{2,1,0:T(8,128)(2,1)S(1)} %bitcast.12, s32[8,512]{1,0:T(8,128)S(1)} %get-tuple-element.29.opens_ref, ...), custom_call_target="tpu_custom_call" | custom-call | tf_op jit(solution)/shard_map/inner_terms/pallas_call | solution.py:396
  7.2 0.7 %collective-permute-done.1.beside_ref = bf16[32,1024]{1,0:T(8,128)(2,1)S(1)} collective-permute-done((bf16[32,1024]{1,0:T(8,128)(2,1)S(1)}, bf16[32,1024]{1,0:T(8,128)(2,1)S(1)}, u32[]{:S(2)}, u32[]{:S(2)}) %collective-permute-start.1) | collective-permute-done | bytes 65568 | tf_op jit(solution)/shard_map/ppermute | solution.py:351
  8.0 1.1 %local_terms.1 = (bf16[16,1024]{1,0:T(8,128)(2,1)S(1)}, f32[472,128]{1,0:T(8,128)S(1)}, f32[472,128]{1,0:T(8,128)S(1)}, f32[472,128]{1,0:T(8,128)S(1)}, f32[472,...) custom-call(bf16[32,1024]{1,0:T(8,128)(2,1)S(1)} %collective-permute, ...), custom_call_target="tpu_custom_call" | custom-call | tf_op jit(solution)/shard_map/local_terms/pallas_call | solution.py:418
  9.1 0.5 %collective-permute-start.2 = (bf16[472,128]{1,0:T(8,128)(2,1)S(1)}, bf16[472,128]{1,0:T(8,128)(2,1)S(1)}, u32[]{:S(2)}, u32[]{:S(2)}) collective-permute-start(bf16[472,128]{1,0:T(8,128)(2,1)S(1)} %get-tuple-element.38), channel_id=1, source_target_pairs={{0,8},{1,9},{2,10},{3,11},{4,12},{5,13},{6,14},{7,15},{8,0},{9,1},... | collective-permute-start | bytes 362504 | tf_op jit(solution)/shard_map/ppermute | solution.py:309
  9.7 0.4 %collective-permute-start.7 = (bf16[472,128]{1,0:T(8,128)(2,1)S(1)}, bf16[472,128]{1,0:T(8,128)(2,1)S(1)}, u32[]{:S(2)}, u32[]{:S(2)}) collective-permute-start(bf16[472,128]{1,0:T(8,128)(2,1)S(1)} %get-tuple-element.44), channel_id=1, source_target_pairs={{0,8},{1,9},{2,10},{3,11},{4,12},{5,13},{6,14},{7,15},{8,0},{9,1},... | collective-permute-start | bytes 362504 | tf_op jit(solution)/shard_map/ppermute | solution.py:309
  10.5 2.5 %collective-permute-start.4 = (bf16[472,128]{1,0:T(8,128)(2,1)S(1)}, bf16[472,128]{1,0:T(8,128)(2,1)S(1)}, u32[]{:S(2)}, u32[]{:S(2)}) collective-permute-start(bf16[472,128]{1,0:T(8,128)(2,1)S(1)} %add_convert_fusion.5), channel_id=1, source_target_pairs={{0,1},{1,0},{2,3},{3,2},{4,5},{5,4},{6,7},{7,6},{8,24},{9,25},{10,... | collective-permute-start | bytes 362504 | tf_op jit(solution)/shard_map/ppermute | solution.py:309
  13.0 1.7 %collective-permute-start.6 = (bf16[472,128]{1,0:T(8,128)(2,1)S(1)}, bf16[472,128]{1,0:T(8,128)(2,1)S(1)}, u32[]{:S(2)}, u32[]{:S(2)}) collective-permute-start(bf16[472,128]{1,0:T(8,128)(2,1)S(1)} %add_convert_fusion.4), channel_id=1, source_target_pairs={{0,16},{1,17},{2,18},{3,19},{4,20},{5,21},{6,22},{7,23},{8,9},{9,8... | collective-permute-start | bytes 362504 | tf_op jit(solution)/shard_map/ppermute | solution.py:309
  15.1 1.2 %collective-permute-done.4 = bf16[472,128]{1,0:T(8,128)(2,1)S(1)} collective-permute-done((bf16[472,128]{1,0:T(8,128)(2,1)S(1)}, bf16[472,128]{1,0:T(8,128)(2,1)S(1)}, u32[]{:S(2)}, u32[]{:S(2)}) %collective-permute-start.4) | collective-permute-done | bytes 120864 | tf_op jit(solution)/shard_map/ppermute | solution.py:309
  16.2 2.9 %collective-permute-done.6 = bf16[472,128]{1,0:T(8,128)(2,1)S(1)} collective-permute-done((bf16[472,128]{1,0:T(8,128)(2,1)S(1)}, bf16[472,128]{1,0:T(8,128)(2,1)S(1)}, u32[]{:S(2)}, u32[]{:S(2)}) %collective-permute-start.6) | collective-permute-done | bytes 120864 | tf_op jit(solution)/shard_map/ppermute | solution.py:309
  19.2 1.4 %collective-permute-done.8 = bf16[472,128]{1,0:T(8,128)(2,1)S(1)} collective-permute-done((bf16[472,128]{1,0:T(8,128)(2,1)S(1)}, bf16[472,128]{1,0:T(8,128)(2,1)S(1)}, u32[]{:S(2)}, u32[]{:S(2)}) %collective-permute-start.8) | collective-permute-done | bytes 120864 | tf_op jit(solution)/shard_map/ppermute | solution.py:309
  20.7 2.7 %collective-permute-start.9 = (bf16[472,128]{1,0:T(8,128)(2,1)S(1)}, bf16[472,128]{1,0:T(8,128)(2,1)S(1)}, u32[]{:S(2)}, u32[]{:S(2)}) collective-permute-start(bf16[472,128]{1,0:T(8,128)(2,1)S(1)} %add_convert_fusion.2), channel_id=1, source_target_pairs={{0,2},{1,3},{2,0},{3,1},{4,6},{5,7},{6,4},{7,5},{8,12},{9,13},{10,... | collective-permute-start | bytes 362504 | tf_op jit(solution)/shard_map/ppermute | solution.py:309
  23.4 3.3 %collective-permute-done.9 = bf16[472,128]{1,0:T(8,128)(2,1)S(1)} collective-permute-done((bf16[472,128]{1,0:T(8,128)(2,1)S(1)}, bf16[472,128]{1,0:T(8,128)(2,1)S(1)}, u32[]{:S(2)}, u32[]{:S(2)}) %collective-permute-start.9) | collective-permute-done | bytes 120864 | tf_op jit(solution)/shard_map/ppermute | solution.py:309
  26.7 2.6 %collective-permute-start.10 = (bf16[472,128]{1,0:T(8,128)(2,1)S(1)}, bf16[472,128]{1,0:T(8,128)(2,1)S(1)}, u32[]{:S(2)}, u32[]{:S(2)}) collective-permute-start(bf16[472,128]{1,0:T(8,128)(2,1)S(1)} %add_convert_fusion.1), channel_id=1, source_target_pairs={{0,4},{1,5},{2,6},{3,7},{4,0},{5,1},{6,2},{7,3},{8,10},{9,11},{10,... | collective-permute-start | bytes 362504 | tf_op jit(solution)/shard_map/ppermute | solution.py:309
  29.3 3.2 %collective-permute-done.10 = bf16[472,128]{1,0:T(8,128)(2,1)S(1)} collective-permute-done((bf16[472,128]{1,0:T(8,128)(2,1)S(1)}, bf16[472,128]{1,0:T(8,128)(2,1)S(1)}, u32[]{:S(2)}, u32[]{:S(2)}) %collective-permute-start.10) | collective-permute-done | bytes 120864 | tf_op jit(solution)/shard_map/ppermute | solution.py:309
  32.6 1.6 %collective-permute-start.11 = (bf16[472,128]{1,0:T(8,128)(2,1)S(1)}, bf16[472,128]{1,0:T(8,128)(2,1)S(1)}, u32[]{:S(2)}, u32[]{:S(2)}) collective-permute-start(bf16[472,128]{1,0:T(8,128)(2,1)S(1)} %add_convert_fusion.refs_0_), channel_id=1, source_target_pairs={{0,17},{1,16},{2,19},{3,18},{4,21},{5,20},{6,23},{7,22},{8,25},{9,... | collective-permute-start | bytes 362504 | tf_op jit(solution)/shard_map/ppermute | solution.py:309
  34.2 0.7 %collective-permute-start.13 = (bf16[472,128]{1,0:T(8,128)(2,1)S(1)}, bf16[472,128]{1,0:T(8,128)(2,1)S(1)}, u32[]{:S(2)}, u32[]{:S(2)}) collective-permute-start(bf16[472,128]{1,0:T(8,128)(2,1)S(1)} %add_convert_fusion.refs_0_), channel_id=1, source_target_pairs={{0,16},{1,17},{2,18},{3,19},{4,20},{5,21},{6,22},{7,23},{8,9},{9,8... | collective-permute-start | bytes 362504 | tf_op jit(solution)/shard_map/ppermute | solution.py:309
  34.9 1.2 %collective-permute-start.12 = (bf16[472,128]{1,0:T(8,128)(2,1)S(1)}, bf16[472,128]{1,0:T(8,128)(2,1)S(1)}, u32[]{:S(2)}, u32[]{:S(2)}) collective-permute-start(bf16[472,128]{1,0:T(8,128)(2,1)S(1)} %add_convert_fusion.refs_0_), channel_id=1, source_target_pairs={{0,1},{1,0},{2,3},{3,2},{4,5},{5,4},{6,7},{7,6},{8,24},{9,25},{10,... | collective-permute-start | bytes 362504 | tf_op jit(solution)/shard_map/ppermute | solution.py:309
  36.1 2.3 %collective-permute-done.11.refs_1_ = bf16[472,128]{1,0:T(8,128)(2,1)S(1)} collective-permute-done((bf16[472,128]{1,0:T(8,128)(2,1)S(1)}, bf16[472,128]{1,0:T(8,128)(2,1)S(1)}, u32[]{:S(2)}, u32[]{:S(2)}) %collective-permute-start.11) | collective-permute-done | bytes 120864 | tf_op jit(solution)/shard_map/ppermute | solution.py:309
  38.4 0.7 %collective-permute-done.13.refs_3_ = bf16[472,128]{1,0:T(8,128)(2,1)S(1)} collective-permute-done((bf16[472,128]{1,0:T(8,128)(2,1)S(1)}, bf16[472,128]{1,0:T(8,128)(2,1)S(1)}, u32[]{:S(2)}, u32[]{:S(2)}) %collective-permute-start.13) | collective-permute-done | bytes 120864 | tf_op jit(solution)/shard_map/ppermute | solution.py:309
  39.1 0.7 %collective-permute-done.12.refs_2_ = bf16[472,128]{1,0:T(8,128)(2,1)S(1)} collective-permute-done((bf16[472,128]{1,0:T(8,128)(2,1)S(1)}, bf16[472,128]{1,0:T(8,128)(2,1)S(1)}, u32[]{:S(2)}, u32[]{:S(2)}) %collective-permute-start.12) | collective-permute-done | bytes 120864 | tf_op jit(solution)/shard_map/ppermute | solution.py:309
  39.8 1.2 %spread_sums.2 = (f32[8,128,256]{2,1,0:T(8,128)}, f32[1728,128]{1,0:T(8,128)}, bf16[16,1024]{1,0:T(8,128)(2,1)}) custom-call(bf16[472,128]{1,0:T(8,128)(2,1)S(1)} %add_convert_fusion.refs_0_, bf16[472,128]{1,0:T(8,128)(2,1)S(1)} %collective-permute-done.11.refs_1_, bf16[472,128]{1,0:T(8,128)(2,1)S(1)} %collective-permute-done.12.refs_2_, ...), custom_call_target="tpu_custom_call" | custom-call | tf_op jit(solution)/shard_map/spread_sums/pallas_call | solution.py:282
  41.1 0.8 %spread_sums.3 = (f32[8,128,256]{2,1,0:T(8,128)}, f32[1728,128]{1,0:T(8,128)}) custom-call(bf16[472,128]{1,0:T(8,128)(2,1)S(1)} %collective-permute-done.16.refs_0_, bf16[472,128]{1,0:T(8,128)(2,1)S(1)} %collective-permute-done.17.refs_1_, f32[8,128,256]{2,1,0:T(8,128)} %get-tuple-element.47.refs_2_, ...), custom_call_target="tpu_custom_call", output_to_operand_aliasing={{0}: (2, {}), {1}: (3, {})} | custom-call | tf_op jit(solution)/shard_map/spread_sums/pallas_call | solution.py:282
  (27 shorter events, 1.2 us)
Async XLA Ops:
  0.6 5.0 %copy-start = (bf16[1,8,32,1024]{3,2,1,0:T(8,128)(2,1)S(1)}, bf16[1,8,32,1024]{3,2,1,0:T(8,128)(2,1)}, u32[]{:S(2)}) copy-start(bf16[1,8,32,1024]{3,2,1,0:T(8,128)(2,1)} %param.7) | copy-start | bytes 1572868
  1.8 6.1 %collective-permute-start.1 = (bf16[32,1024]{1,0:T(8,128)(2,1)S(1)}, bf16[32,1024]{1,0:T(8,128)(2,1)S(1)}, u32[]{:S(2)}, u32[]{:S(2)}) collective-permute-start(bf16[32,1024]{1,0:T(8,128)(2,1)S(1)} %get-tuple-element.27), channel_id=1, source_target_pairs={{0,1},{1,0},{2,3},{3,2},{4,5},{5,4},{6,7},{7,6},{8,9},{9,8},{10,11... | collective-permute-start | bytes 196616 | tf_op jit(solution)/shard_map/ppermute | solution.py:351
  4.9 3.1 %collective-permute-start = (bf16[32,1024]{1,0:T(8,128)(2,1)S(1)}, bf16[32,1024]{1,0:T(8,128)(2,1)S(1)}, u32[]{:S(2)}, u32[]{:S(2)}) collective-permute-start(bf16[32,1024]{1,0:T(8,128)(2,1)S(1)} %get-tuple-element.27), channel_id=1, source_target_pairs={{0,8},{1,2},{2,1},{3,4},{4,3},{5,6},{6,5},{7,15},{8,0},{9,10},{10,... | collective-permute-start | bytes 196616 | tf_op jit(solution)/shard_map/ppermute | solution.py:350
  9.0 1.4 %collective-permute-start.3 = (bf16[472,128]{1,0:T(8,128)(2,1)S(1)}, bf16[472,128]{1,0:T(8,128)(2,1)S(1)}, u32[]{:S(2)}, u32[]{:S(2)}) collective-permute-start(bf16[472,128]{1,0:T(8,128)(2,1)S(1)} %get-tuple-element.40), channel_id=1, source_target_pairs={{0,8},{1,9},{2,10},{3,11},{4,12},{5,13},{6,14},{7,15},{8,0},{9,1},... | collective-permute-start | bytes 362504 | tf_op jit(solution)/shard_map/ppermute | solution.py:309
  9.1 6.0 %collective-permute-start.2 = (bf16[472,128]{1,0:T(8,128)(2,1)S(1)}, bf16[472,128]{1,0:T(8,128)(2,1)S(1)}, u32[]{:S(2)}, u32[]{:S(2)}) collective-permute-start(bf16[472,128]{1,0:T(8,128)(2,1)S(1)} %get-tuple-element.38), channel_id=1, source_target_pairs={{0,8},{1,9},{2,10},{3,11},{4,12},{5,13},{6,14},{7,15},{8,0},{9,1},... | collective-permute-start | bytes 362504 | tf_op jit(solution)/shard_map/ppermute | solution.py:309
  9.6 3.4 %collective-permute-start.5 = (bf16[472,128]{1,0:T(8,128)(2,1)S(1)}, bf16[472,128]{1,0:T(8,128)(2,1)S(1)}, u32[]{:S(2)}, u32[]{:S(2)}) collective-permute-start(bf16[472,128]{1,0:T(8,128)(2,1)S(1)} %get-tuple-element.42), channel_id=1, source_target_pairs={{0,8},{1,9},{2,10},{3,11},{4,12},{5,13},{6,14},{7,15},{8,0},{9,1},... | collective-permute-start | bytes 362504 | tf_op jit(solution)/shard_map/ppermute | solution.py:309
  9.7 5.0 %collective-permute-start.7 = (bf16[472,128]{1,0:T(8,128)(2,1)S(1)}, bf16[472,128]{1,0:T(8,128)(2,1)S(1)}, u32[]{:S(2)}, u32[]{:S(2)}) collective-permute-start(bf16[472,128]{1,0:T(8,128)(2,1)S(1)} %get-tuple-element.44), channel_id=1, source_target_pairs={{0,8},{1,9},{2,10},{3,11},{4,12},{5,13},{6,14},{7,15},{8,0},{9,1},... | collective-permute-start | bytes 362504 | tf_op jit(solution)/shard_map/ppermute | solution.py:309
  10.5 5.8 %collective-permute-start.4 = (bf16[472,128]{1,0:T(8,128)(2,1)S(1)}, bf16[472,128]{1,0:T(8,128)(2,1)S(1)}, u32[]{:S(2)}, u32[]{:S(2)}) collective-permute-start(bf16[472,128]{1,0:T(8,128)(2,1)S(1)} %add_convert_fusion.5), channel_id=1, source_target_pairs={{0,1},{1,0},{2,3},{3,2},{4,5},{5,4},{6,7},{7,6},{8,24},{9,25},{10,... | collective-permute-start | bytes 362504 | tf_op jit(solution)/shard_map/ppermute | solution.py:309
  13.0 6.1 %collective-permute-start.6 = (bf16[472,128]{1,0:T(8,128)(2,1)S(1)}, bf16[472,128]{1,0:T(8,128)(2,1)S(1)}, u32[]{:S(2)}, u32[]{:S(2)}) collective-permute-start(bf16[472,128]{1,0:T(8,128)(2,1)S(1)} %add_convert_fusion.4), channel_id=1, source_target_pairs={{0,16},{1,17},{2,18},{3,19},{4,20},{5,21},{6,22},{7,23},{8,9},{9,8... | collective-permute-start | bytes 362504 | tf_op jit(solution)/shard_map/ppermute | solution.py:309
  14.7 5.8 %collective-permute-start.8 = (bf16[472,128]{1,0:T(8,128)(2,1)S(1)}, bf16[472,128]{1,0:T(8,128)(2,1)S(1)}, u32[]{:S(2)}, u32[]{:S(2)}) collective-permute-start(bf16[472,128]{1,0:T(8,128)(2,1)S(1)} %add_convert_fusion.3), channel_id=1, source_target_pairs={{0,17},{1,16},{2,19},{3,18},{4,21},{5,20},{6,23},{7,22},{8,25},{9,... | collective-permute-start | bytes 362504 | tf_op jit(solution)/shard_map/ppermute | solution.py:309
  20.7 6.0 %collective-permute-start.9 = (bf16[472,128]{1,0:T(8,128)(2,1)S(1)}, bf16[472,128]{1,0:T(8,128)(2,1)S(1)}, u32[]{:S(2)}, u32[]{:S(2)}) collective-permute-start(bf16[472,128]{1,0:T(8,128)(2,1)S(1)} %add_convert_fusion.2), channel_id=1, source_target_pairs={{0,2},{1,3},{2,0},{3,1},{4,6},{5,7},{6,4},{7,5},{8,12},{9,13},{10,... | collective-permute-start | bytes 362504 | tf_op jit(solution)/shard_map/ppermute | solution.py:309
  26.7 5.8 %collective-permute-start.10 = (bf16[472,128]{1,0:T(8,128)(2,1)S(1)}, bf16[472,128]{1,0:T(8,128)(2,1)S(1)}, u32[]{:S(2)}, u32[]{:S(2)}) collective-permute-start(bf16[472,128]{1,0:T(8,128)(2,1)S(1)} %add_convert_fusion.1), channel_id=1, source_target_pairs={{0,4},{1,5},{2,6},{3,7},{4,0},{5,1},{6,2},{7,3},{8,10},{9,11},{10,... | collective-permute-start | bytes 362504 | tf_op jit(solution)/shard_map/ppermute | solution.py:309
  32.6 5.8 %collective-permute-start.11 = (bf16[472,128]{1,0:T(8,128)(2,1)S(1)}, bf16[472,128]{1,0:T(8,128)(2,1)S(1)}, u32[]{:S(2)}, u32[]{:S(2)}) collective-permute-start(bf16[472,128]{1,0:T(8,128)(2,1)S(1)} %add_convert_fusion.refs_0_), channel_id=1, source_target_pairs={{0,17},{1,16},{2,19},{3,18},{4,21},{5,20},{6,23},{7,22},{8,25},{9,... | collective-permute-start | bytes 362504 | tf_op jit(solution)/shard_map/ppermute | solution.py:309
  34.2 4.9 %collective-permute-start.13 = (bf16[472,128]{1,0:T(8,128)(2,1)S(1)}, bf16[472,128]{1,0:T(8,128)(2,1)S(1)}, u32[]{:S(2)}, u32[]{:S(2)}) collective-permute-start(bf16[472,128]{1,0:T(8,128)(2,1)S(1)} %add_convert_fusion.refs_0_), channel_id=1, source_target_pairs={{0,16},{1,17},{2,18},{3,19},{4,20},{5,21},{6,22},{7,23},{8,9},{9,8... | collective-permute-start | bytes 362504 | tf_op jit(solution)/shard_map/ppermute | solution.py:309
  34.9 4.9 %collective-permute-start.12 = (bf16[472,128]{1,0:T(8,128)(2,1)S(1)}, bf16[472,128]{1,0:T(8,128)(2,1)S(1)}, u32[]{:S(2)}, u32[]{:S(2)}) collective-permute-start(bf16[472,128]{1,0:T(8,128)(2,1)S(1)} %add_convert_fusion.refs_0_), channel_id=1, source_target_pairs={{0,1},{1,0},{2,3},{3,2},{4,5},{5,4},{6,7},{7,6},{8,24},{9,25},{10,... | collective-permute-start | bytes 362504 | tf_op jit(solution)/shard_map/ppermute | solution.py:309
  36.1 3.6 %collective-permute-start.14 = (bf16[472,128]{1,0:T(8,128)(2,1)S(1)}, bf16[472,128]{1,0:T(8,128)(2,1)S(1)}, u32[]{:S(2)}, u32[]{:S(2)}) collective-permute-start(bf16[472,128]{1,0:T(8,128)(2,1)S(1)} %add_convert_fusion.refs_0_), channel_id=1, source_target_pairs={{0,8},{1,9},{2,10},{3,11},{4,12},{5,13},{6,14},{7,15},{8,0},{9,1},... | collective-permute-start | bytes 362504 | tf_op jit(solution)/shard_map/ppermute | solution.py:309
  38.4 1.4 %collective-permute-start.15 = (bf16[472,128]{1,0:T(8,128)(2,1)S(1)}, bf16[472,128]{1,0:T(8,128)(2,1)S(1)}, u32[]{:S(2)}, u32[]{:S(2)}) collective-permute-start(bf16[472,128]{1,0:T(8,128)(2,1)S(1)} %collective-permute-done.11.refs_1_), channel_id=1, source_target_pairs={{0,8},{1,9},{2,10},{3,11},{4,12},{5,13},{6,14},{7,15},{8,0},{9,1},... | collective-permute-start | bytes 362504 | tf_op jit(solution)/shard_map/ppermute | solution.py:309
  39.1 1.9 %collective-permute-start.17 = (bf16[472,128]{1,0:T(8,128)(2,1)S(1)}, bf16[472,128]{1,0:T(8,128)(2,1)S(1)}, u32[]{:S(2)}, u32[]{:S(2)}) collective-permute-start(bf16[472,128]{1,0:T(8,128)(2,1)S(1)} %collective-permute-done.13.refs_3_), channel_id=1, source_target_pairs={{0,8},{1,9},{2,10},{3,11},{4,12},{5,13},{6,14},{7,15},{8,0},{9,1},... | collective-permute-start | bytes 362504 | tf_op jit(solution)/shard_map/ppermute | solution.py:309
  39.7 1.3 %collective-permute-start.16 = (bf16[472,128]{1,0:T(8,128)(2,1)S(1)}, bf16[472,128]{1,0:T(8,128)(2,1)S(1)}, u32[]{:S(2)}, u32[]{:S(2)}) collective-permute-start(bf16[472,128]{1,0:T(8,128)(2,1)S(1)} %collective-permute-done.12.refs_2_), channel_id=1, source_target_pairs={{0,8},{1,9},{2,10},{3,11},{4,12},{5,13},{6,14},{7,15},{8,0},{9,1},... | collective-permute-start | bytes 362504 | tf_op jit(solution)/shard_map/ppermute | solution.py:309

commit v8 on v7

--- a/solution.py
+++ b/solution.py
@@ -314,7 +314,7 @@
 
 
 def total(keep, send):
-    got = {m: swapped(send[m], SIBLING) for m in (1, 2, 3, 0)}
+    got = {m: swapped(send[m], SIBLING) for m in (1, 2, 0, 3)}
     quad = {}
     for m in (1, 2, 3):
         quad[m] = swapped((keep[m] + got[m].astype(F32)).astype(BF16), QUAD[m])

time: 42.3 us -> 42.3 us (level)
  no operation moved by 1% of the time
where the time goes in v8:
time: 42.3 us; the launch traced here: 41.9 us
  starting transfers between devices  17.5 us (41%)
  waiting for transfers between devices  16.7 us (39%)
  Pallas kernels  5.91 us (14%)
  between operations  1.39 us (3%)
    ppermute x16, waiting for transfers between devices, swapped(): return lax.ppermute(value, ('sample', 'space'), pairs)  16 us
    ppermute x16, starting transfers between devices, swapped(): return lax.ppermute(value, ('sample', 'space'), pairs)  14.5 us
    ppermute x1, starting transfers between devices, neighbours_planes(): lax.ppermute(edge, ('sample', 'space'), list(zip(across[0], beside)))  3.03 us
    pallas_call x2, Pallas kernels, spread(): pl.pallas_call(functools.partial(spread_kernel, names, len(whole)), in_sp...  2.05 us
    pallas_call x1, Pallas kernels, body(): pl.pallas_call(inner_kernel, in_specs=[vmem] * 5 + [hbm], out_specs=[vmem...  1.61 us
    pallas_call x1, Pallas kernels, body(): pl.pallas_call(edge_kernel, in_specs=[hbm] * 5, out_specs=[vmem] * 5, out...  1.18 us
    pallas_call x1, Pallas kernels, body(): pl.pallas_call(local_kernel, in_specs=[vmem] * 9, out_specs=[vmem] * 9, o...  1.06 us
  transfers between devices with their start and end apart: 18, of which 11 were waited for; matrix products, arithmetic and copies ran while one was open for 0% of the time, Pallas kernels for 7%

profile of v8, /device:TPU:0, one launch (start us, length us, event | category | flops | bytes accessed | tf_op | source)
XLA Modules:
  0.0 41.9 jit_solution(3881604831222724386)
XLA Ops:
  0.6 1.2 %edge_plane.1 = (bf16[32,1024]{1,0:T(8,128)(2,1)S(1)}, s32[8,512]{1,0:T(8,128)S(1)}, f32[8,128]{1,0:T(8,128)S(1)}, bf16[9,192,128]{2,1,0:T(8,128)(2,1)S(1)}, bf16[16,1024]{1,0:T(8,128)(2,1)S(1)}) custom-call(bf16[8,32,1024]{2,1,0:T(8,128)(2,1)} %bitcast.11, s32[8,512]{1,0:T(8,128)} %bitcast.19, f32[8,128]{1,0:T(8,128)} %table_ref.1, ...), custom_call_target="tpu_custom_call" | custom-call | tf_op jit(solution)/shard_map/edge_plane/pallas_call | solution.py:366
  1.8 3.0 %collective-permute-start.1 = (bf16[32,1024]{1,0:T(8,128)(2,1)S(1)}, bf16[32,1024]{1,0:T(8,128)(2,1)S(1)}, u32[]{:S(2)}, u32[]{:S(2)}) collective-permute-start(bf16[32,1024]{1,0:T(8,128)(2,1)S(1)} %get-tuple-element.27), channel_id=1, source_target_pairs={{0,1},{1,0},{2,3},{3,2},{4,5},{5,4},{6,7},{7,6},{8,9},{9,8},{10,11... | collective-permute-start | bytes 196616 | tf_op jit(solution)/shard_map/ppermute | solution.py:351
  5.6 1.6 %inner_terms.1 = (bf16[3,64,1152]{2,1,0:T(8,128)(2,1)S(1)}, bf16[3,64,1152]{2,1,0:T(8,128)(2,1)S(1)}, f32[512,128]{1,0:T(8,128)S(1)}, bf16[8,128,256]{2,1,0:T(8,128)(2,1)S(1)}, f32[512,128]{1,0:T(8,128)S(1)}) custom-call(bf16[8,32,1024]{2,1,0:T(8,128)(2,1)S(1)} %bitcast.12, s32[8,512]{1,0:T(8,128)S(1)} %get-tuple-element.29.opens_ref, ...), custom_call_target="tpu_custom_call" | custom-call | tf_op jit(solution)/shard_map/inner_terms/pallas_call | solution.py:396
  7.2 0.7 %collective-permute-done.1.beside_ref = bf16[32,1024]{1,0:T(8,128)(2,1)S(1)} collective-permute-done((bf16[32,1024]{1,0:T(8,128)(2,1)S(1)}, bf16[32,1024]{1,0:T(8,128)(2,1)S(1)}, u32[]{:S(2)}, u32[]{:S(2)}) %collective-permute-start.1) | collective-permute-done | bytes 65568 | tf_op jit(solution)/shard_map/ppermute | solution.py:351
  8.0 1.1 %local_terms.1 = (bf16[16,1024]{1,0:T(8,128)(2,1)S(1)}, f32[472,128]{1,0:T(8,128)S(1)}, f32[472,128]{1,0:T(8,128)S(1)}, f32[472,128]{1,0:T(8,128)S(1)}, f32[472,...) custom-call(bf16[32,1024]{1,0:T(8,128)(2,1)S(1)} %collective-permute, ...), custom_call_target="tpu_custom_call" | custom-call | tf_op jit(solution)/shard_map/local_terms/pallas_call | solution.py:418
  9.1 0.5 %collective-permute-start.2 = (bf16[472,128]{1,0:T(8,128)(2,1)S(1)}, bf16[472,128]{1,0:T(8,128)(2,1)S(1)}, u32[]{:S(2)}, u32[]{:S(2)}) collective-permute-start(bf16[472,128]{1,0:T(8,128)(2,1)S(1)} %get-tuple-element.38), channel_id=1, source_target_pairs={{0,8},{1,9},{2,10},{3,11},{4,12},{5,13},{6,14},{7,15},{8,0},{9,1},... | collective-permute-start | bytes 362504 | tf_op jit(solution)/shard_map/ppermute | solution.py:309
  9.7 0.4 %collective-permute-start.7 = (bf16[472,128]{1,0:T(8,128)(2,1)S(1)}, bf16[472,128]{1,0:T(8,128)(2,1)S(1)}, u32[]{:S(2)}, u32[]{:S(2)}) collective-permute-start(bf16[472,128]{1,0:T(8,128)(2,1)S(1)} %get-tuple-element.44), channel_id=1, source_target_pairs={{0,8},{1,9},{2,10},{3,11},{4,12},{5,13},{6,14},{7,15},{8,0},{9,1},... | collective-permute-start | bytes 362504 | tf_op jit(solution)/shard_map/ppermute | solution.py:309
  10.5 2.5 %collective-permute-start.4 = (bf16[472,128]{1,0:T(8,128)(2,1)S(1)}, bf16[472,128]{1,0:T(8,128)(2,1)S(1)}, u32[]{:S(2)}, u32[]{:S(2)}) collective-permute-start(bf16[472,128]{1,0:T(8,128)(2,1)S(1)} %add_convert_fusion.5), channel_id=1, source_target_pairs={{0,1},{1,0},{2,3},{3,2},{4,5},{5,4},{6,7},{7,6},{8,24},{9,25},{10,... | collective-permute-start | bytes 362504 | tf_op jit(solution)/shard_map/ppermute | solution.py:309
  13.0 1.7 %collective-permute-start.6 = (bf16[472,128]{1,0:T(8,128)(2,1)S(1)}, bf16[472,128]{1,0:T(8,128)(2,1)S(1)}, u32[]{:S(2)}, u32[]{:S(2)}) collective-permute-start(bf16[472,128]{1,0:T(8,128)(2,1)S(1)} %add_convert_fusion.4), channel_id=1, source_target_pairs={{0,16},{1,17},{2,18},{3,19},{4,20},{5,21},{6,22},{7,23},{8,9},{9,8... | collective-permute-start | bytes 362504 | tf_op jit(solution)/shard_map/ppermute | solution.py:309
  15.1 1.2 %collective-permute-done.4 = bf16[472,128]{1,0:T(8,128)(2,1)S(1)} collective-permute-done((bf16[472,128]{1,0:T(8,128)(2,1)S(1)}, bf16[472,128]{1,0:T(8,128)(2,1)S(1)}, u32[]{:S(2)}, u32[]{:S(2)}) %collective-permute-start.4) | collective-permute-done | bytes 120864 | tf_op jit(solution)/shard_map/ppermute | solution.py:309
  16.2 2.9 %collective-permute-done.6 = bf16[472,128]{1,0:T(8,128)(2,1)S(1)} collective-permute-done((bf16[472,128]{1,0:T(8,128)(2,1)S(1)}, bf16[472,128]{1,0:T(8,128)(2,1)S(1)}, u32[]{:S(2)}, u32[]{:S(2)}) %collective-permute-start.6) | collective-permute-done | bytes 120864 | tf_op jit(solution)/shard_map/ppermute | solution.py:309
  19.2 1.4 %collective-permute-done.8 = bf16[472,128]{1,0:T(8,128)(2,1)S(1)} collective-permute-done((bf16[472,128]{1,0:T(8,128)(2,1)S(1)}, bf16[472,128]{1,0:T(8,128)(2,1)S(1)}, u32[]{:S(2)}, u32[]{:S(2)}) %collective-permute-start.8) | collective-permute-done | bytes 120864 | tf_op jit(solution)/shard_map/ppermute | solution.py:309
  20.7 2.7 %collective-permute-start.9 = (bf16[472,128]{1,0:T(8,128)(2,1)S(1)}, bf16[472,128]{1,0:T(8,128)(2,1)S(1)}, u32[]{:S(2)}, u32[]{:S(2)}) collective-permute-start(bf16[472,128]{1,0:T(8,128)(2,1)S(1)} %add_convert_fusion.2), channel_id=1, source_target_pairs={{0,2},{1,3},{2,0},{3,1},{4,6},{5,7},{6,4},{7,5},{8,12},{9,13},{10,... | collective-permute-start | bytes 362504 | tf_op jit(solution)/shard_map/ppermute | solution.py:309
  23.4 3.3 %collective-permute-done.9 = bf16[472,128]{1,0:T(8,128)(2,1)S(1)} collective-permute-done((bf16[472,128]{1,0:T(8,128)(2,1)S(1)}, bf16[472,128]{1,0:T(8,128)(2,1)S(1)}, u32[]{:S(2)}, u32[]{:S(2)}) %collective-permute-start.9) | collective-permute-done | bytes 120864 | tf_op jit(solution)/shard_map/ppermute | solution.py:309
  26.7 2.6 %collective-permute-start.10 = (bf16[472,128]{1,0:T(8,128)(2,1)S(1)}, bf16[472,128]{1,0:T(8,128)(2,1)S(1)}, u32[]{:S(2)}, u32[]{:S(2)}) collective-permute-start(bf16[472,128]{1,0:T(8,128)(2,1)S(1)} %add_convert_fusion.1), channel_id=1, source_target_pairs={{0,4},{1,5},{2,6},{3,7},{4,0},{5,1},{6,2},{7,3},{8,10},{9,11},{10,... | collective-permute-start | bytes 362504 | tf_op jit(solution)/shard_map/ppermute | solution.py:309
  29.3 3.2 %collective-permute-done.10 = bf16[472,128]{1,0:T(8,128)(2,1)S(1)} collective-permute-done((bf16[472,128]{1,0:T(8,128)(2,1)S(1)}, bf16[472,128]{1,0:T(8,128)(2,1)S(1)}, u32[]{:S(2)}, u32[]{:S(2)}) %collective-permute-start.10) | collective-permute-done | bytes 120864 | tf_op jit(solution)/shard_map/ppermute | solution.py:309
  32.6 1.6 %collective-permute-start.11 = (bf16[472,128]{1,0:T(8,128)(2,1)S(1)}, bf16[472,128]{1,0:T(8,128)(2,1)S(1)}, u32[]{:S(2)}, u32[]{:S(2)}) collective-permute-start(bf16[472,128]{1,0:T(8,128)(2,1)S(1)} %add_convert_fusion.refs_0_), channel_id=1, source_target_pairs={{0,17},{1,16},{2,19},{3,18},{4,21},{5,20},{6,23},{7,22},{8,25},{9,... | collective-permute-start | bytes 362504 | tf_op jit(solution)/shard_map/ppermute | solution.py:309
  34.2 0.7 %collective-permute-start.13 = (bf16[472,128]{1,0:T(8,128)(2,1)S(1)}, bf16[472,128]{1,0:T(8,128)(2,1)S(1)}, u32[]{:S(2)}, u32[]{:S(2)}) collective-permute-start(bf16[472,128]{1,0:T(8,128)(2,1)S(1)} %add_convert_fusion.refs_0_), channel_id=1, source_target_pairs={{0,16},{1,17},{2,18},{3,19},{4,20},{5,21},{6,22},{7,23},{8,9},{9,8... | collective-permute-start | bytes 362504 | tf_op jit(solution)/shard_map/ppermute | solution.py:309
  34.9 1.2 %collective-permute-start.12 = (bf16[472,128]{1,0:T(8,128)(2,1)S(1)}, bf16[472,128]{1,0:T(8,128)(2,1)S(1)}, u32[]{:S(2)}, u32[]{:S(2)}) collective-permute-start(bf16[472,128]{1,0:T(8,128)(2,1)S(1)} %add_convert_fusion.refs_0_), channel_id=1, source_target_pairs={{0,1},{1,0},{2,3},{3,2},{4,5},{5,4},{6,7},{7,6},{8,24},{9,25},{10,... | collective-permute-start | bytes 362504 | tf_op jit(solution)/shard_map/ppermute | solution.py:309
  36.1 2.3 %collective-permute-done.11.refs_1_ = bf16[472,128]{1,0:T(8,128)(2,1)S(1)} collective-permute-done((bf16[472,128]{1,0:T(8,128)(2,1)S(1)}, bf16[472,128]{1,0:T(8,128)(2,1)S(1)}, u32[]{:S(2)}, u32[]{:S(2)}) %collective-permute-start.11) | collective-permute-done | bytes 120864 | tf_op jit(solution)/shard_map/ppermute | solution.py:309
  38.4 0.7 %collective-permute-done.13.refs_3_ = bf16[472,128]{1,0:T(8,128)(2,1)S(1)} collective-permute-done((bf16[472,128]{1,0:T(8,128)(2,1)S(1)}, bf16[472,128]{1,0:T(8,128)(2,1)S(1)}, u32[]{:S(2)}, u32[]{:S(2)}) %collective-permute-start.13) | collective-permute-done | bytes 120864 | tf_op jit(solution)/shard_map/ppermute | solution.py:309
  39.1 0.7 %collective-permute-done.12.refs_2_ = bf16[472,128]{1,0:T(8,128)(2,1)S(1)} collective-permute-done((bf16[472,128]{1,0:T(8,128)(2,1)S(1)}, bf16[472,128]{1,0:T(8,128)(2,1)S(1)}, u32[]{:S(2)}, u32[]{:S(2)}) %collective-permute-start.12) | collective-permute-done | bytes 120864 | tf_op jit(solution)/shard_map/ppermute | solution.py:309
  39.8 1.2 %spread_sums.2 = (f32[8,128,256]{2,1,0:T(8,128)}, f32[1728,128]{1,0:T(8,128)}, bf16[16,1024]{1,0:T(8,128)(2,1)}) custom-call(bf16[472,128]{1,0:T(8,128)(2,1)S(1)} %add_convert_fusion.refs_0_, bf16[472,128]{1,0:T(8,128)(2,1)S(1)} %collective-permute-done.11.refs_1_, bf16[472,128]{1,0:T(8,128)(2,1)S(1)} %collective-permute-done.12.refs_2_, ...), custom_call_target="tpu_custom_call" | custom-call | tf_op jit(solution)/shard_map/spread_sums/pallas_call | solution.py:282
  41.1 0.8 %spread_sums.3 = (f32[8,128,256]{2,1,0:T(8,128)}, f32[1728,128]{1,0:T(8,128)}) custom-call(bf16[472,128]{1,0:T(8,128)(2,1)S(1)} %collective-permute-done.16.refs_0_, bf16[472,128]{1,0:T(8,128)(2,1)S(1)} %collective-permute-done.17.refs_1_, f32[8,128,256]{2,1,0:T(8,128)} %get-tuple-element.47.refs_2_, ...), custom_call_target="tpu_custom_call", output_to_operand_aliasing={{0}: (2, {}), {1}: (3, {})} | custom-call | tf_op jit(solution)/shard_map/spread_sums/pallas_call | solution.py:282
  (27 shorter events, 1.2 us)
Async XLA Ops:
  0.6 5.0 %copy-start = (bf16[1,8,32,1024]{3,2,1,0:T(8,128)(2,1)S(1)}, bf16[1,8,32,1024]{3,2,1,0:T(8,128)(2,1)}, u32[]{:S(2)}) copy-start(bf16[1,8,32,1024]{3,2,1,0:T(8,128)(2,1)} %param.7) | copy-start | bytes 1572868
  1.8 6.1 %collective-permute-start.1 = (bf16[32,1024]{1,0:T(8,128)(2,1)S(1)}, bf16[32,1024]{1,0:T(8,128)(2,1)S(1)}, u32[]{:S(2)}, u32[]{:S(2)}) collective-permute-start(bf16[32,1024]{1,0:T(8,128)(2,1)S(1)} %get-tuple-element.27), channel_id=1, source_target_pairs={{0,1},{1,0},{2,3},{3,2},{4,5},{5,4},{6,7},{7,6},{8,9},{9,8},{10,11... | collective-permute-start | bytes 196616 | tf_op jit(solution)/shard_map/ppermute | solution.py:351
  4.9 3.1 %collective-permute-start = (bf16[32,1024]{1,0:T(8,128)(2,1)S(1)}, bf16[32,1024]{1,0:T(8,128)(2,1)S(1)}, u32[]{:S(2)}, u32[]{:S(2)}) collective-permute-start(bf16[32,1024]{1,0:T(8,128)(2,1)S(1)} %get-tuple-element.27), channel_id=1, source_target_pairs={{0,8},{1,2},{2,1},{3,4},{4,3},{5,6},{6,5},{7,15},{8,0},{9,10},{10,... | collective-permute-start | bytes 196616 | tf_op jit(solution)/shard_map/ppermute | solution.py:350
  9.0 1.4 %collective-permute-start.3 = (bf16[472,128]{1,0:T(8,128)(2,1)S(1)}, bf16[472,128]{1,0:T(8,128)(2,1)S(1)}, u32[]{:S(2)}, u32[]{:S(2)}) collective-permute-start(bf16[472,128]{1,0:T(8,128)(2,1)S(1)} %get-tuple-element.40), channel_id=1, source_target_pairs={{0,8},{1,9},{2,10},{3,11},{4,12},{5,13},{6,14},{7,15},{8,0},{9,1},... | collective-permute-start | bytes 362504 | tf_op jit(solution)/shard_map/ppermute | solution.py:309
  9.1 6.0 %collective-permute-start.2 = (bf16[472,128]{1,0:T(8,128)(2,1)S(1)}, bf16[472,128]{1,0:T(8,128)(2,1)S(1)}, u32[]{:S(2)}, u32[]{:S(2)}) collective-permute-start(bf16[472,128]{1,0:T(8,128)(2,1)S(1)} %get-tuple-element.38), channel_id=1, source_target_pairs={{0,8},{1,9},{2,10},{3,11},{4,12},{5,13},{6,14},{7,15},{8,0},{9,1},... | collective-permute-start | bytes 362504 | tf_op jit(solution)/shard_map/ppermute | solution.py:309
  9.6 3.4 %collective-permute-start.5 = (bf16[472,128]{1,0:T(8,128)(2,1)S(1)}, bf16[472,128]{1,0:T(8,128)(2,1)S(1)}, u32[]{:S(2)}, u32[]{:S(2)}) collective-permute-start(bf16[472,128]{1,0:T(8,128)(2,1)S(1)} %get-tuple-element.42), channel_id=1, source_target_pairs={{0,8},{1,9},{2,10},{3,11},{4,12},{5,13},{6,14},{7,15},{8,0},{9,1},... | collective-permute-start | bytes 362504 | tf_op jit(solution)/shard_map/ppermute | solution.py:309
  9.7 5.0 %collective-permute-start.7 = (bf16[472,128]{1,0:T(8,128)(2,1)S(1)}, bf16[472,128]{1,0:T(8,128)(2,1)S(1)}, u32[]{:S(2)}, u32[]{:S(2)}) collective-permute-start(bf16[472,128]{1,0:T(8,128)(2,1)S(1)} %get-tuple-element.44), channel_id=1, source_target_pairs={{0,8},{1,9},{2,10},{3,11},{4,12},{5,13},{6,14},{7,15},{8,0},{9,1},... | collective-permute-start | bytes 362504 | tf_op jit(solution)/shard_map/ppermute | solution.py:309
  10.5 5.8 %collective-permute-start.4 = (bf16[472,128]{1,0:T(8,128)(2,1)S(1)}, bf16[472,128]{1,0:T(8,128)(2,1)S(1)}, u32[]{:S(2)}, u32[]{:S(2)}) collective-permute-start(bf16[472,128]{1,0:T(8,128)(2,1)S(1)} %add_convert_fusion.5), channel_id=1, source_target_pairs={{0,1},{1,0},{2,3},{3,2},{4,5},{5,4},{6,7},{7,6},{8,24},{9,25},{10,... | collective-permute-start | bytes 362504 | tf_op jit(solution)/shard_map/ppermute | solution.py:309
  13.0 6.1 %collective-permute-start.6 = (bf16[472,128]{1,0:T(8,128)(2,1)S(1)}, bf16[472,128]{1,0:T(8,128)(2,1)S(1)}, u32[]{:S(2)}, u32[]{:S(2)}) collective-permute-start(bf16[472,128]{1,0:T(8,128)(2,1)S(1)} %add_convert_fusion.4), channel_id=1, source_target_pairs={{0,16},{1,17},{2,18},{3,19},{4,20},{5,21},{6,22},{7,23},{8,9},{9,8... | collective-permute-start | bytes 362504 | tf_op jit(solution)/shard_map/ppermute | solution.py:309
  14.7 5.8 %collective-permute-start.8 = (bf16[472,128]{1,0:T(8,128)(2,1)S(1)}, bf16[472,128]{1,0:T(8,128)(2,1)S(1)}, u32[]{:S(2)}, u32[]{:S(2)}) collective-permute-start(bf16[472,128]{1,0:T(8,128)(2,1)S(1)} %add_convert_fusion.3), channel_id=1, source_target_pairs={{0,17},{1,16},{2,19},{3,18},{4,21},{5,20},{6,23},{7,22},{8,25},{9,... | collective-permute-start | bytes 362504 | tf_op jit(solution)/shard_map/ppermute | solution.py:309
  20.7 6.0 %collective-permute-start.9 = (bf16[472,128]{1,0:T(8,128)(2,1)S(1)}, bf16[472,128]{1,0:T(8,128)(2,1)S(1)}, u32[]{:S(2)}, u32[]{:S(2)}) collective-permute-start(bf16[472,128]{1,0:T(8,128)(2,1)S(1)} %add_convert_fusion.2), channel_id=1, source_target_pairs={{0,2},{1,3},{2,0},{3,1},{4,6},{5,7},{6,4},{7,5},{8,12},{9,13},{10,... | collective-permute-start | bytes 362504 | tf_op jit(solution)/shard_map/ppermute | solution.py:309
  26.7 5.8 %collective-permute-start.10 = (bf16[472,128]{1,0:T(8,128)(2,1)S(1)}, bf16[472,128]{1,0:T(8,128)(2,1)S(1)}, u32[]{:S(2)}, u32[]{:S(2)}) collective-permute-start(bf16[472,128]{1,0:T(8,128)(2,1)S(1)} %add_convert_fusion.1), channel_id=1, source_target_pairs={{0,4},{1,5},{2,6},{3,7},{4,0},{5,1},{6,2},{7,3},{8,10},{9,11},{10,... | collective-permute-start | bytes 362504 | tf_op jit(solution)/shard_map/ppermute | solution.py:309
  32.6 5.8 %collective-permute-start.11 = (bf16[472,128]{1,0:T(8,128)(2,1)S(1)}, bf16[472,128]{1,0:T(8,128)(2,1)S(1)}, u32[]{:S(2)}, u32[]{:S(2)}) collective-permute-start(bf16[472,128]{1,0:T(8,128)(2,1)S(1)} %add_convert_fusion.refs_0_), channel_id=1, source_target_pairs={{0,17},{1,16},{2,19},{3,18},{4,21},{5,20},{6,23},{7,22},{8,25},{9,... | collective-permute-start | bytes 362504 | tf_op jit(solution)/shard_map/ppermute | solution.py:309
  34.2 4.9 %collective-permute-start.13 = (bf16[472,128]{1,0:T(8,128)(2,1)S(1)}, bf16[472,128]{1,0:T(8,128)(2,1)S(1)}, u32[]{:S(2)}, u32[]{:S(2)}) collective-permute-start(bf16[472,128]{1,0:T(8,128)(2,1)S(1)} %add_convert_fusion.refs_0_), channel_id=1, source_target_pairs={{0,16},{1,17},{2,18},{3,19},{4,20},{5,21},{6,22},{7,23},{8,9},{9,8... | collective-permute-start | bytes 362504 | tf_op jit(solution)/shard_map/ppermute | solution.py:309
  34.9 4.9 %collective-permute-start.12 = (bf16[472,128]{1,0:T(8,128)(2,1)S(1)}, bf16[472,128]{1,0:T(8,128)(2,1)S(1)}, u32[]{:S(2)}, u32[]{:S(2)}) collective-permute-start(bf16[472,128]{1,0:T(8,128)(2,1)S(1)} %add_convert_fusion.refs_0_), channel_id=1, source_target_pairs={{0,1},{1,0},{2,3},{3,2},{4,5},{5,4},{6,7},{7,6},{8,24},{9,25},{10,... | collective-permute-start | bytes 362504 | tf_op jit(solution)/shard_map/ppermute | solution.py:309
  36.1 3.6 %collective-permute-start.14 = (bf16[472,128]{1,0:T(8,128)(2,1)S(1)}, bf16[472,128]{1,0:T(8,128)(2,1)S(1)}, u32[]{:S(2)}, u32[]{:S(2)}) collective-permute-start(bf16[472,128]{1,0:T(8,128)(2,1)S(1)} %add_convert_fusion.refs_0_), channel_id=1, source_target_pairs={{0,8},{1,9},{2,10},{3,11},{4,12},{5,13},{6,14},{7,15},{8,0},{9,1},... | collective-permute-start | bytes 362504 | tf_op jit(solution)/shard_map/ppermute | solution.py:309
  38.4 1.4 %collective-permute-start.15 = (bf16[472,128]{1,0:T(8,128)(2,1)S(1)}, bf16[472,128]{1,0:T(8,128)(2,1)S(1)}, u32[]{:S(2)}, u32[]{:S(2)}) collective-permute-start(bf16[472,128]{1,0:T(8,128)(2,1)S(1)} %collective-permute-done.11.refs_1_), channel_id=1, source_target_pairs={{0,8},{1,9},{2,10},{3,11},{4,12},{5,13},{6,14},{7,15},{8,0},{9,1},... | collective-permute-start | bytes 362504 | tf_op jit(solution)/shard_map/ppermute | solution.py:309
  39.1 1.9 %collective-permute-start.17 = (bf16[472,128]{1,0:T(8,128)(2,1)S(1)}, bf16[472,128]{1,0:T(8,128)(2,1)S(1)}, u32[]{:S(2)}, u32[]{:S(2)}) collective-permute-start(bf16[472,128]{1,0:T(8,128)(2,1)S(1)} %collective-permute-done.13.refs_3_), channel_id=1, source_target_pairs={{0,8},{1,9},{2,10},{3,11},{4,12},{5,13},{6,14},{7,15},{8,0},{9,1},... | collective-permute-start | bytes 362504 | tf_op jit(solution)/shard_map/ppermute | solution.py:309
  39.7 1.3 %collective-permute-start.16 = (bf16[472,128]{1,0:T(8,128)(2,1)S(1)}, bf16[472,128]{1,0:T(8,128)(2,1)S(1)}, u32[]{:S(2)}, u32[]{:S(2)}) collective-permute-start(bf16[472,128]{1,0:T(8,128)(2,1)S(1)} %collective-permute-done.12.refs_2_), channel_id=1, source_target_pairs={{0,8},{1,9},{2,10},{3,11},{4,12},{5,13},{6,14},{7,15},{8,0},{9,1},... | collective-permute-start | bytes 362504 | tf_op jit(solution)/shard_map/ppermute | solution.py:309
